TPU v7x, 256 devices: a whole 4x4x8 slice. The times are simulated.
256 devices in a mesh: head: 16 (over y, x_lo, core), ctx: 16 (over x_hi, z).
Axes of the slice: x: 4 (x_hi: 2, x_lo: 2; x = x_hi * 2 + x_lo), y: 4, z: 8, core: 2. Of those that a mesh axis runs over, the one named last changes fastest.
Arguments:
- queries: bfloat16 [65536, 2048], P(('ctx', 'head')), may hold values from -6 to 6
- keys: bfloat16 [65536, 2048], P(('ctx', 'head')), may hold values from -6 to 6
- values: bfloat16 [65536, 2048], P(('ctx', 'head')), may hold values from -24 to 24
- picks: int32 [128, 2], replicated, may hold values from 0 to 127, as said below
Outputs:
- attended: bfloat16 [65536, 2048], P(('ctx', 'head'))
Inputs may be any that keep to these rules, and one draw needn't show every extreme that they name: `picks`: rows 8 * c to 8 * c + 7 are the query blocks held by index c of ctx, and blocks 8 * o to 8 * o + 7 are held by index o. Among the 16 entries of one such group of rows, at most 2 name blocks held by any one index of ctx; one index o, the same for every group, is named exactly 2 times by every group.
All inputs are finite; a program needn't handle non-finite values.
Results may differ from a plain program's by a relative error of at most 0.0039.
Values may be sent and summed in bfloat16 or wider, within the bound.
A program may use at most 128 MiB of HBM per device.

v0:
```python
import math

import jax
import jax.numpy as jnp
from jax import lax
from jax.sharding import PartitionSpec as P

HEADS = 16
HD = 128
BLOCK = 512
RSEL = 2


def block_pair(query_block, key_block, value_block, score_scale):
    scores = (
        jnp.einsum("qhd,khd->hqk", query_block, key_block, preferred_element_type=jnp.float32)
        * score_scale
    )
    row_max = jnp.max(scores, axis=-1)
    exponent = jnp.exp(scores - row_max[..., None])
    row_sum = jnp.sum(exponent, axis=-1)
    weights = exponent.astype(jnp.bfloat16)
    partial_out = jnp.einsum(
        "hqk,khd->qhd", weights, value_block, preferred_element_type=jnp.float32
    )
    return (partial_out, row_max, row_sum)


def route_tables(picks, local_blocks, ctx_count):
    slots = local_blocks * RSEL
    owners = (picks // local_blocks).reshape(ctx_count, slots)
    within = (picks % local_blocks).reshape(ctx_count, slots)
    owner_ids = jnp.arange(ctx_count, dtype=jnp.int32)
    one_hot = (owners[:, :, None] == owner_ids[None, None, :]).astype(jnp.int32)
    running = jnp.cumsum(one_hot, axis=1)
    position = jnp.sum(one_hot * running, axis=-1) - 1
    return (owners, within, position)


def local(queries, keys, values, picks):
    head_count = lax.axis_size("head")
    ctx_count = lax.axis_size("ctx")
    my_index = lax.axis_index("ctx")
    heads_here = HEADS // head_count
    tok_rows = queries.shape[0]
    score_scale = 1.0 / math.sqrt(HD)
    q_split = queries.reshape(tok_rows, HEADS, HD)
    k_split = keys.reshape(tok_rows, HEADS, HD)
    v_split = values.reshape(tok_rows, HEADS, HD)
    q_heads, k_heads, v_heads = (
        lax.all_to_all(q_split, "head", split_axis=1, concat_axis=0, tiled=True),
        lax.all_to_all(k_split, "head", split_axis=1, concat_axis=0, tiled=True),
        lax.all_to_all(v_split, "head", split_axis=1, concat_axis=0, tiled=True),
    )
    local_blocks = q_heads.shape[0] // BLOCK
    q_blocks = q_heads.reshape(local_blocks, BLOCK, heads_here, HD)
    k_blocks = k_heads.reshape(local_blocks, BLOCK, heads_here, HD)
    v_blocks = v_heads.reshape(local_blocks, BLOCK, heads_here, HD)
    capacity = (local_blocks * RSEL + ctx_count - 1) // ctx_count + 1
    slots = local_blocks * RSEL
    owners, within, position = route_tables(picks, local_blocks, ctx_count)
    mine_owner = lax.dynamic_index_in_dim(owners, my_index, 0, keepdims=False)
    mine_pos = lax.dynamic_index_in_dim(position, my_index, 0, keepdims=False)
    slot_ids = jnp.arange(capacity, dtype=jnp.int32)
    asked = (owners == my_index)[:, :, None] & (position[:, :, None] == slot_ids[None, None, :])
    wanted = jnp.sum(asked.astype(jnp.int32) * within[:, :, None], axis=1)
    pick_back = mine_owner * capacity + mine_pos

    def own_pair(blocks):
        return block_pair(blocks[0], blocks[1], blocks[2], score_scale)

    own_out, own_max, own_sum = lax.map(own_pair, (q_blocks, k_blocks, v_blocks))
    owner_ids = jnp.arange(ctx_count, dtype=jnp.int32)
    chosen = (mine_owner[:, None, None] == owner_ids[None, :, None]) & (
        mine_pos[:, None, None] == slot_ids[None, None, :]
    )
    query_of_slot = jnp.arange(slots, dtype=jnp.int32) // RSEL
    source_block = jnp.sum(chosen.astype(jnp.int32) * query_of_slot[:, None, None], axis=0)
    send_queries = q_blocks[source_block]
    arrived = lax.all_to_all(send_queries, "ctx", split_axis=0, concat_axis=0, tiled=True)
    arrived_flat = arrived.reshape(ctx_count * capacity, BLOCK, heads_here, HD)

    def owner_pair(items):
        query_block, block_index = items
        return block_pair(query_block, k_blocks[block_index], v_blocks[block_index], score_scale)

    remote_out, remote_max, remote_sum = lax.map(owner_pair, (arrived_flat, wanted.reshape(-1)))
    remote_out = remote_out.reshape(ctx_count, capacity, BLOCK, heads_here, HD)
    remote_max = remote_max.reshape(ctx_count, capacity, heads_here, BLOCK)
    remote_sum = remote_sum.reshape(ctx_count, capacity, heads_here, BLOCK)
    back_out, back_max, back_sum = (
        lax.all_to_all(remote_out, "ctx", split_axis=0, concat_axis=0, tiled=True),
        lax.all_to_all(remote_max, "ctx", split_axis=0, concat_axis=0, tiled=True),
        lax.all_to_all(remote_sum, "ctx", split_axis=0, concat_axis=0, tiled=True),
    )
    far_out = back_out.reshape(ctx_count * capacity, BLOCK, heads_here, HD)[pick_back]
    far_max = back_max.reshape(ctx_count * capacity, heads_here, BLOCK)[pick_back]
    far_sum = back_sum.reshape(ctx_count * capacity, heads_here, BLOCK)[pick_back]
    far_out = far_out.reshape(local_blocks, RSEL, BLOCK, heads_here, HD)
    far_max = far_max.reshape(local_blocks, RSEL, heads_here, BLOCK)
    far_sum = far_sum.reshape(local_blocks, RSEL, heads_here, BLOCK)
    overall = jnp.maximum(own_max, jnp.max(far_max, axis=1))
    own_factor = jnp.exp(own_max - overall)
    far_factor = jnp.exp(far_max - overall[:, None])
    numer = own_out * jnp.transpose(own_factor, (0, 2, 1))[..., None]
    numer = numer + jnp.sum(far_out * jnp.transpose(far_factor, (0, 1, 3, 2))[..., None], axis=1)
    denom = own_sum * own_factor + jnp.sum(far_sum * far_factor, axis=1)
    result = (numer / jnp.transpose(denom, (0, 2, 1))[..., None]).astype(jnp.bfloat16)
    result = result.reshape(local_blocks * BLOCK, heads_here, HD)
    restored = lax.all_to_all(result, "head", split_axis=0, concat_axis=1, tiled=True)
    return restored.reshape(tok_rows, HEADS * HD)


def solution(mesh):
    placed = (P(("ctx", "head"), None), P(("ctx", "head"), None), P(("ctx", "head"), None), P())
    return jax.shard_map(
        local, mesh=mesh, in_specs=placed, out_specs=P(("ctx", "head"), None), check_vma=False
    )
```

profile of v0, /device:TPU:1, one launch (start us, length us, event | category | flops | bytes accessed | tf_op | source)
XLA Modules:
  0.0 578.9 jit_solution(18382969166931936499)
XLA Ops:
  0.0 2.4 copy.120
  2.4 6.9 %all-to-all-start.1 = ((bf16[256,16,128]{0,2,1:T(8,128)(2,1)}), bf16[256,16,128]{0,2,1:T(8,128)(2,1)S(1)}, u32[]{:S(2)}, u32[]{:S(2)}) async-start(bf16[256,16,128]{0,2,1:T(8,128)(2,1)} %bitcast.22), calls=%async_computation.1 | async-start | bytes 2097152 | tf_op jit(solution)/shard_map/all_to_all | solution.py:51
  10.6 14.5 %all-to-all-done.1 = bf16[256,16,128]{0,2,1:T(8,128)(2,1)S(1)} async-done(((bf16[256,16,128]{0,2,1:T(8,128)(2,1)}), bf16[256,16,128]{0,2,1:T(8,128)(2,1)S(1)}, u32[]{:S(2)}, u32[]{:S(2)}) %all-to-all-start.1) | async-done | bytes 1048608 | tf_op jit(solution)/shard_map/all_to_all | solution.py:51
  25.1 4.3 all-to-all-start
  29.7 2.3 copy.122
  32.7 12.7 %all-to-all-done = bf16[256,16,128]{0,2,1:T(8,128)(2,1)S(1)} async-done(((bf16[256,16,128]{0,2,1:T(8,128)(2,1)}), bf16[256,16,128]{0,2,1:T(8,128)(2,1)S(1)}, u32[]{:S(2)}, u32[]{:S(2)}) %all-to-all-start) | async-done | bytes 1048608 | tf_op jit(solution)/shard_map/all_to_all | solution.py:53
  45.3 4.9 all-to-all-start.2
  51.3 3.1 gather_fusion
  54.4 11.9 %all-to-all-done.2 = bf16[256,16,128]{0,2,1:T(8,128)(2,1)} async-done(((bf16[256,16,128]{0,2,1:T(8,128)(2,1)}), bf16[256,16,128]{0,2,1:T(8,128)(2,1)}, u32[]{:S(2)}, u32[]{:S(2)}) %all-to-all-start.2) | async-done | bytes 1048608 | tf_op jit(solution)/shard_map/all_to_all | solution.py:52
  66.3 10.5 %all-to-all-start.3 = ((bf16[16,2,512,1,128]{4,2,1,3,0:T(8,128)(2,1)}), bf16[16,2,512,1,128]{4,2,1,3,0:T(8,128)(2,1)}, u32[]{:S(2)}, u32[]{:S(2)}) async-start(bf16[16,2,512,1,128]{4,2,1,3,0:T(8,128)(2,1)} %bitcast.142), calls=%async_computation.3 | async-start | bytes 8388608 | tf_op jit(solution)/shard_map/all_to_all | solution.py:80
  78.1 1.6 copy.123
  79.7 93.3 %all-to-all-done.3 = bf16[16,2,512,1,128]{4,2,1,3,0:T(8,128)(2,1)} async-done(((bf16[16,2,512,1,128]{4,2,1,3,0:T(8,128)(2,1)}), bf16[16,2,512,1,128]{4,2,1,3,0:T(8,128)(2,1)}, u32[]{:S(2)}, u32[]{:S(2)}) %all-to-all-start.3) | async-done | bytes 4194336 | tf_op jit(solution)/shard_map/all_to_all | solution.py:80
  173.0 152.0 %while.29 = (s32[]{:T(128)}, f32[32,512,1,128]{1,3,2,0:T(8,128)}, f32[32,1,512]{2,1,0:T(1,128)S(1)}, f32[32,1,512]{2,1,0:T(1,128)S(1)}, s32[32]{0:T(128)S(1)}, /...) while((s32[]{:T(128)}, f32[32,512,1,128]{1,3,2,0:T(8,128)}, ...), condition=%wide.region_11.12_spmd, body=%wide.region_8.11_spmd.sunk | while | flops 135789568 | bytes 3818663 | solution.py:87
  325.8 7.0 %all-to-all-start.4 = ((f32[16,2,1,512]{3,1,2,0:T(2,128)}), f32[16,2,1,512]{3,1,2,0:T(2,128)S(1)}, u32[]{:S(2)}, u32[]{:S(2)}) async-start(f32[16,2,1,512]{3,1,2,0:T(2,128)} %reshape.320), calls=%async_computation.4 | async-start | bytes 131072 | tf_op jit(solution)/shard_map/all_to_all | solution.py:93
  333.0 8.8 %all-to-all-done.4 = f32[16,2,1,512]{3,1,2,0:T(2,128)S(1)} async-done(((f32[16,2,1,512]{3,1,2,0:T(2,128)}), f32[16,2,1,512]{3,1,2,0:T(2,128)S(1)}, u32[]{:S(2)}, u32[]{:S(2)}) %all-to-all-start.4) | async-done | bytes 65568 | tf_op jit(solution)/shard_map/all_to_all | solution.py:93
  341.7 11.4 %all_to_all.80 = f32[16,2,1,512]{3,1,2,0:T(2,128)S(1)} all-to-all(f32[16,2,1,512]{3,1,2,0:T(2,128)S(1)} %reshape.326), channel_id=1, replica_groups=mesh['head'=16,'ctx'=16] {'ctx'}, dimensions={0} | all-to-all | bytes 131072 | tf_op jit(solution)/shard_map/all_to_all | solution.py:94
  353.2 4.7 all-to-all-start.5
  358.0 12.5 %while.28 = (s32[]{:T(128)}, f32[8,512,1,128]{1,3,2,0:T(8,128)}, f32[8,1,512]{2,1,0:T(1,128)S(1)}, f32[8,1,512]{2,1,0:T(1,128)S(1)}, bf16[8,512,1,128]{3,1,2,0:T...) while((s32[]{:T(128)}, f32[8,512,1,128]{1,3,2,0:T(8,128)}, ...), condition=%wide.region_3.4_spmd, body=%wide.region_0.3_spmd.sunk | while | flops 135789568 | bytes 3819609 | solution.py:72
  372.1 169.2 %all-to-all-done.5 = f32[16,2,512,1,128]{2,4,1,3,0:T(8,128)} async-done(((f32[16,2,512,1,128]{2,4,1,3,0:T(8,128)}), f32[16,2,512,1,128]{2,4,1,3,0:T(8,128)}, u32[]{:S(2)}, u32[]{:S(2)}) %all-to-all-start.5) | async-done | bytes 8388640 | tf_op jit(solution)/shard_map/all_to_all | solution.py:92
  541.3 6.2 %gather_fusion.2 = f32[16,512,128]{1,2,0:T(8,128)} fusion(f32[32,512,128]{1,2,0:T(8,128)} %bitcast.44, s32[1024]{0:T(1024)S(1)} %pad_clamp_fusion), kind=kCustom, calls=%fused_computation.2 | custom fusion | bytes 8388672 | tf_op jit(solution)/shard_map/gather | solution.py:96
  547.5 3.1 multiply_reduce_fusion
  552.4 1.4 reduce.19
  554.1 21.6 %all_to_all.81 = bf16[16,2,16384]{2,1,0:T(2,128)(2,1)S(1)} all-to-all(bf16[16,2,16384]{2,1,0:T(2,128)(2,1)S(1)} %reshape.387), channel_id=1, replica_groups=mesh['head'=16,'ctx'=16] {'head'}, dimensions={0} | all-to-all | bytes 2097152 | tf_op jit(solution)/shard_map/all_to_all | solution.py:110
  577.4 1.4 copy.143
  (256 shorter events, 120.7 us)
Async XLA Ops:
  0.0 9.3 %copy-start.1 = (bf16[256,2048]{1,0:T(8,128)(2,1)S(1)}, bf16[256,2048]{1,0:T(8,128)(2,1)}, u32[]{:S(2)}) copy-start(bf16[256,2048]{1,0:T(8,128)(2,1)} %param.10) | copy-start | bytes 3145732
  0.0 29.4 %copy-start.2 = (s32[128,2]{0,1:T(2,128)S(1)}, s32[128,2]{0,1:T(2,128)}, u32[]{:S(2)}) copy-start(s32[128,2]{0,1:T(2,128)} %param.11) | copy-start | bytes 3076
  2.4 22.7 %all-to-all-start.1 = ((bf16[256,16,128]{0,2,1:T(8,128)(2,1)}), bf16[256,16,128]{0,2,1:T(8,128)(2,1)S(1)}, u32[]{:S(2)}, u32[]{:S(2)}) async-start(bf16[256,16,128]{0,2,1:T(8,128)(2,1)} %bitcast.22), calls=%async_computation.1 | async-start | bytes 2097152 | tf_op jit(solution)/shard_map/all_to_all | solution.py:51
  25.1 20.2 %all-to-all-start = ((bf16[256,16,128]{0,2,1:T(8,128)(2,1)}), bf16[256,16,128]{0,2,1:T(8,128)(2,1)S(1)}, u32[]{:S(2)}, u32[]{:S(2)}) async-start(bf16[256,16,128]{0,2,1:T(8,128)(2,1)} %bitcast.17), calls=%async_computation | async-start | bytes 2097152 | tf_op jit(solution)/shard_map/all_to_all | solution.py:53
  45.3 21.0 %all-to-all-start.2 = ((bf16[256,16,128]{0,2,1:T(8,128)(2,1)}), bf16[256,16,128]{0,2,1:T(8,128)(2,1)}, u32[]{:S(2)}, u32[]{:S(2)}) async-start(bf16[256,16,128]{0,2,1:T(8,128)(2,1)} %bitcast.27), calls=%async_computation.2 | async-start | bytes 2097152 | tf_op jit(solution)/shard_map/all_to_all | solution.py:52
  66.3 106.7 %all-to-all-start.3 = ((bf16[16,2,512,1,128]{4,2,1,3,0:T(8,128)(2,1)}), bf16[16,2,512,1,128]{4,2,1,3,0:T(8,128)(2,1)}, u32[]{:S(2)}, u32[]{:S(2)}) async-start(bf16[16,2,512,1,128]{4,2,1,3,0:T(8,128)(2,1)} %bitcast.142), calls=%async_computation.3 | async-start | bytes 8388608 | tf_op jit(solution)/shard_map/all_to_all | solution.py:80
  325.8 15.9 %all-to-all-start.4 = ((f32[16,2,1,512]{3,1,2,0:T(2,128)}), f32[16,2,1,512]{3,1,2,0:T(2,128)S(1)}, u32[]{:S(2)}, u32[]{:S(2)}) async-start(f32[16,2,1,512]{3,1,2,0:T(2,128)} %reshape.320), calls=%async_computation.4 | async-start | bytes 131072 | tf_op jit(solution)/shard_map/all_to_all | solution.py:93
  353.2 188.1 %all-to-all-start.5 = ((f32[16,2,512,1,128]{2,4,1,3,0:T(8,128)}), f32[16,2,512,1,128]{2,4,1,3,0:T(8,128)}, u32[]{:S(2)}, u32[]{:S(2)}) async-start(f32[16,2,512,1,128]{2,4,1,3,0:T(8,128)} %bitcast.144), calls=%async_computation.5 | async-start | bytes 16777216 | tf_op jit(solution)/shard_map/all_to_all | solution.py:92
  547.5 3.2 copy-start
where the time goes:
time: 589 us; the launch traced here: 579 us
  waiting for transfers between devices  310 us (53%)
  matrix products  83 us (14%)
  loops' own time  54.6 us (9%)
  local copies, waits for them, and re-layouts  44.7 us (8%)
  starting transfers between devices  38.4 us (7%)
  blocking collectives  33 us (6%)
  other arithmetic  14.5 us (2%)
    all_to_all x1, waiting for transfers between devices, local(): lax.all_to_all(remote_out, 'ctx', split_axis=0, concat_axis=0, tiled=True)  169 us
    all_to_all x1, waiting for transfers between devices, local(): lax.all_to_all(send_queries, 'ctx', split_axis=0, concat_axis=0, tiled=True)  93.3 us
    another operation x1, loops' own time, local(): lax.map(owner_pair, (arrived_flat, wanted.reshape(-1)))  54.5 us
    dot_general x40, matrix products, block_pair(): jnp.einsum('qhd,khd->hqk', query_block, key_block, preferred_element_type...  41.5 us
    dot_general x40, matrix products, block_pair(): jnp.einsum('hqk,khd->qhd', weights, value_block, preferred_element_type=j...  41.5 us
    all_to_all x1, blocking collectives, local(): lax.all_to_all(result, 'head', split_axis=0, concat_axis=1, tiled=True)  21.6 us
    dynamic_slice x32, local copies, waits for them, and re-layouts, local(): lax.map(owner_pair, (arrived_flat, wanted.reshape(-1)))  18.6 us
    all_to_all x1, waiting for transfers between devices, local(): lax.all_to_all(q_split, 'head', split_axis=1, concat_axis=0, tiled=True)  14.5 us
  transfers between devices with their start and end apart: 6, of which 6 were waited for; matrix products, arithmetic and copies ran while one was open for 4% of the time, Pallas kernels for 0%

commit v1 on v0

v1 whole, which is shorter than its diff:
```python
import functools
import math

import jax
import jax.numpy as jnp
from jax import lax
from jax.experimental import pallas as pl
from jax.experimental.pallas import tpu as pltpu
from jax.sharding import PartitionSpec as P

HEADS = 16
HD = 128
BLOCK = 512
RSEL = 2


def route_tables(picks, local_blocks, ctx_count):
    slots = local_blocks * RSEL
    owners = (picks // local_blocks).reshape(ctx_count, slots)
    within = (picks % local_blocks).reshape(ctx_count, slots)
    owner_ids = jnp.arange(ctx_count, dtype=jnp.int32)
    one_hot = (owners[:, :, None] == owner_ids[None, None, :]).astype(jnp.int32)
    running = jnp.cumsum(one_hot, axis=1)
    position = jnp.sum(one_hot * running, axis=-1) - 1
    return (owners, within, position)


def slot_attention(q, k, v, scale):
    scores = lax.dot_general(
        q, k, (((1,), (1,)), ((), ())), preferred_element_type=jnp.float32
    ) * scale
    row_max = jnp.max(scores, axis=1, keepdims=True)
    exponent = jnp.exp(scores - row_max)
    row_sum = jnp.sum(exponent, axis=1, keepdims=True)
    partial = jnp.dot(
        exponent.astype(jnp.bfloat16), v, preferred_element_type=jnp.float32
    )
    return row_max, row_sum, partial


def attend_kernel(idx_ref, q_ref, kv_ref, far0_ref, far1_ref, o_ref, *, heads_here, scale):
    for h in range(heads_here):
        cols = slice(h * HD, (h + 1) * HD)
        q = q_ref[0, :, cols]
        parts = [
            slot_attention(q, kv_ref[0, 0, :, cols], kv_ref[1, 0, :, cols], scale),
            slot_attention(q, far0_ref[0, 0, :, cols], far0_ref[1, 0, :, cols], scale),
            slot_attention(q, far1_ref[0, 0, :, cols], far1_ref[1, 0, :, cols], scale),
        ]
        top = jnp.maximum(jnp.maximum(parts[0][0], parts[1][0]), parts[2][0])
        numer = None
        denom = None
        for row_max, row_sum, partial in parts:
            factor = jnp.exp(row_max - top)
            numer = partial * factor if numer is None else numer + partial * factor
            denom = row_sum * factor if denom is None else denom + row_sum * factor
        o_ref[0, :, cols] = (numer / denom).astype(o_ref.dtype)


def attend(far_index, q_blocks, kv_blocks, far_kv, scale):
    local_blocks, _, width = q_blocks.shape
    heads_here = width // HD
    kernel = functools.partial(attend_kernel, heads_here=heads_here, scale=scale)
    grid_spec = pltpu.PrefetchScalarGridSpec(
        num_scalar_prefetch=1,
        grid=(local_blocks,),
        in_specs=[
            pl.BlockSpec((1, BLOCK, width), lambda i, idx: (i, 0, 0)),
            pl.BlockSpec((2, 1, BLOCK, width), lambda i, idx: (0, i, 0, 0)),
            pl.BlockSpec((2, 1, BLOCK, width), lambda i, idx: (0, idx[i * RSEL], 0, 0)),
            pl.BlockSpec((2, 1, BLOCK, width), lambda i, idx: (0, idx[i * RSEL + 1], 0, 0)),
        ],
        out_specs=pl.BlockSpec((1, BLOCK, width), lambda i, idx: (i, 0, 0)),
    )
    flops = local_blocks * heads_here * 3 * 4 * BLOCK * BLOCK * HD
    return pl.pallas_call(
        kernel,
        out_shape=jax.ShapeDtypeStruct((local_blocks, BLOCK, width), jnp.bfloat16),
        grid_spec=grid_spec,
        cost_estimate=pl.CostEstimate(
            flops=flops,
            transcendentals=local_blocks * heads_here * 3 * BLOCK * BLOCK,
            bytes_accessed=local_blocks * BLOCK * width * 2 * 8,
        ),
    )(far_index, q_blocks, kv_blocks, far_kv, far_kv)


def local(queries, keys, values, picks):
    head_count = lax.axis_size("head")
    ctx_count = lax.axis_size("ctx")
    my_index = lax.axis_index("ctx")
    heads_here = HEADS // head_count
    width = heads_here * HD
    tok_rows = queries.shape[0]
    score_scale = 1.0 / math.sqrt(HD)
    kv_split = jnp.stack([keys, values]).reshape(2, tok_rows, HEADS, HD)
    kv_heads = lax.all_to_all(kv_split, "head", split_axis=2, concat_axis=1, tiled=True)
    q_heads = lax.all_to_all(
        queries.reshape(tok_rows, HEADS, HD), "head", split_axis=1, concat_axis=0, tiled=True
    )
    local_blocks = q_heads.shape[0] // BLOCK
    q_blocks = q_heads.reshape(local_blocks, BLOCK, width)
    kv_blocks = kv_heads.reshape(2, local_blocks, BLOCK, width)

    capacity = (local_blocks * RSEL + ctx_count - 1) // ctx_count + 1
    owners, within, position = route_tables(picks, local_blocks, ctx_count)
    mine_owner = lax.dynamic_index_in_dim(owners, my_index, 0, keepdims=False)
    mine_pos = lax.dynamic_index_in_dim(position, my_index, 0, keepdims=False)
    slot_ids = jnp.arange(capacity, dtype=jnp.int32)
    asked = (owners == my_index)[:, :, None] & (position[:, :, None] == slot_ids[None, None, :])
    wanted = jnp.sum(asked.astype(jnp.int32) * within[:, :, None], axis=1)
    far_index = (mine_owner * capacity + mine_pos).astype(jnp.int32)

    send_kv = kv_blocks[:, wanted.reshape(-1)].reshape(
        2, ctx_count, capacity, BLOCK, width
    )
    got_kv = lax.all_to_all(send_kv, "ctx", split_axis=1, concat_axis=1, tiled=True)
    far_kv = got_kv.reshape(2, ctx_count * capacity, BLOCK, width)

    result = attend(far_index, q_blocks, kv_blocks, far_kv, score_scale)
    result = result.reshape(local_blocks * BLOCK, heads_here, HD)
    restored = lax.all_to_all(result, "head", split_axis=0, concat_axis=1, tiled=True)
    return restored.reshape(tok_rows, HEADS * HD)


def solution(mesh):
    placed = (P(("ctx", "head"), None), P(("ctx", "head"), None), P(("ctx", "head"), None), P())
    return jax.shard_map(
        local, mesh=mesh, in_specs=placed, out_specs=P(("ctx", "head"), None), check_vma=False
    )
```

time: 589 us -> 327 us (0.56)
  waiting for transfers between devices: 310 us -> 217 us
  matrix products: 83 us -> 0 us
  loops' own time: 54.6 us -> 0 us
  starting transfers between devices: 38.4 us -> 22.7 us
  Pallas kernels: 0 us -> 15 us
  blocking collectives: 33 us -> 19.5 us
  other arithmetic: 14.5 us -> 5.73 us
    all_to_all x6 -> x3, waiting for transfers between devices: 310 us -> 217 us  [the longest x1 184 us: local(): lax.all_to_all(send_kv, 'ctx', split_axis=1, concat_axis=1, tiled=True)]
    dot_general x80 -> x0, matrix products: 83 us -> none  [the longest x40 41.5 us: block_pair(): jnp.einsum('qhd,khd->hqk', query_block, key_block, preferred_element_type...]
    another operation x2 -> x0, loops' own time: 54.6 us -> none  [the longest x1 54.5 us: local(): lax.map(owner_pair, (arrived_flat, wanted.reshape(-1)))]
    dynamic_slice x32 -> x0, local copies, waits for them, and re-layouts: 18.6 us -> none  [local(): lax.map(owner_pair, (arrived_flat, wanted.reshape(-1)))]
    all_to_all x6 -> x3, starting transfers between devices: 38.4 us -> 22.7 us  [the longest x1 10.4 us: local(): lax.all_to_all(send_kv, 'ctx', split_axis=1, concat_axis=1, tiled=True)]
    pallas_call x0 -> x1, Pallas kernels: none -> 15 us  [attend(): pl.pallas_call(kernel, out_shape=jax.ShapeDtypeStruct((local_blocks, BLOC...]
    all_to_all x1 -> x0, blocking collectives: 11.4 us -> none  [local(): lax.all_to_all(remote_sum, 'ctx', split_axis=0, concat_axis=0, tiled=True)]
    reduce_sum x43 -> x0, other arithmetic: 11.1 us -> none  [the longest x40 7.82 us: block_pair(): row_sum = jnp.sum(exponent, axis=-1)]
  transfers between devices with their start and end apart: 6 -> 3, of which waited for: 6 -> 3; matrix products, arithmetic and copies ran while one was open for 4% -> 3% of each run, Pallas kernels for 0% -> 0%
where the time goes in v1:
time: 327 us; the launch traced here: 322 us
  waiting for transfers between devices  217 us (66%)
  local copies, waits for them, and re-layouts  41.3 us (13%)
  starting transfers between devices  22.7 us (7%)
  blocking collectives  19.5 us (6%)
  Pallas kernels  15 us (5%)
  other arithmetic  5.73 us (2%)
    all_to_all x1, waiting for transfers between devices, local(): lax.all_to_all(send_kv, 'ctx', split_axis=1, concat_axis=1, tiled=True)  184 us
    all_to_all x1, waiting for transfers between devices, local(): lax.all_to_all(kv_split, 'head', split_axis=2, concat_axis=1, tiled=True)  25.8 us
    all_to_all x1, blocking collectives, local(): lax.all_to_all(result, 'head', split_axis=0, concat_axis=1, tiled=True)  19.5 us
    pallas_call x1, Pallas kernels, attend(): pl.pallas_call(kernel, out_shape=jax.ShapeDtypeStruct((local_blocks, BLOC...  15 us
    unnamed x17, local copies, waits for them, and re-layouts  11.8 us
    all_to_all x1, starting transfers between devices, local(): lax.all_to_all(send_kv, 'ctx', split_axis=1, concat_axis=1, tiled=True)  10.4 us
    reshape x1, local copies, waits for them, and re-layouts, local(): kv_blocks[:, wanted.reshape(-1)]  7.6 us
    all_to_all x1, local copies, waits for them, and re-layouts, local(): lax.all_to_all(send_kv, 'ctx', split_axis=1, concat_axis=1, tiled=True)  7.6 us
  transfers between devices with their start and end apart: 3, of which 3 were waited for; matrix products, arithmetic and copies ran while one was open for 3% of the time, Pallas kernels for 0%

profile of v1, /device:TPU:1, one launch (start us, length us, event | category | flops | bytes accessed | tf_op | source)
XLA Modules:
  0.0 321.5 jit_solution(7285197011315412540)
XLA Ops:
  0.0 2.4 copy.62
  2.4 1.3 copy.63
  3.7 1.7 pad_maximum_fusion
  5.5 2.4 copy.64
  7.9 7.0 %all-to-all-start.1 = ((bf16[2,256,16,128]{3,1,0,2:T(8,128)(2,1)}), bf16[2,256,16,128]{3,1,0,2:T(8,128)(2,1)S(1)}, u32[]{:S(2)}, u32[]{:S(2)}) async-start(bf16[2,256,16,128]{3,1,0,2:T(8,128)(2,1)} %copy.64), calls=%async_computation.1 | async-start | bytes 4194304 | tf_op jit(solution)/shard_map/all_to_all | solution.py:97
  16.3 25.8 %all-to-all-done.1 = bf16[2,256,16,128]{3,1,0,2:T(8,128)(2,1)S(1)} async-done(((bf16[2,256,16,128]{3,1,0,2:T(8,128)(2,1)}), bf16[2,256,16,128]{3,1,0,2:T(8,128)(2,1)S(1)}, u32[]{:S(2)}, u32[]{:S(2)}) %all-to-all-start.1) | async-done | bytes 2097184 | tf_op jit(solution)/shard_map/all_to_all | solution.py:97
  42.0 1.3 copy-done.2
  43.4 1.7 copy.65
  45.1 4.9 %gather_fusion = bf16[32,2,512,128]{3,2,1,0:T(8,128)(2,1)} fusion(bf16[2,8,512,128]{3,2,1,0:T(8,128)(2,1)S(1)} %bitcast.27, s32[1024]{0:T(1024)S(1)} %pad_clamp_fusion), kind=kCustom, calls=%fused_computation | custom fusion | bytes 16777344 | tf_op jit(solution)/shard_map/gather | solution.py:114
  50.0 7.6 %copy.69 = bf16[2,16,2,512,128]{4,3,2,0,1:T(8,128)(2,1)} copy(bf16[2,16,2,512,128]{4,3,0,2,1:T(8,128)(2,1)} %bitcast.31) | data formatting | bytes 16777216 | tf_op jit(solution)/shard_map/reshape | solution.py:114
  57.6 10.4 %all-to-all-start.2 = ((bf16[2,16,2,512,128]{4,3,2,0,1:T(8,128)(2,1)}), bf16[2,16,2,512,128]{4,3,2,0,1:T(8,128)(2,1)}, u32[]{:S(2)}, u32[]{:S(2)}) async-start(bf16[2,16,2,512,128]{4,3,2,0,1:T(8,128)(2,1)} %copy.69), calls=%async_computation.2 | async-start | bytes 16777216 | tf_op jit(solution)/shard_map/all_to_all | solution.py:117
  68.1 1.2 copy_bitcast_fusion
  69.3 183.8 %all-to-all-done.2 = bf16[2,16,2,512,128]{4,3,2,0,1:T(8,128)(2,1)} async-done(((bf16[2,16,2,512,128]{4,3,2,0,1:T(8,128)(2,1)}), bf16[2,16,2,512,128]{4,3,2,0,1:T(8,128)(2,1)}, u32[]{:S(2)}, u32[]{:S(2)}) %all-to-all-start.2) | async-done | bytes 8388640 | tf_op jit(solution)/shard_map/all_to_all | solution.py:117
  253.1 5.2 %all-to-all-start = ((bf16[256,16,128]{2,0,1:T(8,128)(2,1)}), bf16[256,16,128]{2,0,1:T(8,128)(2,1)S(1)}, u32[]{:S(2)}, u32[]{:S(2)}) async-start(bf16[256,16,128]{2,0,1:T(8,128)(2,1)} %copy_bitcast_fusion), calls=%async_computation | async-start | bytes 2097152 | tf_op jit(solution)/shard_map/all_to_all | solution.py:98
  259.0 7.6 %copy.70 = bf16[2,16,2,512,128]{4,3,2,1,0:T(8,128)(2,1)} copy(bf16[2,16,2,512,128]{4,3,2,0,1:T(8,128)(2,1)} %all-to-all-done.2) | data formatting | bytes 16777216 | tf_op jit(solution)/shard_map/all_to_all | solution.py:117
  266.6 7.6 %all-to-all-done = bf16[256,16,128]{2,0,1:T(8,128)(2,1)S(1)} async-done(((bf16[256,16,128]{2,0,1:T(8,128)(2,1)}), bf16[256,16,128]{2,0,1:T(8,128)(2,1)S(1)}, u32[]{:S(2)}, u32[]{:S(2)}) %all-to-all-start) | async-done | bytes 1048608 | tf_op jit(solution)/shard_map/all_to_all | solution.py:98
  274.2 1.0 copy-done.3
  275.2 15.0 %shard_map.46 = bf16[8,512,128]{2,1,0:T(8,128)(2,1)} custom-call(s32[16]{0:T(128)} %add_reduce_fusion.idx_ref, bf16[8,512,128]{2,1,0:T(8,128)(2,1)} %bitcast.34, bf16[2,8,512,128]{3,2,1,0:T(8,128)(2,1)} %bitcast.28, bf16[2,32,512,128]{3,2,1,0:T(8,128)(2,1)} %bitcast.29, bf16[2,32,512,128]{3,2,1,0:T(8,128)(2,1)} %bitcast.30), custom_call_target="tpu_custom_call" | custom-call | flops 3221225472 | bytes 8388608 | tf_op jit(solution)/shard_map/pallas_call | solution.py:76
  290.8 2.7 reduce.2
  293.7 19.5 %all_to_all.50 = bf16[16,2,16384]{2,1,0:T(2,128)(2,1)} all-to-all(bf16[16,2,16384]{2,1,0:T(2,128)(2,1)S(1)} %reshape.94), channel_id=1, replica_groups=mesh['head'=16,'ctx'=16] {'head'}, dimensions={0} | all-to-all | bytes 2097152 | tf_op jit(solution)/shard_map/all_to_all | solution.py:122
  313.2 4.3 %reshape.95 = bf16[4096,1,128]{2,1,0:T(2,128)(2,1)S(1)} reshape(bf16[16,2,16384]{2,1,0:T(2,128)(2,1)} %all_to_all.50) | data formatting | bytes 2097152
  317.5 1.1 copy.74
  318.6 1.5 copy.72
  320.1 1.4 copy.73
  (28 shorter events, 2.9 us)
Async XLA Ops:
  0.0 68.0 %copy-start = (bf16[256,2048]{1,0:T(8,128)(2,1)S(1)}, bf16[256,2048]{1,0:T(8,128)(2,1)}, u32[]{:S(2)}) copy-start(bf16[256,2048]{1,0:T(8,128)(2,1)} %param.4) | copy-start | bytes 3145732
  0.0 2.4 copy-start.4
  7.9 7.1 %copy-start.5 = (s32[128,2]{0,1:T(2,128)S(1)}, s32[128,2]{0,1:T(2,128)}, u32[]{:S(2)}) copy-start(s32[128,2]{0,1:T(2,128)} %param.7) | copy-start | bytes 3076
  7.9 34.2 %all-to-all-start.1 = ((bf16[2,256,16,128]{3,1,0,2:T(8,128)(2,1)}), bf16[2,256,16,128]{3,1,0,2:T(8,128)(2,1)S(1)}, u32[]{:S(2)}, u32[]{:S(2)}) async-start(bf16[2,256,16,128]{3,1,0,2:T(8,128)(2,1)} %copy.64), calls=%async_computation.1 | async-start | bytes 4194304 | tf_op jit(solution)/shard_map/all_to_all | solution.py:97
  42.0 1.4 copy-start.2
  45.1 4.9 %copy-start.1 = (bf16[2,16,256,1,128]{4,2,1,0,3:T(8,128)(2,1)}, bf16[2,16,256,1,128]{4,2,1,0,3:T(8,128)(2,1)S(1)}, u32[]{:S(2)}) copy-start(bf16[2,16,256,1,128]{4,2,1,0,3:T(8,128)(2,1)S(1)} %copy.65) | copy-start | bytes 6291460
  57.6 195.5 %all-to-all-start.2 = ((bf16[2,16,2,512,128]{4,3,2,0,1:T(8,128)(2,1)}), bf16[2,16,2,512,128]{4,3,2,0,1:T(8,128)(2,1)}, u32[]{:S(2)}, u32[]{:S(2)}) async-start(bf16[2,16,2,512,128]{4,3,2,0,1:T(8,128)(2,1)} %copy.69), calls=%async_computation.2 | async-start | bytes 16777216 | tf_op jit(solution)/shard_map/all_to_all | solution.py:117
  253.1 21.1 %all-to-all-start = ((bf16[256,16,128]{2,0,1:T(8,128)(2,1)}), bf16[256,16,128]{2,0,1:T(8,128)(2,1)S(1)}, u32[]{:S(2)}, u32[]{:S(2)}) async-start(bf16[256,16,128]{2,0,1:T(8,128)(2,1)} %copy_bitcast_fusion), calls=%async_computation | async-start | bytes 2097152 | tf_op jit(solution)/shard_map/all_to_all | solution.py:98
  274.2 1.0 copy-start.3

commit v2 on v1

v2 whole, which is shorter than its diff:
```python
import functools
import math

import jax
import jax.numpy as jnp
from jax import lax
from jax.experimental import pallas as pl
from jax.experimental.pallas import tpu as pltpu
from jax.sharding import PartitionSpec as P

MESH = pl.DeviceIdType.MESH

HEADS = 16
HD = 128
BLOCK = 512
RSEL = 2


def exchange_kernel(*refs, axis, axes, n, split_axis, concat_axis, count):
    srcs, dsts = refs[:count], refs[count:2 * count]
    send_sems, recv_sems = refs[2 * count], refs[2 * count + 1]
    me = lax.axis_index(axis)

    def device(peer):
        return tuple(peer if name == axis else lax.axis_index(name) for name in axes)

    barrier = pltpu.get_barrier_semaphore()
    for k in range(1, n):
        pl.semaphore_signal(barrier, inc=1, device_id=device((me + k) % n), device_id_type=MESH)
    pl.semaphore_wait(barrier, n - 1)

    def view(ref, dim, index):
        size = ref.shape[dim] // n
        where = [slice(None)] * len(ref.shape)
        where[dim] = pl.ds(index * size, size)
        return ref.at[tuple(where)]

    copies = []
    for a in range(count):
        own = pltpu.make_async_copy(
            view(srcs[a], split_axis, me), view(dsts[a], concat_axis, me), send_sems.at[a, 0]
        )
        own.start()
        copies.append(own)
        for k in range(1, n):
            peer = (me + k) % n
            copy = pltpu.make_async_remote_copy(
                src_ref=view(srcs[a], split_axis, peer),
                dst_ref=view(dsts[a], concat_axis, me),
                send_sem=send_sems.at[a, k],
                recv_sem=recv_sems.at[a, k],
                device_id=device(peer),
                device_id_type=MESH,
            )
            copy.start()
            copies.append(copy)
    for copy in copies:
        copy.wait()


def exchange(arrays, axis, axes, split_axis, concat_axis, collective_id):
    n = lax.axis_size(axis)
    count = len(arrays)
    out_shapes = []
    for x in arrays:
        shape = list(x.shape)
        shape[split_axis] //= n
        shape[concat_axis] *= n
        out_shapes.append(jax.ShapeDtypeStruct(tuple(shape), x.dtype))
    kernel = functools.partial(
        exchange_kernel, axis=axis, axes=axes, n=n, split_axis=split_axis,
        concat_axis=concat_axis, count=count,
    )
    return pl.pallas_call(
        kernel,
        out_shape=tuple(out_shapes),
        in_specs=[pl.BlockSpec(memory_space=pl.ANY)] * count,
        out_specs=tuple(pl.BlockSpec(memory_space=pl.ANY) for _ in range(count)),
        scratch_shapes=[
            pltpu.SemaphoreType.DMA((count, n)),
            pltpu.SemaphoreType.DMA((count, n)),
        ],
        compiler_params=pltpu.CompilerParams(collective_id=collective_id, has_side_effects=True),
    )(*arrays)


def route_tables(picks, local_blocks, ctx_count):
    slots = local_blocks * RSEL
    owners = (picks // local_blocks).reshape(ctx_count, slots)
    within = (picks % local_blocks).reshape(ctx_count, slots)
    owner_ids = jnp.arange(ctx_count, dtype=jnp.int32)
    one_hot = (owners[:, :, None] == owner_ids[None, None, :]).astype(jnp.int32)
    running = jnp.cumsum(one_hot, axis=1)
    position = jnp.sum(one_hot * running, axis=-1) - 1
    return (owners, within, position)


def slot_attention(q, k, v, scale):
    scores = lax.dot_general(
        q, k, (((1,), (1,)), ((), ())), preferred_element_type=jnp.float32
    ) * scale
    row_max = jnp.max(scores, axis=1, keepdims=True)
    exponent = jnp.exp(scores - row_max)
    row_sum = jnp.sum(exponent, axis=1, keepdims=True)
    partial = jnp.dot(
        exponent.astype(jnp.bfloat16), v, preferred_element_type=jnp.float32
    )
    return row_max, row_sum, partial


def attend_kernel(
    idx_ref, q_ref, k_ref, v_ref, fk0_ref, fv0_ref, fk1_ref, fv1_ref, o_ref, *, heads_here, scale
):
    for h in range(heads_here):
        cols = slice(h * HD, (h + 1) * HD)
        q = q_ref[0, :, cols]
        parts = [
            slot_attention(q, k_ref[0, :, cols], v_ref[0, :, cols], scale),
            slot_attention(q, fk0_ref[0, :, cols], fv0_ref[0, :, cols], scale),
            slot_attention(q, fk1_ref[0, :, cols], fv1_ref[0, :, cols], scale),
        ]
        top = jnp.maximum(jnp.maximum(parts[0][0], parts[1][0]), parts[2][0])
        numer = None
        denom = None
        for row_max, row_sum, partial in parts:
            factor = jnp.exp(row_max - top)
            numer = partial * factor if numer is None else numer + partial * factor
            denom = row_sum * factor if denom is None else denom + row_sum * factor
        o_ref[0, :, cols] = (numer / denom).astype(o_ref.dtype)


def attend(far_index, q_blocks, k_blocks, v_blocks, far_k, far_v, scale):
    local_blocks, _, width = q_blocks.shape
    heads_here = width // HD
    kernel = functools.partial(attend_kernel, heads_here=heads_here, scale=scale)
    grid_spec = pltpu.PrefetchScalarGridSpec(
        num_scalar_prefetch=1,
        grid=(local_blocks,),
        in_specs=[
            pl.BlockSpec((1, BLOCK, width), lambda i, idx: (i, 0, 0)),
            pl.BlockSpec((1, BLOCK, width), lambda i, idx: (i, 0, 0)),
            pl.BlockSpec((1, BLOCK, width), lambda i, idx: (i, 0, 0)),
            pl.BlockSpec((1, BLOCK, width), lambda i, idx: (idx[i * RSEL], 0, 0)),
            pl.BlockSpec((1, BLOCK, width), lambda i, idx: (idx[i * RSEL], 0, 0)),
            pl.BlockSpec((1, BLOCK, width), lambda i, idx: (idx[i * RSEL + 1], 0, 0)),
            pl.BlockSpec((1, BLOCK, width), lambda i, idx: (idx[i * RSEL + 1], 0, 0)),
        ],
        out_specs=pl.BlockSpec((1, BLOCK, width), lambda i, idx: (i, 0, 0)),
    )
    flops = local_blocks * heads_here * 3 * 4 * BLOCK * BLOCK * HD
    return pl.pallas_call(
        kernel,
        out_shape=jax.ShapeDtypeStruct((local_blocks, BLOCK, width), jnp.bfloat16),
        grid_spec=grid_spec,
        cost_estimate=pl.CostEstimate(
            flops=flops,
            transcendentals=local_blocks * heads_here * 3 * BLOCK * BLOCK,
            bytes_accessed=local_blocks * BLOCK * width * 2 * 8,
        ),
    )(far_index, q_blocks, k_blocks, v_blocks, far_k, far_v, far_k, far_v)


def local(queries, keys, values, picks, axes):
    head_count = lax.axis_size("head")
    ctx_count = lax.axis_size("ctx")
    my_index = lax.axis_index("ctx")
    heads_here = HEADS // head_count
    width = heads_here * HD
    tok_rows = queries.shape[0]
    score_scale = 1.0 / math.sqrt(HD)
    q_heads, k_heads, v_heads = exchange(
        (queries, keys, values), "head", axes, split_axis=1, concat_axis=0, collective_id=0
    )
    local_blocks = q_heads.shape[0] // BLOCK
    q_blocks = q_heads.reshape(local_blocks, BLOCK, width)
    k_blocks = k_heads.reshape(local_blocks, BLOCK, width)
    v_blocks = v_heads.reshape(local_blocks, BLOCK, width)

    capacity = (local_blocks * RSEL + ctx_count - 1) // ctx_count + 1
    owners, within, position = route_tables(picks, local_blocks, ctx_count)
    mine_owner = lax.dynamic_index_in_dim(owners, my_index, 0, keepdims=False)
    mine_pos = lax.dynamic_index_in_dim(position, my_index, 0, keepdims=False)
    slot_ids = jnp.arange(capacity, dtype=jnp.int32)
    asked = (owners == my_index)[:, :, None] & (position[:, :, None] == slot_ids[None, None, :])
    wanted = jnp.sum(asked.astype(jnp.int32) * within[:, :, None], axis=1)
    far_index = (mine_owner * capacity + mine_pos).astype(jnp.int32)

    send_k = k_blocks[wanted.reshape(-1)]
    send_v = v_blocks[wanted.reshape(-1)]
    far_k, far_v = exchange(
        (send_k, send_v), "ctx", axes, split_axis=0, concat_axis=0, collective_id=1
    )

    result = attend(far_index, q_blocks, k_blocks, v_blocks, far_k, far_v, score_scale)
    result = result.reshape(local_blocks * BLOCK, width)
    (restored,) = exchange((result,), "head", axes, split_axis=0, concat_axis=1, collective_id=2)
    return restored


def solution(mesh):
    placed = (P(("ctx", "head"), None), P(("ctx", "head"), None), P(("ctx", "head"), None), P())
    return jax.shard_map(
        functools.partial(local, axes=tuple(mesh.axis_names)), mesh=mesh, in_specs=placed, out_specs=P(("ctx", "head"), None), check_vma=False
    )
```

time: 327 us -> 298 us (0.911); the launches traced: 322 us -> 298 us
  Pallas kernels: 15 us -> 285 us
  waiting for transfers between devices: 217 us -> 0 us
  local copies, waits for them, and re-layouts: 41.3 us -> 10.4 us
  starting transfers between devices: 22.7 us -> 0 us
  blocking collectives: 19.5 us -> 0 us
  other arithmetic: 5.73 us -> 1.99 us
    pallas_call x0 -> x3, Pallas kernels: none -> 270 us  [exchange(): pl.pallas_call(kernel, out_shape=tuple(out_shapes), in_specs=[pl.BlockSpe...]
    all_to_all x3 -> x0, waiting for transfers between devices: 217 us -> none  [the longest x1 184 us: local(): lax.all_to_all(send_kv, 'ctx', split_axis=1, concat_axis=1, tiled=True)]
    all_to_all x3 -> x0, starting transfers between devices: 22.7 us -> none  [the longest x1 10.4 us: local(): lax.all_to_all(send_kv, 'ctx', split_axis=1, concat_axis=1, tiled=True)]
    all_to_all x1 -> x0, blocking collectives: 19.5 us -> none  [local(): lax.all_to_all(result, 'head', split_axis=0, concat_axis=1, tiled=True)]
    all_to_all x3 -> x0, local copies, waits for them, and re-layouts: 10.8 us -> none  [the longest x1 7.6 us: local(): lax.all_to_all(send_kv, 'ctx', split_axis=1, concat_axis=1, tiled=True)]
    reshape x5 -> x1, local copies, waits for them, and re-layouts: 10.9 us -> 0.09 us  [local(): send_k = k_blocks[wanted.reshape(-1)]]
    unnamed x17 -> x3, local copies, waits for them, and re-layouts: 11.8 us -> 2.31 us
    gather x1 -> x2, local copies, waits for them, and re-layouts: 4.88 us -> 7.41 us  [the longest x1 4.37 us: local(): send_k = k_blocks[wanted.reshape(-1)]]
  transfers between devices with their start and end apart: 3 -> 0, of which waited for: 3 -> 0; matrix products, arithmetic and copies ran while one was open for 3% -> 0% of each run, Pallas kernels for 0% -> 0%
where the time goes in v2:
time: 298 us
  Pallas kernels  285 us (96%)
  local copies, waits for them, and re-layouts  10.4 us (3%)
    pallas_call x3, Pallas kernels, exchange(): pl.pallas_call(kernel, out_shape=tuple(out_shapes), in_specs=[pl.BlockSpe...  270 us
    pallas_call x1, Pallas kernels, attend(): pl.pallas_call(kernel, out_shape=jax.ShapeDtypeStruct((local_blocks, BLOC...  15.4 us

profile of v2, /device:TPU:1, one launch (start us, length us, event | category | flops | bytes accessed | tf_op | source)
XLA Modules:
  0.0 297.5 jit_solution(2788662155145102979)
XLA Ops:
  0.0 0.7 and_select_fusion
  0.7 0.1 copy.23
  0.8 0.1 mul.19
  0.9 0.1 copy.19
  1.0 0.1 reshape.60
  1.1 0.1 copy.20
  1.2 0.5 fusion.4
  1.6 0.7 add_reduce_fusion.idx_ref
  2.3 0.1 copy.22
  2.4 0.1 select_reduce_fusion
  2.5 0.1 copy.24
  2.6 0.1 reshape.64
  2.7 42.9 %shard_map.46 = (bf16[4096,128]{1,0:T(8,128)(2,1)}, bf16[4096,128]{1,0:T(8,128)(2,1)}, bf16[4096,128]{1,0:T(8,128)(2,1)}) custom-call(bf16[256,2048]{1,0:T(8,128)(2,1)} %refs_0_.1, bf16[256,2048]{1,0:T(8,128)(2,1)} %refs_1_.1, bf16[256,2048]{1,0:T(8,128)(2,1)} %refs_2_.1), custom_call_target="tpu_custom_call" | custom-call | tf_op jit(solution)/shard_map/pallas_call | solution.py:74
  45.7 0.0 copy-start
  45.7 4.4 %gather_fusion = bf16[32,512,128]{2,1,0:T(8,128)(2,1)} fusion(bf16[8,512,128]{2,1,0:T(8,128)(2,1)} %bitcast.6, s32[1024]{0:T(1024)S(1)} %pad_clamp_fusion), kind=kCustom, calls=%fused_computation | custom fusion | bytes 8388736 | tf_op jit(solution)/shard_map/gather | solution.py:188
  50.0 0.0 copy-done
  50.0 3.0 %gather_fusion.1 = bf16[32,512,128]{2,1,0:T(8,128)(2,1)} fusion(bf16[8,512,128]{2,1,0:T(8,128)(2,1)S(1)} %bitcast.9, s32[1024]{0:T(1024)S(1)} %pad_clamp_fusion), kind=kCustom, calls=%fused_computation.1 | custom fusion | bytes 8388736 | tf_op jit(solution)/shard_map/gather | solution.py:189
  53.1 201.4 %shard_map.47 = (bf16[32,512,128]{2,1,0:T(8,128)(2,1)}, bf16[32,512,128]{2,1,0:T(8,128)(2,1)}) custom-call(bf16[32,512,128]{2,1,0:T(8,128)(2,1)} %gather_fusion, bf16[32,512,128]{2,1,0:T(8,128)(2,1)} %gather_fusion.1), custom_call_target="tpu_custom_call" | custom-call | tf_op jit(solution)/shard_map/pallas_call | solution.py:74
  254.5 15.4 %shard_map.48 = bf16[8,512,128]{2,1,0:T(8,128)(2,1)} custom-call(s32[16]{0:T(128)} %add_reduce_fusion.idx_ref, bf16[8,512,128]{2,1,0:T(8,128)(2,1)} %bitcast.11, bf16[8,512,128]{2,1,0:T(8,128)(2,1)} %bitcast.7, bf16[8,512,128]{2,1,0:T(8,128)(2,1)} %bitcast.8, bf16[32,512,128]{2,1,0:T(8,128)(2,1)} %get-tuple-element.13.fk0_ref.fk1_ref, ...), custom_call_target="tpu_custom_call" | custom-call | flops 3221225472 | bytes 8388608 | tf_op jit(solution)/shard_map/pallas_call | solution.py:151
  269.9 25.3 %shard_map.49 = bf16[256,2048]{1,0:T(8,128)(2,1)} custom-call(bf16[4096,128]{1,0:T(8,128)(2,1)} %bitcast.10), custom_call_target="tpu_custom_call" | custom-call | tf_op jit(solution)/shard_map/pallas_call | solution.py:74
  295.2 2.3 copy.26
  (4 shorter events, 0.0 us)
Async XLA Ops:
  45.7 4.4 %copy-start = (bf16[4096,128]{1,0:T(8,128)(2,1)S(1)}, bf16[4096,128]{1,0:T(8,128)(2,1)}, u32[]{:S(2)}) copy-start(bf16[4096,128]{1,0:T(8,128)(2,1)} %get-tuple-element.12) | copy-start | bytes 3145732

commit v3 on v2

--- a/solution.py
+++ b/solution.py
@@ -16,40 +16,50 @@
 RSEL = 2
 
 
-def exchange_kernel(*refs, axis, axes, n, split_axis, concat_axis, count):
+def exchange_kernel(*refs, axes, jobs):
+    count = len(jobs)
     srcs, dsts = refs[:count], refs[count:2 * count]
     send_sems, recv_sems = refs[2 * count], refs[2 * count + 1]
-    me = lax.axis_index(axis)
-
-    def device(peer):
+
+    def device(axis, peer):
         return tuple(peer if name == axis else lax.axis_index(name) for name in axes)
 
     barrier = pltpu.get_barrier_semaphore()
-    for k in range(1, n):
-        pl.semaphore_signal(barrier, inc=1, device_id=device((me + k) % n), device_id_type=MESH)
-    pl.semaphore_wait(barrier, n - 1)
-
-    def view(ref, dim, index):
+    peers = 0
+    for axis in sorted({job[0] for job in jobs}):
+        n = lax.axis_size(axis)
+        me = lax.axis_index(axis)
+        for k in range(1, n):
+            pl.semaphore_signal(
+                barrier, inc=1, device_id=device(axis, (me + k) % n), device_id_type=MESH
+            )
+        peers += n - 1
+    pl.semaphore_wait(barrier, peers)
+
+    def view(ref, dim, index, n):
         size = ref.shape[dim] // n
         where = [slice(None)] * len(ref.shape)
         where[dim] = pl.ds(index * size, size)
         return ref.at[tuple(where)]
 
     copies = []
-    for a in range(count):
+    for a, (axis, split_axis, concat_axis) in enumerate(jobs):
+        n = lax.axis_size(axis)
+        me = lax.axis_index(axis)
         own = pltpu.make_async_copy(
-            view(srcs[a], split_axis, me), view(dsts[a], concat_axis, me), send_sems.at[a, 0]
+            view(srcs[a], split_axis, me, n), view(dsts[a], concat_axis, me, n),
+            send_sems.at[a, 0],
         )
         own.start()
         copies.append(own)
         for k in range(1, n):
             peer = (me + k) % n
             copy = pltpu.make_async_remote_copy(
-                src_ref=view(srcs[a], split_axis, peer),
-                dst_ref=view(dsts[a], concat_axis, me),
+                src_ref=view(srcs[a], split_axis, peer, n),
+                dst_ref=view(dsts[a], concat_axis, me, n),
                 send_sem=send_sems.at[a, k],
                 recv_sem=recv_sems.at[a, k],
-                device_id=device(peer),
+                device_id=device(axis, peer),
                 device_id_type=MESH,
             )
             copy.start()
@@ -58,27 +68,24 @@
         copy.wait()
 
 
-def exchange(arrays, axis, axes, split_axis, concat_axis, collective_id):
-    n = lax.axis_size(axis)
-    count = len(arrays)
+def exchange(arrays, jobs, axes, collective_id):
     out_shapes = []
-    for x in arrays:
+    for x, (axis, split_axis, concat_axis) in zip(arrays, jobs):
+        n = lax.axis_size(axis)
         shape = list(x.shape)
         shape[split_axis] //= n
         shape[concat_axis] *= n
         out_shapes.append(jax.ShapeDtypeStruct(tuple(shape), x.dtype))
-    kernel = functools.partial(
-        exchange_kernel, axis=axis, axes=axes, n=n, split_axis=split_axis,
-        concat_axis=concat_axis, count=count,
-    )
+    widest = max(lax.axis_size(job[0]) for job in jobs)
+    count = len(arrays)
     return pl.pallas_call(
-        kernel,
+        functools.partial(exchange_kernel, axes=axes, jobs=tuple(jobs)),
         out_shape=tuple(out_shapes),
         in_specs=[pl.BlockSpec(memory_space=pl.ANY)] * count,
         out_specs=tuple(pl.BlockSpec(memory_space=pl.ANY) for _ in range(count)),
         scratch_shapes=[
-            pltpu.SemaphoreType.DMA((count, n)),
-            pltpu.SemaphoreType.DMA((count, n)),
+            pltpu.SemaphoreType.DMA((count, widest)),
+            pltpu.SemaphoreType.DMA((count, widest)),
         ],
         compiler_params=pltpu.CompilerParams(collective_id=collective_id, has_side_effects=True),
     )(*arrays)
@@ -168,11 +175,9 @@
     width = heads_here * HD
     tok_rows = queries.shape[0]
     score_scale = 1.0 / math.sqrt(HD)
-    q_heads, k_heads, v_heads = exchange(
-        (queries, keys, values), "head", axes, split_axis=1, concat_axis=0, collective_id=0
-    )
-    local_blocks = q_heads.shape[0] // BLOCK
-    q_blocks = q_heads.reshape(local_blocks, BLOCK, width)
+    head_in = ("head", 1, 0)
+    k_heads, v_heads = exchange((keys, values), (head_in, head_in), axes, collective_id=0)
+    local_blocks = k_heads.shape[0] // BLOCK
     k_blocks = k_heads.reshape(local_blocks, BLOCK, width)
     v_blocks = v_heads.reshape(local_blocks, BLOCK, width)
 
@@ -187,13 +192,15 @@
 
     send_k = k_blocks[wanted.reshape(-1)]
     send_v = v_blocks[wanted.reshape(-1)]
-    far_k, far_v = exchange(
-        (send_k, send_v), "ctx", axes, split_axis=0, concat_axis=0, collective_id=1
-    )
+    ctx_move = ("ctx", 0, 0)
+    q_heads, far_k, far_v = exchange(
+        (queries, send_k, send_v), (head_in, ctx_move, ctx_move), axes, collective_id=1
+    )
+    q_blocks = q_heads.reshape(local_blocks, BLOCK, width)
 
     result = attend(far_index, q_blocks, k_blocks, v_blocks, far_k, far_v, score_scale)
     result = result.reshape(local_blocks * BLOCK, width)
-    (restored,) = exchange((result,), "head", axes, split_axis=0, concat_axis=1, collective_id=2)
+    (restored,) = exchange((result,), (("head", 0, 1),), axes, collective_id=2)
     return restored
 
 

time: 298 us -> 287 us (0.963)
  Pallas kernels: 285 us -> 274 us
    pallas_call x3, Pallas kernels: 270 us -> 259 us  [exchange(): pl.pallas_call(functools.partial(exchange_kernel, axes=axes, jobs=tuple(j...]
where the time goes in v3:
time: 287 us
  Pallas kernels  274 us (95%)
  local copies, waits for them, and re-layouts  10.4 us (4%)
    pallas_call x3, Pallas kernels, exchange(): pl.pallas_call(functools.partial(exchange_kernel, axes=axes, jobs=tuple(j...  259 us
    pallas_call x1, Pallas kernels, attend(): pl.pallas_call(kernel, out_shape=jax.ShapeDtypeStruct((local_blocks, BLOC...  15.4 us

profile of v3, /device:TPU:1, one launch (start us, length us, event | category | flops | bytes accessed | tf_op | source)
XLA Modules:
  0.0 286.6 jit_solution(7617412089446097753)
XLA Ops:
  0.0 0.7 and_select_fusion
  0.7 0.1 copy.23
  0.8 0.1 mul.19
  0.9 0.1 copy.19
  1.0 0.1 reshape.60
  1.1 0.1 copy.20
  1.2 0.5 fusion.4
  1.6 0.7 add_reduce_fusion.idx_ref
  2.3 0.1 copy.22
  2.4 0.1 select_reduce_fusion
  2.5 0.1 copy.24
  2.6 0.1 reshape.62
  2.7 31.1 %shard_map.46 = (bf16[4096,128]{1,0:T(8,128)(2,1)}, bf16[4096,128]{1,0:T(8,128)(2,1)}) custom-call(bf16[256,2048]{1,0:T(8,128)(2,1)} %refs_0_.2, bf16[256,2048]{1,0:T(8,128)(2,1)} %refs_1_.1), custom_call_target="tpu_custom_call" | custom-call | tf_op jit(solution)/shard_map/pallas_call | solution.py:81
  33.9 0.0 copy-start
  33.9 4.4 %gather_fusion.1 = bf16[32,512,128]{2,1,0:T(8,128)(2,1)} fusion(bf16[8,512,128]{2,1,0:T(8,128)(2,1)} %bitcast.8, s32[1024]{0:T(1024)S(1)} %pad_clamp_fusion), kind=kCustom, calls=%fused_computation.1 | custom fusion | bytes 8388736 | tf_op jit(solution)/shard_map/gather | solution.py:194
  38.2 0.0 copy-done
  38.2 3.1 %gather_fusion = bf16[32,512,128]{2,1,0:T(8,128)(2,1)} fusion(bf16[8,512,128]{2,1,0:T(8,128)(2,1)S(1)} %bitcast.7, s32[1024]{0:T(1024)S(1)} %pad_clamp_fusion), kind=kCustom, calls=%fused_computation | custom fusion | bytes 8388736 | tf_op jit(solution)/shard_map/gather | solution.py:193
  41.3 207.8 %shard_map.47 = (bf16[4096,128]{1,0:T(8,128)(2,1)}, bf16[32,512,128]{2,1,0:T(8,128)(2,1)}, bf16[32,512,128]{2,1,0:T(8,128)(2,1)}) custom-call(bf16[256,2048]{1,0:T(8,128)(2,1)} %refs_0_.3, bf16[32,512,128]{2,1,0:T(8,128)(2,1)} %gather_fusion, bf16[32,512,128]{2,1,0:T(8,128)(2,1)} %gather_fusion.1), custom_call_target="tpu_custom_call" | custom-call | tf_op jit(solution)/shard_map/pallas_call | solution.py:81
  249.1 15.4 %shard_map.48 = bf16[8,512,128]{2,1,0:T(8,128)(2,1)} custom-call(s32[16]{0:T(128)} %add_reduce_fusion.idx_ref, bf16[8,512,128]{2,1,0:T(8,128)(2,1)} %bitcast.11, bf16[8,512,128]{2,1,0:T(8,128)(2,1)} %bitcast.6, bf16[8,512,128]{2,1,0:T(8,128)(2,1)} %bitcast.9, bf16[32,512,128]{2,1,0:T(8,128)(2,1)} %get-tuple-element.13.fk0_ref.fk1_ref, ...), custom_call_target="tpu_custom_call" | custom-call | flops 3221225472 | bytes 8388608 | tf_op jit(solution)/shard_map/pallas_call | solution.py:158
  264.4 19.9 %shard_map.49 = bf16[256,2048]{1,0:T(8,128)(2,1)} custom-call(bf16[4096,128]{1,0:T(8,128)(2,1)} %bitcast.10), custom_call_target="tpu_custom_call" | custom-call | tf_op jit(solution)/shard_map/pallas_call | solution.py:81
  284.3 2.3 copy.26
  (4 shorter events, 0.0 us)
Async XLA Ops:
  33.9 4.4 %copy-start = (bf16[4096,128]{1,0:T(8,128)(2,1)S(1)}, bf16[4096,128]{1,0:T(8,128)(2,1)}, u32[]{:S(2)}) copy-start(bf16[4096,128]{1,0:T(8,128)(2,1)} %get-tuple-element.10) | copy-start | bytes 3145732

commit v4 on v3

--- a/solution.py
+++ b/solution.py
@@ -116,55 +116,125 @@
 
 
 def attend_kernel(
-    idx_ref, q_ref, k_ref, v_ref, fk0_ref, fv0_ref, fk1_ref, fv1_ref, o_ref, *, heads_here, scale
+    idx_ref, q_ref, k_ref, v_ref, fk_ref, fv_ref, y_ref, stage, send_sems, recv_sems,
+    *, axes, heads_here, scale,
 ):
-    for h in range(heads_here):
-        cols = slice(h * HD, (h + 1) * HD)
-        q = q_ref[0, :, cols]
-        parts = [
-            slot_attention(q, k_ref[0, :, cols], v_ref[0, :, cols], scale),
-            slot_attention(q, fk0_ref[0, :, cols], fv0_ref[0, :, cols], scale),
-            slot_attention(q, fk1_ref[0, :, cols], fv1_ref[0, :, cols], scale),
-        ]
-        top = jnp.maximum(jnp.maximum(parts[0][0], parts[1][0]), parts[2][0])
-        numer = None
-        denom = None
-        for row_max, row_sum, partial in parts:
-            factor = jnp.exp(row_max - top)
-            numer = partial * factor if numer is None else numer + partial * factor
-            denom = row_sum * factor if denom is None else denom + row_sum * factor
-        o_ref[0, :, cols] = (numer / denom).astype(o_ref.dtype)
-
-
-def attend(far_index, q_blocks, k_blocks, v_blocks, far_k, far_v, scale):
+    n = lax.axis_size("head")
+    me = lax.axis_index("head")
+    local_blocks = q_ref.shape[0]
+    rows = y_ref.shape[0]
+    width = heads_here * HD
+    per_block = BLOCK // rows
+
+    def device(peer):
+        return tuple(peer if name == "head" else lax.axis_index(name) for name in axes)
+
+    barrier = pltpu.get_barrier_semaphore()
+    for k in range(1, n):
+        pl.semaphore_signal(barrier, inc=1, device_id=device((me + k) % n), device_id_type=MESH)
+    pl.semaphore_wait(barrier, n - 1)
+
+    mine = y_ref.at[:, pl.ds(me * width, width)]
+
+    def piece(i, r):
+        return stage.at[i, pl.ds(r * rows, rows), :]
+
+    def remote(i, r, dest):
+        return pltpu.make_async_remote_copy(
+            src_ref=piece(i, r), dst_ref=mine,
+            send_sem=send_sems.at[i * per_block + r], recv_sem=recv_sems.at[me],
+            device_id=device(dest), device_id_type=MESH,
+        )
+
+    def own(i, r):
+        return pltpu.make_async_copy(piece(i, r), mine, send_sems.at[i * per_block + r])
+
+    def send(i):
+        for r in range(per_block):
+            dest = i * per_block + r
+
+            @pl.when(dest == me)
+            def _():
+                own(i, r).start()
+
+            @pl.when(dest != me)
+            def _():
+                remote(i, r, dest).start()
+
+    def finish(i):
+        for r in range(per_block):
+            dest = i * per_block + r
+
+            @pl.when(dest == me)
+            def _():
+                own(i, r).wait()
+
+            @pl.when(dest != me)
+            def _():
+                remote(i, r, dest).wait_send()
+
+    for i in range(local_blocks):
+        for h in range(heads_here):
+            cols = slice(h * HD, (h + 1) * HD)
+            q = q_ref[i, :, cols]
+            j0 = idx_ref[i * RSEL]
+            j1 = idx_ref[i * RSEL + 1]
+            parts = [
+                slot_attention(q, k_ref[i, :, cols], v_ref[i, :, cols], scale),
+                slot_attention(q, fk_ref[j0, :, cols], fv_ref[j0, :, cols], scale),
+                slot_attention(q, fk_ref[j1, :, cols], fv_ref[j1, :, cols], scale),
+            ]
+            top = jnp.maximum(jnp.maximum(parts[0][0], parts[1][0]), parts[2][0])
+            numer = None
+            denom = None
+            for row_max, row_sum, partial in parts:
+                factor = jnp.exp(row_max - top)
+                numer = partial * factor if numer is None else numer + partial * factor
+                denom = row_sum * factor if denom is None else denom + row_sum * factor
+            stage[i, :, cols] = (numer / denom).astype(stage.dtype)
+        if i >= 1:
+            send(i - 1)
+    for i in range(local_blocks - 1):
+        finish(i)
+    send(local_blocks - 1)
+    finish(local_blocks - 1)
+    for sender in range(n):
+
+        @pl.when(sender != me)
+        def _():
+            pltpu.make_async_remote_copy(
+                src_ref=piece(0, 0), dst_ref=mine,
+                send_sem=send_sems.at[0], recv_sem=recv_sems.at[sender],
+                device_id=device(sender), device_id_type=MESH,
+            ).wait_recv()
+
+
+def attend(far_index, q_blocks, k_blocks, v_blocks, far_k, far_v, scale, axes, tok_rows):
     local_blocks, _, width = q_blocks.shape
     heads_here = width // HD
-    kernel = functools.partial(attend_kernel, heads_here=heads_here, scale=scale)
-    grid_spec = pltpu.PrefetchScalarGridSpec(
-        num_scalar_prefetch=1,
-        grid=(local_blocks,),
-        in_specs=[
-            pl.BlockSpec((1, BLOCK, width), lambda i, idx: (i, 0, 0)),
-            pl.BlockSpec((1, BLOCK, width), lambda i, idx: (i, 0, 0)),
-            pl.BlockSpec((1, BLOCK, width), lambda i, idx: (i, 0, 0)),
-            pl.BlockSpec((1, BLOCK, width), lambda i, idx: (idx[i * RSEL], 0, 0)),
-            pl.BlockSpec((1, BLOCK, width), lambda i, idx: (idx[i * RSEL], 0, 0)),
-            pl.BlockSpec((1, BLOCK, width), lambda i, idx: (idx[i * RSEL + 1], 0, 0)),
-            pl.BlockSpec((1, BLOCK, width), lambda i, idx: (idx[i * RSEL + 1], 0, 0)),
-        ],
-        out_specs=pl.BlockSpec((1, BLOCK, width), lambda i, idx: (i, 0, 0)),
-    )
+    n = HEADS // heads_here
+    kernel = functools.partial(attend_kernel, axes=axes, heads_here=heads_here, scale=scale)
+    vmem = pl.BlockSpec(memory_space=pltpu.VMEM)
     flops = local_blocks * heads_here * 3 * 4 * BLOCK * BLOCK * HD
     return pl.pallas_call(
         kernel,
-        out_shape=jax.ShapeDtypeStruct((local_blocks, BLOCK, width), jnp.bfloat16),
-        grid_spec=grid_spec,
+        out_shape=jax.ShapeDtypeStruct((tok_rows, n * width), jnp.bfloat16),
+        in_specs=[pl.BlockSpec(memory_space=pltpu.SMEM)] + [vmem] * 5,
+        out_specs=pl.BlockSpec(memory_space=pl.ANY),
+        scratch_shapes=[
+            pltpu.VMEM((local_blocks, BLOCK, width), jnp.bfloat16),
+            pltpu.SemaphoreType.DMA((local_blocks * (BLOCK // tok_rows),)),
+            pltpu.SemaphoreType.DMA((n,)),
+        ],
+        compiler_params=pltpu.CompilerParams(
+            collective_id=2, has_side_effects=True, vmem_limit_bytes=48 * 1024 * 1024
+        ),
         cost_estimate=pl.CostEstimate(
             flops=flops,
             transcendentals=local_blocks * heads_here * 3 * BLOCK * BLOCK,
             bytes_accessed=local_blocks * BLOCK * width * 2 * 8,
         ),
-    )(far_index, q_blocks, k_blocks, v_blocks, far_k, far_v, far_k, far_v)
+    )(far_index, q_blocks, k_blocks, v_blocks, far_k, far_v)
 
 
 def local(queries, keys, values, picks, axes):
@@ -198,10 +268,9 @@
     )
     q_blocks = q_heads.reshape(local_blocks, BLOCK, width)
 
-    result = attend(far_index, q_blocks, k_blocks, v_blocks, far_k, far_v, score_scale)
-    result = result.reshape(local_blocks * BLOCK, width)
-    (restored,) = exchange((result,), (("head", 0, 1),), axes, collective_id=2)
-    return restored
+    return attend(
+        far_index, q_blocks, k_blocks, v_blocks, far_k, far_v, score_scale, axes, tok_rows
+    )
 
 
 def solution(mesh):

time: 287 us -> 292 us (1.017); the launches traced: 287 us -> 288 us
  Pallas kernels: 274 us -> 277 us
    pallas_call x1, Pallas kernels: 15.4 us -> 37.6 us  [attend(): pl.pallas_call(kernel, out_shape=jax.ShapeDtypeStruct((tok_rows, n * widt...]
    pallas_call x3 -> x2, Pallas kernels: 259 us -> 239 us  [exchange(): pl.pallas_call(functools.partial(exchange_kernel, axes=axes, jobs=tuple(j...]
where the time goes in v4:
time: 292 us; the launch traced here: 288 us
  Pallas kernels  277 us (95%)
  local copies, waits for them, and re-layouts  10.3 us (4%)
    pallas_call x2, Pallas kernels, exchange(): pl.pallas_call(functools.partial(exchange_kernel, axes=axes, jobs=tuple(j...  239 us
    pallas_call x1, Pallas kernels, attend(): pl.pallas_call(kernel, out_shape=jax.ShapeDtypeStruct((tok_rows, n * widt...  37.6 us

profile of v4, /device:TPU:1, one launch (start us, length us, event | category | flops | bytes accessed | tf_op | source)
XLA Modules:
  0.0 288.3 jit_solution(6215536140044966615)
XLA Ops:
  0.0 0.7 and_select_fusion
  0.7 0.1 copy.23
  0.8 0.1 mul.19
  0.9 0.1 copy.19
  1.0 0.1 reshape.57
  1.1 0.1 copy.20
  1.2 0.5 fusion.4
  1.6 0.2 add_reduce_fusion.idx_ref
  1.8 0.1 copy.22
  1.9 0.1 select_reduce_fusion
  2.0 0.1 copy.24
  2.1 0.1 reshape.59
  2.2 31.1 %shard_map.46 = (bf16[4096,128]{1,0:T(8,128)(2,1)}, bf16[4096,128]{1,0:T(8,128)(2,1)}) custom-call(bf16[256,2048]{1,0:T(8,128)(2,1)} %refs_0_.2, bf16[256,2048]{1,0:T(8,128)(2,1)} %refs_1_.1), custom_call_target="tpu_custom_call" | custom-call | tf_op jit(solution)/shard_map/pallas_call | solution.py:81
  33.3 0.0 copy-start
  33.4 4.3 %gather_fusion.1 = bf16[32,512,128]{2,1,0:T(8,128)(2,1)} fusion(bf16[8,512,128]{2,1,0:T(8,128)(2,1)} %bitcast.7, s32[1024]{0:T(1024)S(1)} %pad_clamp_fusion), kind=kCustom, calls=%fused_computation.1 | custom fusion | bytes 8388736 | tf_op jit(solution)/shard_map/gather | solution.py:264
  37.7 0.0 copy-done
  37.7 3.0 %gather_fusion = bf16[32,512,128]{2,1,0:T(8,128)(2,1)} fusion(bf16[8,512,128]{2,1,0:T(8,128)(2,1)S(1)} %bitcast.5, s32[1024]{0:T(1024)S(1)} %pad_clamp_fusion), kind=kCustom, calls=%fused_computation | custom fusion | bytes 8388736 | tf_op jit(solution)/shard_map/gather | solution.py:263
  40.7 0.0 copy-start.1
  40.7 207.8 %shard_map.47 = (bf16[4096,128]{1,0:T(8,128)(2,1)}, bf16[32,512,128]{2,1,0:T(8,128)(2,1)}, bf16[32,512,128]{2,1,0:T(8,128)(2,1)}) custom-call(bf16[256,2048]{1,0:T(8,128)(2,1)} %refs_0_.3, bf16[32,512,128]{2,1,0:T(8,128)(2,1)} %gather_fusion, bf16[32,512,128]{2,1,0:T(8,128)(2,1)} %gather_fusion.1), custom_call_target="tpu_custom_call" | custom-call | tf_op jit(solution)/shard_map/pallas_call | solution.py:81
  248.5 0.0 copy-done.1
  248.5 0.0 copy-start.2
  248.6 1.2 copy-done.2
  249.8 37.6 %shard_map.48 = bf16[256,2048]{1,0:T(8,128)(2,1)S(1)} custom-call(s32[16]{0:T(128)S(1)} %add_reduce_fusion.idx_ref, bf16[8,512,128]{2,1,0:T(8,128)(2,1)S(1)} %bitcast.9, bf16[8,512,128]{2,1,0:T(8,128)(2,1)S(1)} %bitcast.6, bf16[8,512,128]{2,1,0:T(8,128)(2,1)S(1)} %bitcast.8, bf16[32,512,128]{2,1,0:T(8,128)(2,1)} %get-tuple-element.13.fk_ref, ...), custom_call_target="tpu_custom_call" | custom-call | flops 3221225472 | bytes 8388608 | tf_op jit(solution)/shard_map/pallas_call | solution.py:219
  287.4 1.0 copy.26
  (4 shorter events, 0.0 us)
Async XLA Ops:
  33.3 4.3 %copy-start = (bf16[4096,128]{1,0:T(8,128)(2,1)S(1)}, bf16[4096,128]{1,0:T(8,128)(2,1)}, u32[]{:S(2)}) copy-start(bf16[4096,128]{1,0:T(8,128)(2,1)} %get-tuple-element.10) | copy-start | bytes 3145732
  40.7 207.8 %copy-start.1 = (bf16[4096,128]{1,0:T(8,128)(2,1)S(1)}, bf16[4096,128]{1,0:T(8,128)(2,1)}, u32[]{:S(2)}) copy-start(bf16[4096,128]{1,0:T(8,128)(2,1)} %get-tuple-element.11) | copy-start | bytes 3145732
  248.5 1.2 copy-start.2

commit v5 on v3

--- a/solution.py
+++ b/solution.py
@@ -116,15 +116,75 @@
 
 
 def attend_kernel(
-    idx_ref, q_ref, k_ref, v_ref, fk0_ref, fv0_ref, fk1_ref, fv1_ref, o_ref, *, heads_here, scale
+    q_ref, k_ref, v_ref, fk_ref, fv_ref, y_ref, stage, send_sems, recv_sems,
+    *, axes, heads_here, scale,
 ):
+    n = lax.axis_size("head")
+    me = lax.axis_index("head")
+    i = pl.program_id(0)
+    local_blocks = pl.num_programs(0)
+    rows = y_ref.shape[0]
+    width = heads_here * HD
+    per_block = BLOCK // rows
+
+    def device(peer):
+        return tuple(peer if name == "head" else lax.axis_index(name) for name in axes)
+
+    @pl.when(i == 0)
+    def _():
+        barrier = pltpu.get_barrier_semaphore()
+        for k in range(1, n):
+            pl.semaphore_signal(
+                barrier, inc=1, device_id=device((me + k) % n), device_id_type=MESH
+            )
+        pl.semaphore_wait(barrier, n - 1)
+
+    mine = y_ref.at[:, pl.ds(me * width, width)]
+
+    def piece(b, r):
+        return stage.at[b, pl.ds(r * rows, rows), :]
+
+    def remote(b, r, dest):
+        return pltpu.make_async_remote_copy(
+            src_ref=piece(b, r), dst_ref=mine,
+            send_sem=send_sems.at[b * per_block + r], recv_sem=recv_sems.at[me],
+            device_id=device(dest), device_id_type=MESH,
+        )
+
+    def own(b, r):
+        return pltpu.make_async_copy(piece(b, r), mine, send_sems.at[b * per_block + r])
+
+    def send(b):
+        for r in range(per_block):
+            dest = b * per_block + r
+
+            @pl.when(dest == me)
+            def _():
+                own(b, r).start()
+
+            @pl.when(dest != me)
+            def _():
+                remote(b, r, dest).start()
+
+    def finish(b):
+        for r in range(per_block):
+            dest = b * per_block + r
+
+            @pl.when(dest == me)
+            def _():
+                own(b, r).wait()
+
+            @pl.when(dest != me)
+            def _():
+                remote(b, r, dest).wait_send()
+
     for h in range(heads_here):
         cols = slice(h * HD, (h + 1) * HD)
         q = q_ref[0, :, cols]
         parts = [
             slot_attention(q, k_ref[0, :, cols], v_ref[0, :, cols], scale),
-            slot_attention(q, fk0_ref[0, :, cols], fv0_ref[0, :, cols], scale),
-            slot_attention(q, fk1_ref[0, :, cols], fv1_ref[0, :, cols], scale),
+            slot_attention(q, fk_ref[0, :, cols], fv_ref[0, :, cols], scale),
+            slot_attention(q, fk_ref[1, :, cols], fv_ref[1, :, cols], scale),
         ]
         top = jnp.maximum(jnp.maximum(parts[0][0], parts[1][0]), parts[2][0])
         numer = None
@@ -133,38 +193,58 @@
             factor = jnp.exp(row_max - top)
             numer = partial * factor if numer is None else numer + partial * factor
             denom = row_sum * factor if denom is None else denom + row_sum * factor
-        o_ref[0, :, cols] = (numer / denom).astype(o_ref.dtype)
-
-
-def attend(far_index, q_blocks, k_blocks, v_blocks, far_k, far_v, scale):
+        stage[i, :, cols] = (numer / denom).astype(stage.dtype)
+
+    @pl.when(i >= 1)
+    def _():
+        send(i - 1)
+
+    @pl.when(i == local_blocks - 1)
+    def _():
+        def settle(b, carry):
+            finish(b)
+            return carry
+
+        lax.fori_loop(0, local_blocks - 1, settle, 0)
+        send(local_blocks - 1)
+        finish(local_blocks - 1)
+        for sender in range(n):
+
+            @pl.when(sender != me)
+            def _():
+                pltpu.make_async_remote_copy(
+                    src_ref=piece(0, 0), dst_ref=mine,
+                    send_sem=send_sems.at[0], recv_sem=recv_sems.at[sender],
+                    device_id=device(sender), device_id_type=MESH,
+                ).wait_recv()
+
+
+def attend(q_blocks, k_blocks, v_blocks, near_k, near_v, scale, axes, tok_rows):
     local_blocks, _, width = q_blocks.shape
     heads_here = width // HD
-    kernel = functools.partial(attend_kernel, heads_here=heads_here, scale=scale)
-    grid_spec = pltpu.PrefetchScalarGridSpec(
-        num_scalar_prefetch=1,
-        grid=(local_blocks,),
-        in_specs=[
-            pl.BlockSpec((1, BLOCK, width), lambda i, idx: (i, 0, 0)),
-            pl.BlockSpec((1, BLOCK, width), lambda i, idx: (i, 0, 0)),
-            pl.BlockSpec((1, BLOCK, width), lambda i, idx: (i, 0, 0)),
-            pl.BlockSpec((1, BLOCK, width), lambda i, idx: (idx[i * RSEL], 0, 0)),
-            pl.BlockSpec((1, BLOCK, width), lambda i, idx: (idx[i * RSEL], 0, 0)),
-            pl.BlockSpec((1, BLOCK, width), lambda i, idx: (idx[i * RSEL + 1], 0, 0)),
-            pl.BlockSpec((1, BLOCK, width), lambda i, idx: (idx[i * RSEL + 1], 0, 0)),
-        ],
-        out_specs=pl.BlockSpec((1, BLOCK, width), lambda i, idx: (i, 0, 0)),
-    )
+    n = HEADS // heads_here
+    kernel = functools.partial(attend_kernel, axes=axes, heads_here=heads_here, scale=scale)
+    one = pl.BlockSpec((1, BLOCK, width), lambda i: (i, 0, 0))
+    pair = pl.BlockSpec((RSEL, BLOCK, width), lambda i: (i, 0, 0))
     flops = local_blocks * heads_here * 3 * 4 * BLOCK * BLOCK * HD
     return pl.pallas_call(
         kernel,
-        out_shape=jax.ShapeDtypeStruct((local_blocks, BLOCK, width), jnp.bfloat16),
-        grid_spec=grid_spec,
+        out_shape=jax.ShapeDtypeStruct((tok_rows, n * width), jnp.bfloat16),
+        grid=(local_blocks,),
+        in_specs=[one, one, one, pair, pair],
+        out_specs=pl.BlockSpec(memory_space=pl.ANY),
+        scratch_shapes=[
+            pltpu.VMEM((local_blocks, BLOCK, width), jnp.bfloat16),
+            pltpu.SemaphoreType.DMA((local_blocks * (BLOCK // tok_rows),)),
+            pltpu.SemaphoreType.DMA((n,)),
+        ],
+        compiler_params=pltpu.CompilerParams(collective_id=2, has_side_effects=True),
         cost_estimate=pl.CostEstimate(
             flops=flops,
             transcendentals=local_blocks * heads_here * 3 * BLOCK * BLOCK,
             bytes_accessed=local_blocks * BLOCK * width * 2 * 8,
         ),
-    )(far_index, q_blocks, k_blocks, v_blocks, far_k, far_v, far_k, far_v)
+    )(q_blocks, k_blocks, v_blocks, near_k, near_v)
 
 
 def local(queries, keys, values, picks, axes):
@@ -198,10 +278,9 @@
     )
     q_blocks = q_heads.reshape(local_blocks, BLOCK, width)
 
-    result = attend(far_index, q_blocks, k_blocks, v_blocks, far_k, far_v, score_scale)
-    result = result.reshape(local_blocks * BLOCK, width)
-    (restored,) = exchange((result,), (("head", 0, 1),), axes, collective_id=2)
-    return restored
+    near_k = far_k[far_index]
+    near_v = far_v[far_index]
+    return attend(q_blocks, k_blocks, v_blocks, near_k, near_v, score_scale, axes, tok_rows)
 
 
 def solution(mesh):

time: 287 us -> 298 us (1.038); the launches traced: 287 us -> 294 us
  local copies, waits for them, and re-layouts: 10.4 us -> 19.2 us
    pallas_call x3 -> x2, Pallas kernels: 259 us -> 239 us  [exchange(): pl.pallas_call(functools.partial(exchange_kernel, axes=axes, jobs=tuple(j...]
    pallas_call x1, Pallas kernels: 15.4 us -> 34.9 us  [attend(): pl.pallas_call(kernel, out_shape=jax.ShapeDtypeStruct((tok_rows, n * widt...]
    gather x0 -> x2, local copies, waits for them, and re-layouts: none -> 8.73 us  [the longest x1 4.4 us: local(): near_k = far_k[far_index]]
where the time goes in v5:
time: 298 us; the launch traced here: 294 us
  Pallas kernels  274 us (92%)
  local copies, waits for them, and re-layouts  19.2 us (6%)
    pallas_call x2, Pallas kernels, exchange(): pl.pallas_call(functools.partial(exchange_kernel, axes=axes, jobs=tuple(j...  239 us
    pallas_call x1, Pallas kernels, attend(): pl.pallas_call(kernel, out_shape=jax.ShapeDtypeStruct((tok_rows, n * widt...  34.9 us

profile of v5, /device:TPU:1, one launch (start us, length us, event | category | flops | bytes accessed | tf_op | source)
XLA Modules:
  0.0 294.5 jit_solution(7860528754675770083)
XLA Ops:
  0.0 0.7 and_select_fusion.1
  0.7 0.1 copy.19
  0.8 0.1 reshape.87
  0.9 0.1 copy.20
  1.0 0.5 fusion.5
  1.4 0.2 add_reduce_fusion
  1.6 0.1 copy.21
  1.7 0.1 copy.22
  1.8 0.1 mul.25
  1.9 0.1 select_reduce_fusion
  2.0 0.1 copy.23
  2.1 0.1 reshape.88
  2.2 31.1 %shard_map.46 = (bf16[4096,128]{1,0:T(8,128)(2,1)}, bf16[4096,128]{1,0:T(8,128)(2,1)}) custom-call(bf16[256,2048]{1,0:T(8,128)(2,1)} %refs_0_.2, bf16[256,2048]{1,0:T(8,128)(2,1)} %refs_1_.1), custom_call_target="tpu_custom_call" | custom-call | tf_op jit(solution)/shard_map/pallas_call | solution.py:81
  33.4 0.0 copy-start
  33.4 4.4 %gather_fusion.1 = bf16[32,512,128]{2,1,0:T(8,128)(2,1)} fusion(bf16[8,512,128]{2,1,0:T(8,128)(2,1)} %bitcast.11, s32[1024]{0:T(1024)S(1)} %pad_clamp_fusion.1), kind=kCustom, calls=%fused_computation.1 | custom fusion | bytes 8388736 | tf_op jit(solution)/shard_map/gather | solution.py:274
  37.7 0.0 copy-done
  37.7 3.1 %gather_fusion = bf16[32,512,128]{2,1,0:T(8,128)(2,1)} fusion(bf16[8,512,128]{2,1,0:T(8,128)(2,1)S(1)} %bitcast.10, s32[1024]{0:T(1024)S(1)} %pad_clamp_fusion.1), kind=kCustom, calls=%fused_computation | custom fusion | bytes 8388736 | tf_op jit(solution)/shard_map/gather | solution.py:273
  40.8 207.8 %shard_map.47 = (bf16[4096,128]{1,0:T(8,128)(2,1)}, bf16[32,512,128]{2,1,0:T(8,128)(2,1)}, bf16[32,512,128]{2,1,0:T(8,128)(2,1)}) custom-call(bf16[256,2048]{1,0:T(8,128)(2,1)} %refs_0_.3, bf16[32,512,128]{2,1,0:T(8,128)(2,1)} %gather_fusion, bf16[32,512,128]{2,1,0:T(8,128)(2,1)} %gather_fusion.1), custom_call_target="tpu_custom_call" | custom-call | tf_op jit(solution)/shard_map/pallas_call | solution.py:81
  248.6 4.4 %gather_fusion.2 = bf16[16,512,128]{2,1,0:T(8,128)(2,1)} fusion(bf16[32,512,128]{2,1,0:T(8,128)(2,1)} %get-tuple-element.13, s32[1024]{0:T(1024)S(1)} %pad_clamp_fusion), kind=kCustom, calls=%fused_computation.2 | custom fusion | bytes 4194368 | tf_op jit(solution)/shard_map/gather | solution.py:281
  253.0 4.3 %gather_fusion.3 = bf16[16,512,128]{2,1,0:T(8,128)(2,1)} fusion(bf16[32,512,128]{2,1,0:T(8,128)(2,1)} %get-tuple-element.14, s32[1024]{0:T(1024)S(1)} %pad_clamp_fusion), kind=kCustom, calls=%fused_computation.3 | custom fusion | bytes 4194368 | tf_op jit(solution)/shard_map/gather | solution.py:282
  257.3 34.9 %shard_map.48 = bf16[256,2048]{1,0:T(8,128)(2,1)} custom-call(bf16[8,512,128]{2,1,0:T(8,128)(2,1)} %bitcast.13, bf16[8,512,128]{2,1,0:T(8,128)(2,1)} %bitcast.9, bf16[8,512,128]{2,1,0:T(8,128)(2,1)} %bitcast.12, bf16[16,512,128]{2,1,0:T(8,128)(2,1)} %gather_fusion.2, bf16[16,512,128]{2,1,0:T(8,128)(2,1)} %gather_fusion.3), custom_call_target="tpu_custom_call" | custom-call | flops 3221225472 | bytes 8388608 | tf_op jit(solution)/shard_map/pallas_call | solution.py:230
  292.2 2.3 copy.26
  (6 shorter events, 0.0 us)
Async XLA Ops:
  33.4 4.4 %copy-start = (bf16[4096,128]{1,0:T(8,128)(2,1)S(1)}, bf16[4096,128]{1,0:T(8,128)(2,1)}, u32[]{:S(2)}) copy-start(bf16[4096,128]{1,0:T(8,128)(2,1)} %get-tuple-element.10) | copy-start | bytes 3145732

commit v6 on v5

--- a/solution.py
+++ b/solution.py
@@ -116,21 +116,23 @@
 
 
 def attend_kernel(
-    q_ref, k_ref, v_ref, fk_ref, fv_ref, y_ref, stage, send_sems, recv_sems,
+    idx_ref, q_ref, k_ref, v_ref, fk_ref, fv_ref, y_ref, stage, send_sems, recv_sems,
     *, axes, heads_here, scale,
 ):
     n = lax.axis_size("head")
     me = lax.axis_index("head")
-    i = pl.program_id(0)
+    step = pl.program_id(0)
     local_blocks = pl.num_programs(0)
     rows = y_ref.shape[0]
     width = heads_here * HD
     per_block = BLOCK // rows
+    turn = me // per_block
+    i = (step + turn) % local_blocks
 
     def device(peer):
         return tuple(peer if name == "head" else lax.axis_index(name) for name in axes)
 
-    @pl.when(i == 0)
+    @pl.when(step == 0)
     def _():
         barrier = pltpu.get_barrier_semaphore()
         for k in range(1, n):
@@ -178,13 +180,15 @@
             def _():
                 remote(b, r, dest).wait_send()
 
+    j0 = idx_ref[i * RSEL]
+    j1 = idx_ref[i * RSEL + 1]
     for h in range(heads_here):
         cols = slice(h * HD, (h + 1) * HD)
         q = q_ref[0, :, cols]
         parts = [
             slot_attention(q, k_ref[0, :, cols], v_ref[0, :, cols], scale),
-            slot_attention(q, fk_ref[0, :, cols], fv_ref[0, :, cols], scale),
-            slot_attention(q, fk_ref[1, :, cols], fv_ref[1, :, cols], scale),
+            slot_attention(q, fk_ref[j0, :, cols], fv_ref[j0, :, cols], scale),
+            slot_attention(q, fk_ref[j1, :, cols], fv_ref[j1, :, cols], scale),
         ]
         top = jnp.maximum(jnp.maximum(parts[0][0], parts[1][0]), parts[2][0])
         numer = None
@@ -195,19 +199,19 @@
             denom = row_sum * factor if denom is None else denom + row_sum * factor
         stage[i, :, cols] = (numer / denom).astype(stage.dtype)
 
-    @pl.when(i >= 1)
+    @pl.when(step >= 1)
     def _():
-        send(i - 1)
-
-    @pl.when(i == local_blocks - 1)
+        send((step - 1 + turn) % local_blocks)
+
+    @pl.when(step == local_blocks - 1)
     def _():
-        def settle(b, carry):
-            finish(b)
+        def settle(t, carry):
+            finish((t + turn) % local_blocks)
             return carry
 
         lax.fori_loop(0, local_blocks - 1, settle, 0)
-        send(local_blocks - 1)
-        finish(local_blocks - 1)
+        send(i)
+        finish(i)
         for sender in range(n):
 
             @pl.when(sender != me)
@@ -219,19 +223,25 @@
                 ).wait_recv()
 
 
-def attend(q_blocks, k_blocks, v_blocks, near_k, near_v, scale, axes, tok_rows):
+def attend(far_index, q_blocks, k_blocks, v_blocks, far_k, far_v, scale, axes, tok_rows):
     local_blocks, _, width = q_blocks.shape
     heads_here = width // HD
     n = HEADS // heads_here
     kernel = functools.partial(attend_kernel, axes=axes, heads_here=heads_here, scale=scale)
-    one = pl.BlockSpec((1, BLOCK, width), lambda i: (i, 0, 0))
-    pair = pl.BlockSpec((RSEL, BLOCK, width), lambda i: (i, 0, 0))
+    per_block = BLOCK // tok_rows
+
+    def rotated(i):
+        return ((i + lax.axis_index("head") // per_block) % local_blocks, 0, 0)
+
+    one = pl.BlockSpec((1, BLOCK, width), rotated)
+    whole = pl.BlockSpec(far_k.shape, lambda i: (0, 0, 0), pipeline_mode=pl.Buffered(1))
+    smem = pl.BlockSpec(memory_space=pltpu.SMEM)
     flops = local_blocks * heads_here * 3 * 4 * BLOCK * BLOCK * HD
     return pl.pallas_call(
         kernel,
         out_shape=jax.ShapeDtypeStruct((tok_rows, n * width), jnp.bfloat16),
         grid=(local_blocks,),
-        in_specs=[one, one, one, pair, pair],
+        in_specs=[smem, one, one, one, whole, whole],
         out_specs=pl.BlockSpec(memory_space=pl.ANY),
         scratch_shapes=[
             pltpu.VMEM((local_blocks, BLOCK, width), jnp.bfloat16),
@@ -244,7 +254,7 @@
             transcendentals=local_blocks * heads_here * 3 * BLOCK * BLOCK,
             bytes_accessed=local_blocks * BLOCK * width * 2 * 8,
         ),
-    )(q_blocks, k_blocks, v_blocks, near_k, near_v)
+    )(far_index, q_blocks, k_blocks, v_blocks, far_k, far_v)
 
 
 def local(queries, keys, values, picks, axes):
@@ -278,9 +288,9 @@
     )
     q_blocks = q_heads.reshape(local_blocks, BLOCK, width)
 
-    near_k = far_k[far_index]
-    near_v = far_v[far_index]
-    return attend(q_blocks, k_blocks, v_blocks, near_k, near_v, score_scale, axes, tok_rows)
+    return attend(
+        far_index, q_blocks, k_blocks, v_blocks, far_k, far_v, score_scale, axes, tok_rows
+    )
 
 
 def solution(mesh):

time: 298 us -> 285 us (0.956); the launches traced: 294 us -> 285 us
  local copies, waits for them, and re-layouts: 19.2 us -> 10.4 us
    gather x2 -> x0, local copies, waits for them, and re-layouts: 8.73 us -> none  [the longest x1 4.4 us: local(): near_k = far_k[far_index]]
where the time goes in v6:
time: 285 us
  Pallas kernels  272 us (95%)
  local copies, waits for them, and re-layouts  10.4 us (4%)
    pallas_call x2, Pallas kernels, exchange(): pl.pallas_call(functools.partial(exchange_kernel, axes=axes, jobs=tuple(j...  239 us
    pallas_call x1, Pallas kernels, attend(): pl.pallas_call(kernel, out_shape=jax.ShapeDtypeStruct((tok_rows, n * widt...  33.4 us

profile of v6, /device:TPU:1, one launch (start us, length us, event | category | flops | bytes accessed | tf_op | source)
XLA Modules:
  0.0 284.8 jit_solution(12070029535516514197)
XLA Ops:
  0.0 0.7 and_select_fusion
  0.7 0.1 copy.23
  0.8 0.1 mul.19
  0.9 0.1 copy.19
  1.0 0.1 reshape.57
  1.1 0.1 copy.20
  1.2 0.5 fusion.4
  1.6 0.7 add_reduce_fusion.idx_ref
  2.3 0.1 copy.22
  2.4 0.1 select_reduce_fusion
  2.5 0.1 copy.24
  2.6 0.1 reshape.59
  2.7 31.1 %shard_map.46 = (bf16[4096,128]{1,0:T(8,128)(2,1)}, bf16[4096,128]{1,0:T(8,128)(2,1)}) custom-call(bf16[256,2048]{1,0:T(8,128)(2,1)} %refs_0_.2, bf16[256,2048]{1,0:T(8,128)(2,1)} %refs_1_.1), custom_call_target="tpu_custom_call" | custom-call | tf_op jit(solution)/shard_map/pallas_call | solution.py:81
  33.9 0.0 copy-start
  33.9 4.4 %gather_fusion.1 = bf16[32,512,128]{2,1,0:T(8,128)(2,1)} fusion(bf16[8,512,128]{2,1,0:T(8,128)(2,1)} %bitcast.7, s32[1024]{0:T(1024)S(1)} %pad_clamp_fusion), kind=kCustom, calls=%fused_computation.1 | custom fusion | bytes 8388736 | tf_op jit(solution)/shard_map/gather | solution.py:284
  38.2 0.0 copy-done
  38.2 3.1 %gather_fusion = bf16[32,512,128]{2,1,0:T(8,128)(2,1)} fusion(bf16[8,512,128]{2,1,0:T(8,128)(2,1)S(1)} %bitcast.6, s32[1024]{0:T(1024)S(1)} %pad_clamp_fusion), kind=kCustom, calls=%fused_computation | custom fusion | bytes 8388736 | tf_op jit(solution)/shard_map/gather | solution.py:283
  41.3 207.8 %shard_map.47 = (bf16[4096,128]{1,0:T(8,128)(2,1)}, bf16[32,512,128]{2,1,0:T(8,128)(2,1)}, bf16[32,512,128]{2,1,0:T(8,128)(2,1)}) custom-call(bf16[256,2048]{1,0:T(8,128)(2,1)} %refs_0_.3, bf16[32,512,128]{2,1,0:T(8,128)(2,1)} %gather_fusion, bf16[32,512,128]{2,1,0:T(8,128)(2,1)} %gather_fusion.1), custom_call_target="tpu_custom_call" | custom-call | tf_op jit(solution)/shard_map/pallas_call | solution.py:81
  249.1 33.4 %shard_map.48 = bf16[256,2048]{1,0:T(8,128)(2,1)} custom-call(s32[16]{0:T(128)} %add_reduce_fusion.idx_ref, bf16[8,512,128]{2,1,0:T(8,128)(2,1)} %bitcast.9, bf16[8,512,128]{2,1,0:T(8,128)(2,1)} %bitcast.5, bf16[8,512,128]{2,1,0:T(8,128)(2,1)} %bitcast.8, bf16[32,512,128]{2,1,0:T(8,128)(2,1)} %get-tuple-element.13.fk_ref, ...), custom_call_target="tpu_custom_call" | custom-call | flops 3221225472 | bytes 8388608 | tf_op jit(solution)/shard_map/pallas_call | solution.py:240
  282.5 2.3 copy.26
  (4 shorter events, 0.0 us)
Async XLA Ops:
  33.9 4.4 %copy-start = (bf16[4096,128]{1,0:T(8,128)(2,1)S(1)}, bf16[4096,128]{1,0:T(8,128)(2,1)}, u32[]{:S(2)}) copy-start(bf16[4096,128]{1,0:T(8,128)(2,1)} %get-tuple-element.10) | copy-start | bytes 3145732

commit v7 on v6

--- a/solution.py
+++ b/solution.py
@@ -266,10 +266,10 @@
     tok_rows = queries.shape[0]
     score_scale = 1.0 / math.sqrt(HD)
     head_in = ("head", 1, 0)
-    k_heads, v_heads = exchange((keys, values), (head_in, head_in), axes, collective_id=0)
+    ctx_move = ("ctx", 0, 0)
+    (k_heads,) = exchange((keys,), (head_in,), axes, collective_id=0)
     local_blocks = k_heads.shape[0] // BLOCK
     k_blocks = k_heads.reshape(local_blocks, BLOCK, width)
-    v_blocks = v_heads.reshape(local_blocks, BLOCK, width)
 
     capacity = (local_blocks * RSEL + ctx_count - 1) // ctx_count + 1
     owners, within, position = route_tables(picks, local_blocks, ctx_count)
@@ -281,13 +281,13 @@
     far_index = (mine_owner * capacity + mine_pos).astype(jnp.int32)
 
     send_k = k_blocks[wanted.reshape(-1)]
-    send_v = v_blocks[wanted.reshape(-1)]
-    ctx_move = ("ctx", 0, 0)
-    q_heads, far_k, far_v = exchange(
-        (queries, send_k, send_v), (head_in, ctx_move, ctx_move), axes, collective_id=1
+    far_k, v_heads, q_heads = exchange(
+        (send_k, values, queries), (ctx_move, head_in, head_in), axes, collective_id=1
     )
     q_blocks = q_heads.reshape(local_blocks, BLOCK, width)
-
+    v_blocks = v_heads.reshape(local_blocks, BLOCK, width)
+    send_v = v_blocks[wanted.reshape(-1)]
+    (far_v,) = exchange((send_v,), (ctx_move,), axes, collective_id=3)
     return attend(
         far_index, q_blocks, k_blocks, v_blocks, far_k, far_v, score_scale, axes, tok_rows
     )

time: 285 us -> 279 us (0.979)
  Pallas kernels: 272 us -> 264 us
    pallas_call x2 -> x3, Pallas kernels: 239 us -> 232 us  [exchange(): pl.pallas_call(functools.partial(exchange_kernel, axes=axes, jobs=tuple(j...]
where the time goes in v7:
time: 279 us; the launch traced here: 277 us
  Pallas kernels  264 us (95%)
  local copies, waits for them, and re-layouts  11.6 us (4%)
    pallas_call x3, Pallas kernels, exchange(): pl.pallas_call(functools.partial(exchange_kernel, axes=axes, jobs=tuple(j...  232 us
    pallas_call x1, Pallas kernels, attend(): pl.pallas_call(kernel, out_shape=jax.ShapeDtypeStruct((tok_rows, n * widt...  31.8 us

profile of v7, /device:TPU:1, one launch (start us, length us, event | category | flops | bytes accessed | tf_op | source)
XLA Modules:
  0.0 277.4 jit_solution(5258746252737024035)
XLA Ops:
  0.0 0.7 and_select_fusion
  0.7 0.1 copy.23
  0.8 0.1 mul.19
  0.9 0.1 copy.19
  1.0 0.1 reshape.57
  1.1 0.1 copy.20
  1.2 0.5 fusion.4
  1.6 0.7 add_reduce_fusion.idx_ref
  2.3 0.1 copy.22
  2.4 0.1 select_reduce_fusion
  2.5 0.1 copy.24
  2.6 0.1 reshape.59
  2.7 19.3 %shard_map.46 = bf16[4096,128]{1,0:T(8,128)(2,1)} custom-call(bf16[256,2048]{1,0:T(8,128)(2,1)} %refs_0_.1), custom_call_target="tpu_custom_call" | custom-call | tf_op jit(solution)/shard_map/pallas_call | solution.py:81
  22.1 4.3 %gather_fusion = bf16[32,512,128]{2,1,0:T(8,128)(2,1)} fusion(bf16[8,512,128]{2,1,0:T(8,128)(2,1)} %bitcast.5, s32[1024]{0:T(1024)S(1)} %pad_clamp_fusion), kind=kCustom, calls=%fused_computation | custom fusion | bytes 8388736 | tf_op jit(solution)/shard_map/gather | solution.py:283
  26.4 113.0 %shard_map.47 = (bf16[32,512,128]{2,1,0:T(8,128)(2,1)}, bf16[4096,128]{1,0:T(8,128)(2,1)}, bf16[4096,128]{1,0:T(8,128)(2,1)}) custom-call(bf16[32,512,128]{2,1,0:T(8,128)(2,1)} %gather_fusion, bf16[256,2048]{1,0:T(8,128)(2,1)} %refs_1_.1, bf16[256,2048]{1,0:T(8,128)(2,1)} %refs_2_.1), custom_call_target="tpu_custom_call" | custom-call | tf_op jit(solution)/shard_map/pallas_call | solution.py:81
  139.4 4.3 %gather_fusion.1 = bf16[32,512,128]{2,1,0:T(8,128)(2,1)} fusion(bf16[8,512,128]{2,1,0:T(8,128)(2,1)} %bitcast.7, s32[1024]{0:T(1024)S(1)} %pad_clamp_fusion), kind=kCustom, calls=%fused_computation.1 | custom fusion | bytes 8388736 | tf_op jit(solution)/shard_map/gather | solution.py:289
  143.7 99.7 %shard_map.48.fv_ref = bf16[32,512,128]{2,1,0:T(8,128)(2,1)} custom-call(bf16[32,512,128]{2,1,0:T(8,128)(2,1)} %gather_fusion.1), custom_call_target="tpu_custom_call" | custom-call | tf_op jit(solution)/shard_map/pallas_call | solution.py:81
  243.3 31.8 %shard_map.49 = bf16[256,2048]{1,0:T(8,128)(2,1)} custom-call(s32[16]{0:T(128)} %add_reduce_fusion.idx_ref, bf16[8,512,128]{2,1,0:T(8,128)(2,1)} %bitcast.9, bf16[8,512,128]{2,1,0:T(8,128)(2,1)} %bitcast.6, bf16[8,512,128]{2,1,0:T(8,128)(2,1)} %bitcast.8, bf16[32,512,128]{2,1,0:T(8,128)(2,1)} %get-tuple-element.10.fk_ref, bf16[32,512,128]{2,1,0:T(8,128)(2,1)} %shard_map.48.fv_ref), custom_call_target="tpu_custom_call" | custom-call | flops 3221225472 | bytes 8388608 | tf_op jit(solution)/shard_map/pallas_call | solution.py:240
  275.1 2.3 copy.26
  (4 shorter events, 0.0 us)

commit v8 on v7

--- a/solution.py
+++ b/solution.py
@@ -115,31 +115,90 @@
     return row_max, row_sum, partial
 
 
-def attend_kernel(
-    idx_ref, q_ref, k_ref, v_ref, fk_ref, fv_ref, y_ref, stage, send_sems, recv_sems,
-    *, axes, heads_here, scale,
+def finish_kernel(
+    idx_ref, q_hbm, k_hbm, v_hbm, fk_hbm, sv_hbm, y_ref,
+    qv, kv, vv, fkv, fvv, wts, base, fac, stage,
+    load_sems, ctx_send, ctx_recv, out_send, out_recv,
+    *, axes, heads_here, scale, capacity,
 ):
     n = lax.axis_size("head")
     me = lax.axis_index("head")
-    step = pl.program_id(0)
-    local_blocks = pl.num_programs(0)
+    m_ctx = lax.axis_size("ctx")
+    c_me = lax.axis_index("ctx")
+    local_blocks = qv.shape[0]
     rows = y_ref.shape[0]
     width = heads_here * HD
     per_block = BLOCK // rows
     turn = me // per_block
-    i = (step + turn) % local_blocks
-
-    def device(peer):
-        return tuple(peer if name == "head" else lax.axis_index(name) for name in axes)
-
-    @pl.when(step == 0)
-    def _():
-        barrier = pltpu.get_barrier_semaphore()
-        for k in range(1, n):
-            pl.semaphore_signal(
-                barrier, inc=1, device_id=device((me + k) % n), device_id_type=MESH
-            )
-        pl.semaphore_wait(barrier, n - 1)
+
+    def device(axis, peer):
+        return tuple(peer if name == axis else lax.axis_index(name) for name in axes)
+
+    barrier = pltpu.get_barrier_semaphore()
+    for k in range(1, m_ctx):
+        pl.semaphore_signal(
+            barrier, inc=1, device_id=device("ctx", (c_me + k) % m_ctx), device_id_type=MESH
+        )
+    for k in range(1, n):
+        pl.semaphore_signal(
+            barrier, inc=1, device_id=device("head", (me + k) % n), device_id_type=MESH
+        )
+    pl.semaphore_wait(barrier, m_ctx - 1 + n - 1)
+
+    def rows_of(ref, index):
+        return ref.at[pl.ds(index * capacity, capacity)]
+
+    v_copies = [pltpu.make_async_copy(rows_of(sv_hbm, c_me), rows_of(fvv, c_me), ctx_send.at[0])]
+    v_copies[0].start()
+    for k in range(1, m_ctx):
+        peer = (c_me + k) % m_ctx
+        copy = pltpu.make_async_remote_copy(
+            src_ref=rows_of(sv_hbm, peer), dst_ref=rows_of(fvv, c_me),
+            send_sem=ctx_send.at[k], recv_sem=ctx_recv.at[k],
+            device_id=device("ctx", peer), device_id_type=MESH,
+        )
+        copy.start()
+        v_copies.append(copy)
+
+    loads = [
+        pltpu.make_async_copy(src, dst, load_sems.at[a])
+        for a, (src, dst) in enumerate(((q_hbm, qv), (k_hbm, kv), (v_hbm, vv), (fk_hbm, fkv)))
+    ]
+    for load in loads:
+        load.start()
+    for load in loads:
+        load.wait()
+
+    def prepare(i, carry):
+        j0 = idx_ref[i * RSEL]
+        j1 = idx_ref[i * RSEL + 1]
+        for h in range(heads_here):
+            cols = pl.ds(h * HD, HD)
+            q = qv[i, :, cols]
+            m0, l0, acc0 = slot_attention(q, kv[i, :, cols], vv[i, :, cols], scale)
+            stats = []
+            for slot, j in enumerate((j0, j1)):
+                scores = lax.dot_general(
+                    q, fkv[j, :, cols], (((1,), (1,)), ((), ())),
+                    preferred_element_type=jnp.float32,
+                ) * scale
+                row_max = jnp.max(scores, axis=1, keepdims=True)
+                exponent = jnp.exp(scores - row_max)
+                stats.append((row_max, jnp.sum(exponent, axis=1, keepdims=True)))
+                wts[i, h * RSEL + slot] = exponent.astype(jnp.bfloat16)
+            top = jnp.maximum(jnp.maximum(m0, stats[0][0]), stats[1][0])
+            f0 = jnp.exp(m0 - top)
+            f1 = jnp.exp(stats[0][0] - top)
+            f2 = jnp.exp(stats[1][0] - top)
+            base[i, :, cols] = acc0 * f0
+            fac[i, h * 3] = f1
+            fac[i, h * 3 + 1] = f2
+            fac[i, h * 3 + 2] = l0 * f0 + stats[0][1] * f1 + stats[1][1] * f2
+        return carry
+
+    lax.fori_loop(0, local_blocks, prepare, 0)
+    for copy in v_copies:
+        copy.wait()
 
     mine = y_ref.at[:, pl.ds(me * width, width)]
 
@@ -149,12 +208,12 @@
     def remote(b, r, dest):
         return pltpu.make_async_remote_copy(
             src_ref=piece(b, r), dst_ref=mine,
-            send_sem=send_sems.at[b * per_block + r], recv_sem=recv_sems.at[me],
-            device_id=device(dest), device_id_type=MESH,
+            send_sem=out_send.at[b * per_block + r], recv_sem=out_recv.at[me],
+            device_id=device("head", dest), device_id_type=MESH,
         )
 
     def own(b, r):
-        return pltpu.make_async_copy(piece(b, r), mine, send_sems.at[b * per_block + r])
+        return pltpu.make_async_copy(piece(b, r), mine, out_send.at[b * per_block + r])
 
     def send(b):
         for r in range(per_block):
@@ -180,81 +239,88 @@
             def _():
                 remote(b, r, dest).wait_send()
 
-    j0 = idx_ref[i * RSEL]
-    j1 = idx_ref[i * RSEL + 1]
-    for h in range(heads_here):
-        cols = slice(h * HD, (h + 1) * HD)
-        q = q_ref[0, :, cols]
-        parts = [
-            slot_attention(q, k_ref[0, :, cols], v_ref[0, :, cols], scale),
-            slot_attention(q, fk_ref[j0, :, cols], fv_ref[j0, :, cols], scale),
-            slot_attention(q, fk_ref[j1, :, cols], fv_ref[j1, :, cols], scale),
-        ]
-        top = jnp.maximum(jnp.maximum(parts[0][0], parts[1][0]), parts[2][0])
-        numer = None
-        denom = None
-        for row_max, row_sum, partial in parts:
-            factor = jnp.exp(row_max - top)
-            numer = partial * factor if numer is None else numer + partial * factor
-            denom = row_sum * factor if denom is None else denom + row_sum * factor
-        stage[i, :, cols] = (numer / denom).astype(stage.dtype)
-
-    @pl.when(step >= 1)
-    def _():
-        send((step - 1 + turn) % local_blocks)
-
-    @pl.when(step == local_blocks - 1)
-    def _():
-        def settle(t, carry):
-            finish((t + turn) % local_blocks)
-            return carry
-
-        lax.fori_loop(0, local_blocks - 1, settle, 0)
-        send(i)
-        finish(i)
-        for sender in range(n):
-
-            @pl.when(sender != me)
-            def _():
-                pltpu.make_async_remote_copy(
-                    src_ref=piece(0, 0), dst_ref=mine,
-                    send_sem=send_sems.at[0], recv_sem=recv_sems.at[sender],
-                    device_id=device(sender), device_id_type=MESH,
-                ).wait_recv()
-
-
-def attend(far_index, q_blocks, k_blocks, v_blocks, far_k, far_v, scale, axes, tok_rows):
+    def complete(t, carry):
+        i = (t + turn) % local_blocks
+        j0 = idx_ref[i * RSEL]
+        j1 = idx_ref[i * RSEL + 1]
+        for h in range(heads_here):
+            cols = pl.ds(h * HD, HD)
+            p1 = jnp.dot(wts[i, h * RSEL], fvv[j0, :, cols], preferred_element_type=jnp.float32)
+            p2 = jnp.dot(
+                wts[i, h * RSEL + 1], fvv[j1, :, cols], preferred_element_type=jnp.float32
+            )
+            numer = base[i, :, cols] + p1 * fac[i, h * 3] + p2 * fac[i, h * 3 + 1]
+            stage[i, :, cols] = (numer / fac[i, h * 3 + 2]).astype(stage.dtype)
+
+        @pl.when(t >= 1)
+        def _():
+            send((t - 1 + turn) % local_blocks)
+
+        return carry
+
+    lax.fori_loop(0, local_blocks, complete, 0)
+
+    def settle(t, carry):
+        finish((t + turn) % local_blocks)
+        return carry
+
+    lax.fori_loop(0, local_blocks - 1, settle, 0)
+    last = (local_blocks - 1 + turn) % local_blocks
+    send(last)
+    finish(last)
+    for sender in range(n):
+
+        @pl.when(sender != me)
+        def _():
+            pltpu.make_async_remote_copy(
+                src_ref=piece(0, 0), dst_ref=mine,
+                send_sem=out_send.at[0], recv_sem=out_recv.at[sender],
+                device_id=device("head", sender), device_id_type=MESH,
+            ).wait_recv()
+
+
+def finish_attention(
+    far_index, q_blocks, k_blocks, v_blocks, far_k, send_v, scale, axes, tok_rows, capacity
+):
     local_blocks, _, width = q_blocks.shape
     heads_here = width // HD
     n = HEADS // heads_here
-    kernel = functools.partial(attend_kernel, axes=axes, heads_here=heads_here, scale=scale)
-    per_block = BLOCK // tok_rows
-
-    def rotated(i):
-        return ((i + lax.axis_index("head") // per_block) % local_blocks, 0, 0)
-
-    one = pl.BlockSpec((1, BLOCK, width), rotated)
-    whole = pl.BlockSpec(far_k.shape, lambda i: (0, 0, 0), pipeline_mode=pl.Buffered(1))
-    smem = pl.BlockSpec(memory_space=pltpu.SMEM)
+    m_ctx = send_v.shape[0] // capacity
+    kernel = functools.partial(
+        finish_kernel, axes=axes, heads_here=heads_here, scale=scale, capacity=capacity
+    )
+    anywhere = pl.BlockSpec(memory_space=pl.ANY)
     flops = local_blocks * heads_here * 3 * 4 * BLOCK * BLOCK * HD
     return pl.pallas_call(
         kernel,
         out_shape=jax.ShapeDtypeStruct((tok_rows, n * width), jnp.bfloat16),
-        grid=(local_blocks,),
-        in_specs=[smem, one, one, one, whole, whole],
-        out_specs=pl.BlockSpec(memory_space=pl.ANY),
+        in_specs=[pl.BlockSpec(memory_space=pltpu.SMEM)] + [anywhere] * 5,
+        out_specs=anywhere,
         scratch_shapes=[
+            pltpu.VMEM(q_blocks.shape, jnp.bfloat16),
+            pltpu.VMEM(k_blocks.shape, jnp.bfloat16),
+            pltpu.VMEM(v_blocks.shape, jnp.bfloat16),
+            pltpu.VMEM(far_k.shape, jnp.bfloat16),
+            pltpu.VMEM(send_v.shape, jnp.bfloat16),
+            pltpu.VMEM((local_blocks, heads_here * RSEL, BLOCK, BLOCK), jnp.bfloat16),
+            pltpu.VMEM((local_blocks, BLOCK, width), jnp.float32),
+            pltpu.VMEM((local_blocks, heads_here * 3, BLOCK, 1), jnp.float32),
             pltpu.VMEM((local_blocks, BLOCK, width), jnp.bfloat16),
+            pltpu.SemaphoreType.DMA((4,)),
+            pltpu.SemaphoreType.DMA((m_ctx,)),
+            pltpu.SemaphoreType.DMA((m_ctx,)),
             pltpu.SemaphoreType.DMA((local_blocks * (BLOCK // tok_rows),)),
             pltpu.SemaphoreType.DMA((n,)),
         ],
-        compiler_params=pltpu.CompilerParams(collective_id=2, has_side_effects=True),
+        compiler_params=pltpu.CompilerParams(
+            collective_id=2, has_side_effects=True, vmem_limit_bytes=60 * 1024 * 1024
+        ),
         cost_estimate=pl.CostEstimate(
             flops=flops,
             transcendentals=local_blocks * heads_here * 3 * BLOCK * BLOCK,
             bytes_accessed=local_blocks * BLOCK * width * 2 * 8,
         ),
-    )(far_index, q_blocks, k_blocks, v_blocks, far_k, far_v)
+    )(far_index, q_blocks, k_blocks, v_blocks, far_k, send_v)
 
 
 def local(queries, keys, values, picks, axes):
@@ -287,9 +353,9 @@
     q_blocks = q_heads.reshape(local_blocks, BLOCK, width)
     v_blocks = v_heads.reshape(local_blocks, BLOCK, width)
     send_v = v_blocks[wanted.reshape(-1)]
-    (far_v,) = exchange((send_v,), (ctx_move,), axes, collective_id=3)
-    return attend(
-        far_index, q_blocks, k_blocks, v_blocks, far_k, far_v, score_scale, axes, tok_rows
+    return finish_attention(
+        far_index, q_blocks, k_blocks, v_blocks, far_k, send_v, score_scale, axes, tok_rows,
+        capacity,
     )
 
 

time: 279 us -> 265 us (0.950)
  Pallas kernels: 264 us -> 249 us
    pallas_call x3 -> x2, Pallas kernels: 232 us -> 132 us  [exchange(): pl.pallas_call(functools.partial(exchange_kernel, axes=axes, jobs=tuple(j...]
    pallas_call x1, Pallas kernels: 31.8 us -> 117 us  [finish_attention(): pl.pallas_call(kernel, out_shape=jax.ShapeDtypeStruct((tok_rows, n * widt...]
where the time goes in v8:
time: 265 us; the launch traced here: 263 us
  Pallas kernels  249 us (94%)
  local copies, waits for them, and re-layouts  11.6 us (4%)
    pallas_call x2, Pallas kernels, exchange(): pl.pallas_call(functools.partial(exchange_kernel, axes=axes, jobs=tuple(j...  132 us
    pallas_call x1, Pallas kernels, finish_attention(): pl.pallas_call(kernel, out_shape=jax.ShapeDtypeStruct((tok_rows, n * widt...  117 us

profile of v8, /device:TPU:1, one launch (start us, length us, event | category | flops | bytes accessed | tf_op | source)
XLA Modules:
  0.0 262.7 jit_solution(1632451101001068066)
XLA Ops:
  0.0 0.7 and_select_fusion
  0.7 0.1 copy.23
  0.8 0.1 mul.19
  0.9 0.1 copy.19
  1.0 0.1 reshape.57
  1.1 0.1 copy.20
  1.2 0.5 fusion.4
  1.6 0.7 add_reduce_fusion.idx_ref
  2.3 0.1 copy.22
  2.4 0.1 select_reduce_fusion
  2.5 0.1 copy.24
  2.6 0.1 reshape.59
  2.7 19.3 %shard_map.46 = bf16[4096,128]{1,0:T(8,128)(2,1)} custom-call(bf16[256,2048]{1,0:T(8,128)(2,1)} %refs_0_.1), custom_call_target="tpu_custom_call" | custom-call | tf_op jit(solution)/shard_map/pallas_call | solution.py:81
  22.1 4.3 %gather_fusion = bf16[32,512,128]{2,1,0:T(8,128)(2,1)} fusion(bf16[8,512,128]{2,1,0:T(8,128)(2,1)} %bitcast.5, s32[1024]{0:T(1024)S(1)} %pad_clamp_fusion), kind=kCustom, calls=%fused_computation | custom fusion | bytes 8388736 | tf_op jit(solution)/shard_map/gather | solution.py:349
  26.4 113.0 %shard_map.47 = (bf16[32,512,128]{2,1,0:T(8,128)(2,1)}, bf16[4096,128]{1,0:T(8,128)(2,1)}, bf16[4096,128]{1,0:T(8,128)(2,1)}) custom-call(bf16[32,512,128]{2,1,0:T(8,128)(2,1)} %gather_fusion, bf16[256,2048]{1,0:T(8,128)(2,1)} %refs_1_.1, bf16[256,2048]{1,0:T(8,128)(2,1)} %refs_2_.1), custom_call_target="tpu_custom_call" | custom-call | tf_op jit(solution)/shard_map/pallas_call | solution.py:81
  139.4 4.3 %gather_fusion.1 = bf16[32,512,128]{2,1,0:T(8,128)(2,1)} fusion(bf16[8,512,128]{2,1,0:T(8,128)(2,1)} %bitcast.7, s32[1024]{0:T(1024)S(1)} %pad_clamp_fusion), kind=kCustom, calls=%fused_computation.1 | custom fusion | bytes 8388736 | tf_op jit(solution)/shard_map/gather | solution.py:355
  143.7 116.7 %shard_map.48 = bf16[256,2048]{1,0:T(8,128)(2,1)} custom-call(s32[16]{0:T(128)} %add_reduce_fusion.idx_ref, bf16[8,512,128]{2,1,0:T(8,128)(2,1)} %bitcast.9, bf16[8,512,128]{2,1,0:T(8,128)(2,1)} %bitcast.6, bf16[8,512,128]{2,1,0:T(8,128)(2,1)} %bitcast.8, bf16[32,512,128]{2,1,0:T(8,128)(2,1)} %get-tuple-element.10.fk_hbm, bf16[32,512,128]{2,1,0:T(8,128)(2,1)} %gather_fusion.1), custom_call_target="tpu_custom_call" | custom-call | flops 3221225472 | bytes 8388608 | tf_op jit(solution)/shard_map/pallas_call | solution.py:294
  260.4 2.3 copy.26
  (4 shorter events, 0.0 us)

commit v9 on v8

--- a/solution.py
+++ b/solution.py
@@ -89,6 +89,34 @@
         ],
         compiler_params=pltpu.CompilerParams(collective_id=collective_id, has_side_effects=True),
     )(*arrays)
+
+
+def pick_kernel(order_ref, *refs):
+    out_ref = refs[-1]
+    for t, ref in enumerate(refs[:-1]):
+        out_ref[t] = ref[0]
+
+
+def pick_blocks(table, order, per_step=4):
+    slots = order.shape[0]
+    _, block, width = table.shape
+    if slots % per_step:
+        per_step = 1
+
+    def spec(t):
+        return pl.BlockSpec((1, block, width), lambda s, order_ref: (order_ref[s * per_step + t], 0, 0))
+
+    grid_spec = pltpu.PrefetchScalarGridSpec(
+        num_scalar_prefetch=1,
+        grid=(slots // per_step,),
+        in_specs=[spec(t) for t in range(per_step)],
+        out_specs=pl.BlockSpec((per_step, block, width), lambda s, order_ref: (s, 0, 0)),
+    )
+    return pl.pallas_call(
+        pick_kernel,
+        out_shape=jax.ShapeDtypeStruct((slots, block, width), table.dtype),
+        grid_spec=grid_spec,
+    )(order, *([table] * per_step))
 
 
 def route_tables(picks, local_blocks, ctx_count):
@@ -346,13 +374,13 @@
     wanted = jnp.sum(asked.astype(jnp.int32) * within[:, :, None], axis=1)
     far_index = (mine_owner * capacity + mine_pos).astype(jnp.int32)
 
-    send_k = k_blocks[wanted.reshape(-1)]
+    send_k = pick_blocks(k_blocks, wanted.reshape(-1).astype(jnp.int32))
     far_k, v_heads, q_heads = exchange(
         (send_k, values, queries), (ctx_move, head_in, head_in), axes, collective_id=1
     )
     q_blocks = q_heads.reshape(local_blocks, BLOCK, width)
     v_blocks = v_heads.reshape(local_blocks, BLOCK, width)
-    send_v = v_blocks[wanted.reshape(-1)]
+    send_v = pick_blocks(v_blocks, wanted.reshape(-1).astype(jnp.int32))
     return finish_attention(
         far_index, q_blocks, k_blocks, v_blocks, far_k, send_v, score_scale, axes, tok_rows,
         capacity,

time: 265 us -> 272 us (1.026)
  Pallas kernels: 249 us -> 263 us
  local copies, waits for them, and re-layouts: 11.6 us -> 3.56 us
    pallas_call x0 -> x2, Pallas kernels: none -> 13.9 us  [pick_blocks(): pl.pallas_call(pick_kernel, out_shape=jax.ShapeDtypeStruct((slots, block,...]
    gather x2 -> x0, local copies, waits for them, and re-layouts: 8.56 us -> none  [the longest x1 4.28 us: local(): send_k = k_blocks[wanted.reshape(-1)]]
where the time goes in v9:
time: 272 us; the launch traced here: 269 us
  Pallas kernels  263 us (97%)
  local copies, waits for them, and re-layouts  3.56 us (1%)
    pallas_call x2, Pallas kernels, exchange(): pl.pallas_call(functools.partial(exchange_kernel, axes=axes, jobs=tuple(j...  131 us
    pallas_call x1, Pallas kernels, finish_attention(): pl.pallas_call(kernel, out_shape=jax.ShapeDtypeStruct((tok_rows, n * widt...  118 us
    pallas_call x2, Pallas kernels, pick_blocks(): pl.pallas_call(pick_kernel, out_shape=jax.ShapeDtypeStruct((slots, block,...  13.9 us

profile of v9, /device:TPU:1, one launch (start us, length us, event | category | flops | bytes accessed | tf_op | source)
XLA Modules:
  0.0 268.6 jit_solution(15243510474289610133)
XLA Ops:
  0.0 0.7 and_select_fusion
  0.7 0.1 copy.23
  0.8 0.1 mul.19
  0.9 0.1 copy.19
  1.0 0.1 reshape.29
  1.1 0.1 copy.20
  1.2 0.5 fusion.3
  1.6 0.7 add_reduce_fusion.idx_ref
  2.3 0.1 copy.22
  2.4 0.1 select_reduce_fusion
  2.5 0.1 copy.24
  2.6 0.6 reshape.30.order_ref
  3.2 19.1 %shard_map.46 = bf16[4096,128]{1,0:T(8,128)(2,1)} custom-call(bf16[256,2048]{1,0:T(8,128)(2,1)} %refs_0_.1), custom_call_target="tpu_custom_call" | custom-call | tf_op jit(solution)/shard_map/pallas_call | solution.py:81
  22.3 6.9 %shard_map.47.refs_0_ = bf16[32,512,128]{2,1,0:T(8,128)(2,1)} custom-call(s32[32]{0:T(128)} %reshape.30.order_ref, bf16[8,512,128]{2,1,0:T(8,128)(2,1)} %bitcast.3, bf16[8,512,128]{2,1,0:T(8,128)(2,1)} %bitcast.4, bf16[8,512,128]{2,1,0:T(8,128)(2,1)} %bitcast.5, bf16[8,512,128]{2,1,0:T(8,128)(2,1)} %bitcast.6), custom_call_target="tpu_custom_call" | custom-call | tf_op jit(solution)/shard_map/pallas_call | solution.py:115
  29.3 112.2 %shard_map.48 = (bf16[32,512,128]{2,1,0:T(8,128)(2,1)}, bf16[4096,128]{1,0:T(8,128)(2,1)}, bf16[4096,128]{1,0:T(8,128)(2,1)}) custom-call(bf16[32,512,128]{2,1,0:T(8,128)(2,1)} %shard_map.47.refs_0_, bf16[256,2048]{1,0:T(8,128)(2,1)} %refs_1_.1, bf16[256,2048]{1,0:T(8,128)(2,1)} %refs_2_.1), custom_call_target="tpu_custom_call" | custom-call | tf_op jit(solution)/shard_map/pallas_call | solution.py:81
  141.5 6.9 %shard_map.49.sv_hbm = bf16[32,512,128]{2,1,0:T(8,128)(2,1)} custom-call(s32[32]{0:T(128)} %reshape.30.order_ref, bf16[8,512,128]{2,1,0:T(8,128)(2,1)} %bitcast.8, bf16[8,512,128]{2,1,0:T(8,128)(2,1)} %bitcast.9, bf16[8,512,128]{2,1,0:T(8,128)(2,1)} %bitcast.10, bf16[8,512,128]{2,1,0:T(8,128)(2,1)} %bitcast.11), custom_call_target="tpu_custom_call" | custom-call | tf_op jit(solution)/shard_map/pallas_call | solution.py:115
  148.4 117.9 %shard_map.50 = bf16[256,2048]{1,0:T(8,128)(2,1)} custom-call(s32[16]{0:T(128)} %add_reduce_fusion.idx_ref, bf16[8,512,128]{2,1,0:T(8,128)(2,1)} %bitcast.13, bf16[8,512,128]{2,1,0:T(8,128)(2,1)} %bitcast.7, bf16[8,512,128]{2,1,0:T(8,128)(2,1)} %bitcast.12, bf16[32,512,128]{2,1,0:T(8,128)(2,1)} %get-tuple-element.10.fk_hbm, ...), custom_call_target="tpu_custom_call" | custom-call | flops 3221225472 | bytes 8388608 | tf_op jit(solution)/shard_map/pallas_call | solution.py:322
  266.3 2.3 copy.26
  (2 shorter events, 0.0 us)

commit v10 on v8

--- a/solution.py
+++ b/solution.py
@@ -118,7 +118,7 @@
 def finish_kernel(
     idx_ref, q_hbm, k_hbm, v_hbm, fk_hbm, sv_hbm, y_ref,
     qv, kv, vv, fkv, fvv, wts, base, fac, stage,
-    load_sems, ctx_send, ctx_recv, out_send, out_recv,
+    load_sems, ctx_send, ctx_recv, out_send, out_recv, q_send, q_recv,
     *, axes, heads_here, scale, capacity,
 ):
     n = lax.axis_size("head")
@@ -160,12 +160,27 @@
         copy.start()
         v_copies.append(copy)
 
-    loads = [
-        pltpu.make_async_copy(src, dst, load_sems.at[a])
-        for a, (src, dst) in enumerate(((q_hbm, qv), (k_hbm, kv), (v_hbm, vv), (fk_hbm, fkv)))
-    ]
-    for load in loads:
+    def q_rows(owner):
+        return qv.at[owner // per_block, pl.ds((owner % per_block) * rows, rows), :]
+
+    def q_cols(peer):
+        return q_hbm.at[:, pl.ds(peer * width, width)]
+
+    loads = [pltpu.make_async_copy(q_cols(me), q_rows(me), q_send.at[0])]
+    loads[0].start()
+    for k in range(1, n):
+        peer = (me + k) % n
+        copy = pltpu.make_async_remote_copy(
+            src_ref=q_cols(peer), dst_ref=q_rows(me),
+            send_sem=q_send.at[k], recv_sem=q_recv.at[k],
+            device_id=device("head", peer), device_id_type=MESH,
+        )
+        copy.start()
+        loads.append(copy)
+    for a, (src, dst) in enumerate(((k_hbm, kv), (v_hbm, vv), (fk_hbm, fkv))):
+        load = pltpu.make_async_copy(src, dst, load_sems.at[a])
         load.start()
+        loads.append(load)
     for load in loads:
         load.wait()
 
@@ -280,9 +295,9 @@
 
 
 def finish_attention(
-    far_index, q_blocks, k_blocks, v_blocks, far_k, send_v, scale, axes, tok_rows, capacity
+    far_index, queries, k_blocks, v_blocks, far_k, send_v, scale, axes, tok_rows, capacity
 ):
-    local_blocks, _, width = q_blocks.shape
+    local_blocks, _, width = k_blocks.shape
     heads_here = width // HD
     n = HEADS // heads_here
     m_ctx = send_v.shape[0] // capacity
@@ -297,7 +312,7 @@
         in_specs=[pl.BlockSpec(memory_space=pltpu.SMEM)] + [anywhere] * 5,
         out_specs=anywhere,
         scratch_shapes=[
-            pltpu.VMEM(q_blocks.shape, jnp.bfloat16),
+            pltpu.VMEM(k_blocks.shape, jnp.bfloat16),
             pltpu.VMEM(k_blocks.shape, jnp.bfloat16),
             pltpu.VMEM(v_blocks.shape, jnp.bfloat16),
             pltpu.VMEM(far_k.shape, jnp.bfloat16),
@@ -311,6 +326,8 @@
             pltpu.SemaphoreType.DMA((m_ctx,)),
             pltpu.SemaphoreType.DMA((local_blocks * (BLOCK // tok_rows),)),
             pltpu.SemaphoreType.DMA((n,)),
+            pltpu.SemaphoreType.DMA((n,)),
+            pltpu.SemaphoreType.DMA((n,)),
         ],
         compiler_params=pltpu.CompilerParams(
             collective_id=2, has_side_effects=True, vmem_limit_bytes=60 * 1024 * 1024
@@ -320,7 +337,7 @@
             transcendentals=local_blocks * heads_here * 3 * BLOCK * BLOCK,
             bytes_accessed=local_blocks * BLOCK * width * 2 * 8,
         ),
-    )(far_index, q_blocks, k_blocks, v_blocks, far_k, send_v)
+    )(far_index, queries, k_blocks, v_blocks, far_k, send_v)
 
 
 def local(queries, keys, values, picks, axes):
@@ -347,14 +364,11 @@
     far_index = (mine_owner * capacity + mine_pos).astype(jnp.int32)
 
     send_k = k_blocks[wanted.reshape(-1)]
-    far_k, v_heads, q_heads = exchange(
-        (send_k, values, queries), (ctx_move, head_in, head_in), axes, collective_id=1
-    )
-    q_blocks = q_heads.reshape(local_blocks, BLOCK, width)
+    far_k, v_heads = exchange((send_k, values), (ctx_move, head_in), axes, collective_id=1)
     v_blocks = v_heads.reshape(local_blocks, BLOCK, width)
     send_v = v_blocks[wanted.reshape(-1)]
     return finish_attention(
-        far_index, q_blocks, k_blocks, v_blocks, far_k, send_v, score_scale, axes, tok_rows,
+        far_index, queries, k_blocks, v_blocks, far_k, send_v, score_scale, axes, tok_rows,
         capacity,
     )
 

time: 265 us -> 265 us (level)
  no operation moved by 1% of the time
where the time goes in v10:
time: 265 us; the launch traced here: 263 us
  Pallas kernels  249 us (94%)
  local copies, waits for them, and re-layouts  11.6 us (4%)
    pallas_call x2, Pallas kernels, exchange(): pl.pallas_call(functools.partial(exchange_kernel, axes=axes, jobs=tuple(j...  132 us
    pallas_call x1, Pallas kernels, finish_attention(): pl.pallas_call(kernel, out_shape=jax.ShapeDtypeStruct((tok_rows, n * widt...  117 us

profile of v10, /device:TPU:1, one launch (start us, length us, event | category | flops | bytes accessed | tf_op | source)
XLA Modules:
  0.0 262.5 jit_solution(3968508285891296720)
XLA Ops:
  0.0 0.7 and_select_fusion
  0.7 0.1 copy.23
  0.8 0.1 mul.19
  0.9 0.1 copy.19
  1.0 0.1 reshape.54
  1.1 0.1 copy.20
  1.2 0.5 fusion.4
  1.6 0.7 add_reduce_fusion.idx_ref
  2.3 0.1 copy.22
  2.4 0.1 select_reduce_fusion
  2.5 0.1 copy.24
  2.6 0.1 reshape.56
  2.7 19.3 %shard_map.46 = bf16[4096,128]{1,0:T(8,128)(2,1)} custom-call(bf16[256,2048]{1,0:T(8,128)(2,1)} %refs_0_.1), custom_call_target="tpu_custom_call" | custom-call | tf_op jit(solution)/shard_map/pallas_call | solution.py:81
  22.1 4.3 %gather_fusion = bf16[32,512,128]{2,1,0:T(8,128)(2,1)} fusion(bf16[8,512,128]{2,1,0:T(8,128)(2,1)} %bitcast.4, s32[1024]{0:T(1024)S(1)} %pad_clamp_fusion), kind=kCustom, calls=%fused_computation | custom fusion | bytes 8388736 | tf_op jit(solution)/shard_map/gather | solution.py:366
  26.4 112.9 %shard_map.47 = (bf16[32,512,128]{2,1,0:T(8,128)(2,1)}, bf16[4096,128]{1,0:T(8,128)(2,1)}) custom-call(bf16[32,512,128]{2,1,0:T(8,128)(2,1)} %gather_fusion, bf16[256,2048]{1,0:T(8,128)(2,1)} %refs_1_.1), custom_call_target="tpu_custom_call" | custom-call | tf_op jit(solution)/shard_map/pallas_call | solution.py:81
  139.3 4.3 %gather_fusion.1 = bf16[32,512,128]{2,1,0:T(8,128)(2,1)} fusion(bf16[8,512,128]{2,1,0:T(8,128)(2,1)} %bitcast.6, s32[1024]{0:T(1024)S(1)} %pad_clamp_fusion), kind=kCustom, calls=%fused_computation.1 | custom fusion | bytes 8388736 | tf_op jit(solution)/shard_map/gather | solution.py:369
  143.6 116.7 %shard_map.48 = bf16[256,2048]{1,0:T(8,128)(2,1)} custom-call(s32[16]{0:T(128)} %add_reduce_fusion.idx_ref, bf16[256,2048]{1,0:T(8,128)(2,1)} %q_hbm.1, bf16[8,512,128]{2,1,0:T(8,128)(2,1)} %bitcast.5, bf16[8,512,128]{2,1,0:T(8,128)(2,1)} %bitcast.7, bf16[32,512,128]{2,1,0:T(8,128)(2,1)} %get-tuple-element.8.fk_hbm, bf16[32,512,128]{2,1,0:T(8,128)(2,1)} %gather_fusion.1), custom_call_target="tpu_custom_call" | custom-call | flops 3221225472 | bytes 8388608 | tf_op jit(solution)/shard_map/pallas_call | solution.py:309
  260.2 2.3 copy.26
  (4 shorter events, 0.0 us)

commit v11 on v10

--- a/solution.py
+++ b/solution.py
@@ -14,6 +14,18 @@
 HD = 128
 BLOCK = 512
 RSEL = 2
+
+
+def peer_order(axis, n):
+    if axis != "ctx" or n % 2:
+        return list(range(1, n))
+    ring = n // 2
+
+    def reach(k):
+        step = k % ring
+        return min(step, ring - step) + 2 * (k // ring)
+
+    return sorted(range(1, n), key=lambda k: (-reach(k), k))
 
 
 def exchange_kernel(*refs, axes, jobs):
@@ -52,7 +64,7 @@
         )
         own.start()
         copies.append(own)
-        for k in range(1, n):
+        for k in peer_order(axis, n):
             peer = (me + k) % n
             copy = pltpu.make_async_remote_copy(
                 src_ref=view(srcs[a], split_axis, peer, n),
@@ -150,7 +162,7 @@
 
     v_copies = [pltpu.make_async_copy(rows_of(sv_hbm, c_me), rows_of(fvv, c_me), ctx_send.at[0])]
     v_copies[0].start()
-    for k in range(1, m_ctx):
+    for k in peer_order("ctx", m_ctx):
         peer = (c_me + k) % m_ctx
         copy = pltpu.make_async_remote_copy(
             src_ref=rows_of(sv_hbm, peer), dst_ref=rows_of(fvv, c_me),

time: 265 us -> 268 us (1.011)
  Pallas kernels: 249 us -> 253 us
    pallas_call x1, Pallas kernels: 117 us -> 122 us  [finish_attention(): pl.pallas_call(kernel, out_shape=jax.ShapeDtypeStruct((tok_rows, n * widt...]
where the time goes in v11:
time: 268 us; the launch traced here: 266 us
  Pallas kernels  253 us (94%)
  local copies, waits for them, and re-layouts  11.6 us (4%)
    pallas_call x2, Pallas kernels, exchange(): pl.pallas_call(functools.partial(exchange_kernel, axes=axes, jobs=tuple(j...  131 us
    pallas_call x1, Pallas kernels, finish_attention(): pl.pallas_call(kernel, out_shape=jax.ShapeDtypeStruct((tok_rows, n * widt...  122 us

profile of v11, /device:TPU:1, one launch (start us, length us, event | category | flops | bytes accessed | tf_op | source)
XLA Modules:
  0.0 266.4 jit_solution(960438664349875611)
XLA Ops:
  0.0 0.7 and_select_fusion
  0.7 0.1 copy.23
  0.8 0.1 mul.19
  0.9 0.1 copy.19
  1.0 0.1 reshape.54
  1.1 0.1 copy.20
  1.2 0.5 fusion.4
  1.6 0.7 add_reduce_fusion.idx_ref
  2.3 0.1 copy.22
  2.4 0.1 select_reduce_fusion
  2.5 0.1 copy.24
  2.6 0.1 reshape.56
  2.7 19.3 %shard_map.46 = bf16[4096,128]{1,0:T(8,128)(2,1)} custom-call(bf16[256,2048]{1,0:T(8,128)(2,1)} %refs_0_.1), custom_call_target="tpu_custom_call" | custom-call | tf_op jit(solution)/shard_map/pallas_call | solution.py:93
  22.1 4.3 %gather_fusion = bf16[32,512,128]{2,1,0:T(8,128)(2,1)} fusion(bf16[8,512,128]{2,1,0:T(8,128)(2,1)} %bitcast.4, s32[1024]{0:T(1024)S(1)} %pad_clamp_fusion), kind=kCustom, calls=%fused_computation | custom fusion | bytes 8388736 | tf_op jit(solution)/shard_map/gather | solution.py:378
  26.4 111.2 %shard_map.47 = (bf16[32,512,128]{2,1,0:T(8,128)(2,1)}, bf16[4096,128]{1,0:T(8,128)(2,1)}) custom-call(bf16[32,512,128]{2,1,0:T(8,128)(2,1)} %gather_fusion, bf16[256,2048]{1,0:T(8,128)(2,1)} %refs_1_.1), custom_call_target="tpu_custom_call" | custom-call | tf_op jit(solution)/shard_map/pallas_call | solution.py:93
  137.6 4.3 %gather_fusion.1 = bf16[32,512,128]{2,1,0:T(8,128)(2,1)} fusion(bf16[8,512,128]{2,1,0:T(8,128)(2,1)} %bitcast.6, s32[1024]{0:T(1024)S(1)} %pad_clamp_fusion), kind=kCustom, calls=%fused_computation.1 | custom fusion | bytes 8388736 | tf_op jit(solution)/shard_map/gather | solution.py:381
  141.9 122.2 %shard_map.48 = bf16[256,2048]{1,0:T(8,128)(2,1)} custom-call(s32[16]{0:T(128)} %add_reduce_fusion.idx_ref, bf16[256,2048]{1,0:T(8,128)(2,1)} %q_hbm.1, bf16[8,512,128]{2,1,0:T(8,128)(2,1)} %bitcast.5, bf16[8,512,128]{2,1,0:T(8,128)(2,1)} %bitcast.7, bf16[32,512,128]{2,1,0:T(8,128)(2,1)} %get-tuple-element.8.fk_hbm, bf16[32,512,128]{2,1,0:T(8,128)(2,1)} %gather_fusion.1), custom_call_target="tpu_custom_call" | custom-call | flops 3221225472 | bytes 8388608 | tf_op jit(solution)/shard_map/pallas_call | solution.py:321
  264.1 2.3 copy.26
  (4 shorter events, 0.0 us)

commit v12 on v10

--- a/solution.py
+++ b/solution.py
@@ -205,10 +205,10 @@
             f0 = jnp.exp(m0 - top)
             f1 = jnp.exp(stats[0][0] - top)
             f2 = jnp.exp(stats[1][0] - top)
-            base[i, :, cols] = acc0 * f0
-            fac[i, h * 3] = f1
-            fac[i, h * 3 + 1] = f2
-            fac[i, h * 3 + 2] = l0 * f0 + stats[0][1] * f1 + stats[1][1] * f2
+            scale_back = 1.0 / (l0 * f0 + stats[0][1] * f1 + stats[1][1] * f2)
+            base[i, :, cols] = acc0 * (f0 * scale_back)
+            fac[i, h * 2] = f1 * scale_back
+            fac[i, h * 2 + 1] = f2 * scale_back
         return carry
 
     lax.fori_loop(0, local_blocks, prepare, 0)
@@ -264,8 +264,8 @@
             p2 = jnp.dot(
                 wts[i, h * RSEL + 1], fvv[j1, :, cols], preferred_element_type=jnp.float32
             )
-            numer = base[i, :, cols] + p1 * fac[i, h * 3] + p2 * fac[i, h * 3 + 1]
-            stage[i, :, cols] = (numer / fac[i, h * 3 + 2]).astype(stage.dtype)
+            numer = base[i, :, cols] + p1 * fac[i, h * 2] + p2 * fac[i, h * 2 + 1]
+            stage[i, :, cols] = numer.astype(stage.dtype)
 
         @pl.when(t >= 1)
         def _():
@@ -319,7 +319,7 @@
             pltpu.VMEM(send_v.shape, jnp.bfloat16),
             pltpu.VMEM((local_blocks, heads_here * RSEL, BLOCK, BLOCK), jnp.bfloat16),
             pltpu.VMEM((local_blocks, BLOCK, width), jnp.float32),
-            pltpu.VMEM((local_blocks, heads_here * 3, BLOCK, 1), jnp.float32),
+            pltpu.VMEM((local_blocks, heads_here * 2, BLOCK, 1), jnp.float32),
             pltpu.VMEM((local_blocks, BLOCK, width), jnp.bfloat16),
             pltpu.SemaphoreType.DMA((4,)),
             pltpu.SemaphoreType.DMA((m_ctx,)),

time: 265 us -> 265 us (level)
  no operation moved by 1% of the time
where the time goes in v12:
time: 265 us; the launch traced here: 263 us
  Pallas kernels  249 us (94%)
  local copies, waits for them, and re-layouts  11.6 us (4%)
    pallas_call x2, Pallas kernels, exchange(): pl.pallas_call(functools.partial(exchange_kernel, axes=axes, jobs=tuple(j...  132 us
    pallas_call x1, Pallas kernels, finish_attention(): pl.pallas_call(kernel, out_shape=jax.ShapeDtypeStruct((tok_rows, n * widt...  117 us

profile of v12, /device:TPU:1, one launch (start us, length us, event | category | flops | bytes accessed | tf_op | source)
XLA Modules:
  0.0 262.5 jit_solution(7975642010545171917)
XLA Ops:
  0.0 0.7 and_select_fusion
  0.7 0.1 copy.23
  0.8 0.1 mul.19
  0.9 0.1 copy.19
  1.0 0.1 reshape.54
  1.1 0.1 copy.20
  1.2 0.5 fusion.4
  1.6 0.7 add_reduce_fusion.idx_ref
  2.3 0.1 copy.22
  2.4 0.1 select_reduce_fusion
  2.5 0.1 copy.24
  2.6 0.1 reshape.56
  2.7 19.3 %shard_map.46 = bf16[4096,128]{1,0:T(8,128)(2,1)} custom-call(bf16[256,2048]{1,0:T(8,128)(2,1)} %refs_0_.1), custom_call_target="tpu_custom_call" | custom-call | tf_op jit(solution)/shard_map/pallas_call | solution.py:81
  22.1 4.3 %gather_fusion = bf16[32,512,128]{2,1,0:T(8,128)(2,1)} fusion(bf16[8,512,128]{2,1,0:T(8,128)(2,1)} %bitcast.4, s32[1024]{0:T(1024)S(1)} %pad_clamp_fusion), kind=kCustom, calls=%fused_computation | custom fusion | bytes 8388736 | tf_op jit(solution)/shard_map/gather | solution.py:366
  26.4 112.9 %shard_map.47 = (bf16[32,512,128]{2,1,0:T(8,128)(2,1)}, bf16[4096,128]{1,0:T(8,128)(2,1)}) custom-call(bf16[32,512,128]{2,1,0:T(8,128)(2,1)} %gather_fusion, bf16[256,2048]{1,0:T(8,128)(2,1)} %refs_1_.1), custom_call_target="tpu_custom_call" | custom-call | tf_op jit(solution)/shard_map/pallas_call | solution.py:81
  139.3 4.3 %gather_fusion.1 = bf16[32,512,128]{2,1,0:T(8,128)(2,1)} fusion(bf16[8,512,128]{2,1,0:T(8,128)(2,1)} %bitcast.6, s32[1024]{0:T(1024)S(1)} %pad_clamp_fusion), kind=kCustom, calls=%fused_computation.1 | custom fusion | bytes 8388736 | tf_op jit(solution)/shard_map/gather | solution.py:369
  143.6 116.7 %shard_map.48 = bf16[256,2048]{1,0:T(8,128)(2,1)} custom-call(s32[16]{0:T(128)} %add_reduce_fusion.idx_ref, bf16[256,2048]{1,0:T(8,128)(2,1)} %q_hbm.1, bf16[8,512,128]{2,1,0:T(8,128)(2,1)} %bitcast.5, bf16[8,512,128]{2,1,0:T(8,128)(2,1)} %bitcast.7, bf16[32,512,128]{2,1,0:T(8,128)(2,1)} %get-tuple-element.8.fk_hbm, bf16[32,512,128]{2,1,0:T(8,128)(2,1)} %gather_fusion.1), custom_call_target="tpu_custom_call" | custom-call | flops 3221225472 | bytes 8388608 | tf_op jit(solution)/shard_map/pallas_call | solution.py:309
  260.2 2.3 copy.26
  (4 shorter events, 0.0 us)

commit v13 on v10

--- a/solution.py
+++ b/solution.py
@@ -95,10 +95,9 @@
     slots = local_blocks * RSEL
     owners = (picks // local_blocks).reshape(ctx_count, slots)
     within = (picks % local_blocks).reshape(ctx_count, slots)
-    owner_ids = jnp.arange(ctx_count, dtype=jnp.int32)
-    one_hot = (owners[:, :, None] == owner_ids[None, None, :]).astype(jnp.int32)
-    running = jnp.cumsum(one_hot, axis=1)
-    position = jnp.sum(one_hot * running, axis=-1) - 1
+    order = jnp.arange(slots, dtype=jnp.int32)
+    earlier = (owners[:, :, None] == owners[:, None, :]) & (order[None, None, :] < order[None, :, None])
+    position = jnp.sum(earlier.astype(jnp.int32), axis=-1)
     return (owners, within, position)
 
 

time: 265 us -> 265 us (level)
  no operation moved by 1% of the time
where the time goes in v13:
time: 265 us; the launch traced here: 262 us
  Pallas kernels  249 us (94%)
  local copies, waits for them, and re-layouts  11.4 us (4%)
    pallas_call x2, Pallas kernels, exchange(): pl.pallas_call(functools.partial(exchange_kernel, axes=axes, jobs=tuple(j...  132 us
    pallas_call x1, Pallas kernels, finish_attention(): pl.pallas_call(kernel, out_shape=jax.ShapeDtypeStruct((tok_rows, n * widt...  117 us

profile of v13, /device:TPU:1, one launch (start us, length us, event | category | flops | bytes accessed | tf_op | source)
XLA Modules:
  0.0 262.2 jit_solution(5052869137030043013)
XLA Ops:
  0.0 0.7 and_select_fusion
  0.7 0.1 copy.8
  0.8 0.1 mul.15
  0.9 0.1 copy.7
  1.0 0.1 reshape.68
  1.1 0.4 convert_reduce_fusion
  1.5 0.1 select_reduce_fusion
  1.7 0.5 add_bitcast_fusion.idx_ref
  2.2 0.1 copy.9
  2.3 0.1 reshape.70
  2.4 19.3 %shard_map.46 = bf16[4096,128]{1,0:T(8,128)(2,1)} custom-call(bf16[256,2048]{1,0:T(8,128)(2,1)} %refs_0_.1), custom_call_target="tpu_custom_call" | custom-call | tf_op jit(solution)/shard_map/pallas_call | solution.py:81
  21.7 4.3 %gather_fusion = bf16[32,512,128]{2,1,0:T(8,128)(2,1)} fusion(bf16[8,512,128]{2,1,0:T(8,128)(2,1)} %bitcast.6, s32[1024]{0:T(1024)S(1)} %pad_clamp_fusion), kind=kCustom, calls=%fused_computation | custom fusion | bytes 8388736 | tf_op jit(solution)/shard_map/gather | solution.py:365
  26.0 112.9 %shard_map.47 = (bf16[32,512,128]{2,1,0:T(8,128)(2,1)}, bf16[4096,128]{1,0:T(8,128)(2,1)}) custom-call(bf16[32,512,128]{2,1,0:T(8,128)(2,1)} %gather_fusion, bf16[256,2048]{1,0:T(8,128)(2,1)} %refs_1_.1), custom_call_target="tpu_custom_call" | custom-call | tf_op jit(solution)/shard_map/pallas_call | solution.py:81
  138.9 4.3 %gather_fusion.1 = bf16[32,512,128]{2,1,0:T(8,128)(2,1)} fusion(bf16[8,512,128]{2,1,0:T(8,128)(2,1)} %bitcast.8, s32[1024]{0:T(1024)S(1)} %pad_clamp_fusion), kind=kCustom, calls=%fused_computation.1 | custom fusion | bytes 8388736 | tf_op jit(solution)/shard_map/gather | solution.py:368
  143.2 116.7 %shard_map.48 = bf16[256,2048]{1,0:T(8,128)(2,1)} custom-call(s32[16]{0:T(128)} %add_bitcast_fusion.idx_ref, bf16[256,2048]{1,0:T(8,128)(2,1)} %q_hbm.1, bf16[8,512,128]{2,1,0:T(8,128)(2,1)} %bitcast.7, bf16[8,512,128]{2,1,0:T(8,128)(2,1)} %bitcast.9, bf16[32,512,128]{2,1,0:T(8,128)(2,1)} %get-tuple-element.8.fk_hbm, bf16[32,512,128]{2,1,0:T(8,128)(2,1)} %gather_fusion.1), custom_call_target="tpu_custom_call" | custom-call | flops 3221225472 | bytes 8388608 | tf_op jit(solution)/shard_map/pallas_call | solution.py:308
  259.9 2.3 copy.11
  (4 shorter events, 0.0 us)

commit v14 on v10

--- a/solution.py
+++ b/solution.py
@@ -350,7 +350,7 @@
     score_scale = 1.0 / math.sqrt(HD)
     head_in = ("head", 1, 0)
     ctx_move = ("ctx", 0, 0)
-    (k_heads,) = exchange((keys,), (head_in,), axes, collective_id=0)
+    k_heads, v_heads = exchange((keys, values), (head_in, head_in), axes, collective_id=0)
     local_blocks = k_heads.shape[0] // BLOCK
     k_blocks = k_heads.reshape(local_blocks, BLOCK, width)
 
@@ -364,9 +364,9 @@
     far_index = (mine_owner * capacity + mine_pos).astype(jnp.int32)
 
     send_k = k_blocks[wanted.reshape(-1)]
-    far_k, v_heads = exchange((send_k, values), (ctx_move, head_in), axes, collective_id=1)
     v_blocks = v_heads.reshape(local_blocks, BLOCK, width)
     send_v = v_blocks[wanted.reshape(-1)]
+    (far_k,) = exchange((send_k,), (ctx_move,), axes, collective_id=1)
     return finish_attention(
         far_index, queries, k_blocks, v_blocks, far_k, send_v, score_scale, axes, tok_rows,
         capacity,

time: 265 us -> 275 us (1.038)
  Pallas kernels: 249 us -> 260 us
    pallas_call x2, Pallas kernels: 132 us -> 143 us  [exchange(): pl.pallas_call(functools.partial(exchange_kernel, axes=axes, jobs=tuple(j...]
where the time goes in v14:
time: 275 us; the launch traced here: 272 us
  Pallas kernels  260 us (95%)
  local copies, waits for them, and re-layouts  10.4 us (4%)
    pallas_call x2, Pallas kernels, exchange(): pl.pallas_call(functools.partial(exchange_kernel, axes=axes, jobs=tuple(j...  143 us
    pallas_call x1, Pallas kernels, finish_attention(): pl.pallas_call(kernel, out_shape=jax.ShapeDtypeStruct((tok_rows, n * widt...  117 us

profile of v14, /device:TPU:1, one launch (start us, length us, event | category | flops | bytes accessed | tf_op | source)
XLA Modules:
  0.0 272.4 jit_solution(17229515729836427234)
XLA Ops:
  0.0 0.7 and_select_fusion
  0.7 0.1 copy.19
  0.8 0.1 reshape.54
  0.9 0.1 copy.20
  1.0 0.5 fusion.4
  1.4 0.7 add_reduce_fusion.idx_ref
  2.1 0.1 copy.22
  2.2 0.1 copy.23
  2.3 0.1 mul.19
  2.4 0.1 select_reduce_fusion
  2.5 0.1 copy.24
  2.6 0.1 reshape.57
  2.7 31.1 %shard_map.46 = (bf16[4096,128]{1,0:T(8,128)(2,1)}, bf16[4096,128]{1,0:T(8,128)(2,1)}) custom-call(bf16[256,2048]{1,0:T(8,128)(2,1)} %refs_0_.1, bf16[256,2048]{1,0:T(8,128)(2,1)} %refs_1_.1), custom_call_target="tpu_custom_call" | custom-call | tf_op jit(solution)/shard_map/pallas_call | solution.py:81
  33.9 4.3 %gather_fusion = bf16[32,512,128]{2,1,0:T(8,128)(2,1)} fusion(bf16[8,512,128]{2,1,0:T(8,128)(2,1)} %bitcast.4, s32[1024]{0:T(1024)S(1)} %pad_clamp_fusion), kind=kCustom, calls=%fused_computation | custom fusion | bytes 8388736 | tf_op jit(solution)/shard_map/gather | solution.py:366
  38.1 0.0 copy-start
  38.1 111.7 %shard_map.47.fk_hbm = bf16[32,512,128]{2,1,0:T(8,128)(2,1)} custom-call(bf16[32,512,128]{2,1,0:T(8,128)(2,1)} %gather_fusion), custom_call_target="tpu_custom_call" | custom-call | tf_op jit(solution)/shard_map/pallas_call | solution.py:81
  149.9 0.0 copy-done
  149.9 3.1 %gather_fusion.1 = bf16[32,512,128]{2,1,0:T(8,128)(2,1)} fusion(bf16[8,512,128]{2,1,0:T(8,128)(2,1)S(1)} %bitcast.7, s32[1024]{0:T(1024)S(1)} %pad_clamp_fusion), kind=kCustom, calls=%fused_computation.1 | custom fusion | bytes 8388736 | tf_op jit(solution)/shard_map/gather | solution.py:368
  152.9 117.2 %shard_map.48 = bf16[256,2048]{1,0:T(8,128)(2,1)} custom-call(s32[16]{0:T(128)} %add_reduce_fusion.idx_ref, bf16[256,2048]{1,0:T(8,128)(2,1)} %q_hbm.1, bf16[8,512,128]{2,1,0:T(8,128)(2,1)} %bitcast.5, bf16[8,512,128]{2,1,0:T(8,128)(2,1)} %bitcast.6, bf16[32,512,128]{2,1,0:T(8,128)(2,1)} %shard_map.47.fk_hbm, bf16[32,512,128]{2,1,0:T(8,128)(2,1)} %gather_fusion.1), custom_call_target="tpu_custom_call" | custom-call | flops 3221225472 | bytes 8388608 | tf_op jit(solution)/shard_map/pallas_call | solution.py:309
  270.1 2.3 copy.26
  (4 shorter events, 0.0 us)
Async XLA Ops:
  38.1 111.7 %copy-start = (bf16[4096,128]{1,0:T(8,128)(2,1)S(1)}, bf16[4096,128]{1,0:T(8,128)(2,1)}, u32[]{:S(2)}) copy-start(bf16[4096,128]{1,0:T(8,128)(2,1)} %get-tuple-element.8) | copy-start | bytes 3145732

commit v15 on v14

--- a/solution.py
+++ b/solution.py
@@ -43,38 +43,91 @@
         return ref.at[tuple(where)]
 
     copies = []
-    for a, (axis, split_axis, concat_axis) in enumerate(jobs):
+    halves = []
+    for a, (axis, split_axis, concat_axis, parity) in enumerate(jobs):
         n = lax.axis_size(axis)
         me = lax.axis_index(axis)
-        own = pltpu.make_async_copy(
-            view(srcs[a], split_axis, me, n), view(dsts[a], concat_axis, me, n),
-            send_sems.at[a, 0],
-        )
-        own.start()
-        copies.append(own)
-        for k in range(1, n):
+        if parity is None:
+            own = pltpu.make_async_copy(
+                view(srcs[a], split_axis, me, n), view(dsts[a], concat_axis, me, n),
+                send_sems.at[a, 0],
+            )
+            own.start()
+            copies.append(own)
+            for k in range(1, n):
+                peer = (me + k) % n
+                copy = pltpu.make_async_remote_copy(
+                    src_ref=view(srcs[a], split_axis, peer, n),
+                    dst_ref=view(dsts[a], concat_axis, me, n),
+                    send_sem=send_sems.at[a, k],
+                    recv_sem=recv_sems.at[a, k],
+                    device_id=device(axis, peer),
+                    device_id_type=MESH,
+                )
+                copy.start()
+                copies.append(copy)
+            continue
+        half = n // 2
+        slot = me // 2
+
+        def own_half(a=a, n=n, me=me, slot=slot, half=half, split_axis=split_axis,
+                     concat_axis=concat_axis):
+            return pltpu.make_async_copy(
+                view(srcs[a], split_axis, me, n), view(dsts[a], concat_axis, slot, half),
+                send_sems.at[a, 0],
+            )
+
+        def out_half(k, a=a, n=n, me=me, slot=slot, half=half, axis=axis,
+                     split_axis=split_axis, concat_axis=concat_axis):
             peer = (me + k) % n
-            copy = pltpu.make_async_remote_copy(
+            return pltpu.make_async_remote_copy(
                 src_ref=view(srcs[a], split_axis, peer, n),
-                dst_ref=view(dsts[a], concat_axis, me, n),
+                dst_ref=view(dsts[a], concat_axis, slot, half),
                 send_sem=send_sems.at[a, k],
-                recv_sem=recv_sems.at[a, k],
+                recv_sem=recv_sems.at[a, slot],
                 device_id=device(axis, peer),
                 device_id_type=MESH,
             )
-            copy.start()
-            copies.append(copy)
+
+        @pl.when(me % 2 == parity)
+        def _():
+            own_half().start()
+            for k in range(1, n):
+                out_half(k).start()
+
+        halves.append((me, n, parity, own_half, out_half, a))
     for copy in copies:
         copy.wait()
+    for me, n, parity, own_half, out_half, a in halves:
+
+        @pl.when(me % 2 == parity)
+        def _():
+            own_half().wait()
+            for k in range(1, n):
+                out_half(k).wait_send()
+
+        for j in range(n // 2):
+            sender = 2 * j + parity
+
+            @pl.when(sender != me)
+            def _():
+                pltpu.make_async_remote_copy(
+                    src_ref=view(srcs[a], jobs[a][1], 0, n),
+                    dst_ref=view(dsts[a], jobs[a][2], j, n // 2),
+                    send_sem=send_sems.at[a, 0],
+                    recv_sem=recv_sems.at[a, j],
+                    device_id=device(jobs[a][0], sender),
+                    device_id_type=MESH,
+                ).wait_recv()
 
 
 def exchange(arrays, jobs, axes, collective_id):
     out_shapes = []
-    for x, (axis, split_axis, concat_axis) in zip(arrays, jobs):
+    for x, (axis, split_axis, concat_axis, parity) in zip(arrays, jobs):
         n = lax.axis_size(axis)
         shape = list(x.shape)
         shape[split_axis] //= n
-        shape[concat_axis] *= n
+        shape[concat_axis] *= n if parity is None else n // 2
         out_shapes.append(jax.ShapeDtypeStruct(tuple(shape), x.dtype))
     widest = max(lax.axis_size(job[0]) for job in jobs)
     count = len(arrays)
@@ -116,7 +169,7 @@
 
 
 def finish_kernel(
-    idx_ref, q_hbm, k_hbm, v_hbm, fk_hbm, sv_hbm, y_ref,
+    idx_ref, q_hbm, ka_hbm, kb_hbm, v_hbm, fka_hbm, fkb_hbm, sv_hbm, y_ref,
     qv, kv, vv, fkv, fvv, wts, base, fac, stage,
     load_sems, ctx_send, ctx_recv, out_send, out_recv, q_send, q_recv,
     *, axes, heads_here, scale, capacity,
@@ -177,7 +230,13 @@
         )
         copy.start()
         loads.append(copy)
-    for a, (src, dst) in enumerate(((k_hbm, kv), (v_hbm, vv), (fk_hbm, fkv))):
+    top_rows = pl.ds(0, BLOCK // 2)
+    low_rows = pl.ds(BLOCK // 2, BLOCK // 2)
+    pairs = (
+        (ka_hbm, kv.at[:, top_rows, :]), (kb_hbm, kv.at[:, low_rows, :]), (v_hbm, vv),
+        (fka_hbm, fkv.at[:, top_rows, :]), (fkb_hbm, fkv.at[:, low_rows, :]),
+    )
+    for a, (src, dst) in enumerate(pairs):
         load = pltpu.make_async_copy(src, dst, load_sems.at[a])
         load.start()
         loads.append(load)
@@ -295,9 +354,9 @@
 
 
 def finish_attention(
-    far_index, queries, k_blocks, v_blocks, far_k, send_v, scale, axes, tok_rows, capacity
+    far_index, queries, k_parts, v_blocks, far_parts, send_v, scale, axes, tok_rows, capacity
 ):
-    local_blocks, _, width = k_blocks.shape
+    local_blocks, _, width = v_blocks.shape
     heads_here = width // HD
     n = HEADS // heads_here
     m_ctx = send_v.shape[0] // capacity
@@ -309,19 +368,19 @@
     return pl.pallas_call(
         kernel,
         out_shape=jax.ShapeDtypeStruct((tok_rows, n * width), jnp.bfloat16),
-        in_specs=[pl.BlockSpec(memory_space=pltpu.SMEM)] + [anywhere] * 5,
+        in_specs=[pl.BlockSpec(memory_space=pltpu.SMEM)] + [anywhere] * 7,
         out_specs=anywhere,
         scratch_shapes=[
-            pltpu.VMEM(k_blocks.shape, jnp.bfloat16),
-            pltpu.VMEM(k_blocks.shape, jnp.bfloat16),
             pltpu.VMEM(v_blocks.shape, jnp.bfloat16),
-            pltpu.VMEM(far_k.shape, jnp.bfloat16),
+            pltpu.VMEM(v_blocks.shape, jnp.bfloat16),
+            pltpu.VMEM(v_blocks.shape, jnp.bfloat16),
+            pltpu.VMEM(send_v.shape, jnp.bfloat16),
             pltpu.VMEM(send_v.shape, jnp.bfloat16),
             pltpu.VMEM((local_blocks, heads_here * RSEL, BLOCK, BLOCK), jnp.bfloat16),
             pltpu.VMEM((local_blocks, BLOCK, width), jnp.float32),
             pltpu.VMEM((local_blocks, heads_here * 3, BLOCK, 1), jnp.float32),
             pltpu.VMEM((local_blocks, BLOCK, width), jnp.bfloat16),
-            pltpu.SemaphoreType.DMA((4,)),
+            pltpu.SemaphoreType.DMA((6,)),
             pltpu.SemaphoreType.DMA((m_ctx,)),
             pltpu.SemaphoreType.DMA((m_ctx,)),
             pltpu.SemaphoreType.DMA((local_blocks * (BLOCK // tok_rows),)),
@@ -337,7 +396,7 @@
             transcendentals=local_blocks * heads_here * 3 * BLOCK * BLOCK,
             bytes_accessed=local_blocks * BLOCK * width * 2 * 8,
         ),
-    )(far_index, queries, k_blocks, v_blocks, far_k, send_v)
+    )(far_index, queries, *k_parts, v_blocks, *far_parts, send_v)
 
 
 def local(queries, keys, values, picks, axes):
@@ -348,11 +407,12 @@
     width = heads_here * HD
     tok_rows = queries.shape[0]
     score_scale = 1.0 / math.sqrt(HD)
-    head_in = ("head", 1, 0)
-    ctx_move = ("ctx", 0, 0)
-    k_heads, v_heads = exchange((keys, values), (head_in, head_in), axes, collective_id=0)
-    local_blocks = k_heads.shape[0] // BLOCK
-    k_blocks = k_heads.reshape(local_blocks, BLOCK, width)
+    head_in = ("head", 1, 0, None)
+    ctx_move = ("ctx", 0, 0, None)
+    (k_even,) = exchange((keys,), (("head", 1, 0, 0),), axes, collective_id=0)
+    local_blocks = k_even.shape[0] * 2 // BLOCK
+    half_rows = BLOCK // 2
+    k_even = k_even.reshape(local_blocks, half_rows, width)
 
     capacity = (local_blocks * RSEL + ctx_count - 1) // ctx_count + 1
     owners, within, position = route_tables(picks, local_blocks, ctx_count)
@@ -363,12 +423,18 @@
     wanted = jnp.sum(asked.astype(jnp.int32) * within[:, :, None], axis=1)
     far_index = (mine_owner * capacity + mine_pos).astype(jnp.int32)
 
-    send_k = k_blocks[wanted.reshape(-1)]
+    pick = wanted.reshape(-1)
+    far_even, k_odd, v_heads = exchange(
+        (k_even[pick], keys, values), (ctx_move, ("head", 1, 0, 1), head_in), axes,
+        collective_id=1,
+    )
+    k_odd = k_odd.reshape(local_blocks, half_rows, width)
+    (far_odd,) = exchange((k_odd[pick],), (ctx_move,), axes, collective_id=3)
     v_blocks = v_heads.reshape(local_blocks, BLOCK, width)
-    send_v = v_blocks[wanted.reshape(-1)]
-    (far_k,) = exchange((send_k,), (ctx_move,), axes, collective_id=1)
+    send_v = v_blocks[pick]
     return finish_attention(
-        far_index, queries, k_blocks, v_blocks, far_k, send_v, score_scale, axes, tok_rows,
+        far_index, queries, (k_even, k_odd), v_blocks, (far_even, far_odd), send_v, score_scale,
+        axes, tok_rows,
         capacity,
     )
 

time: 275 us -> 265 us (0.964)
  Pallas kernels: 260 us -> 250 us
    pallas_call x2 -> x3, Pallas kernels: 143 us -> 127 us  [exchange(): pl.pallas_call(functools.partial(exchange_kernel, axes=axes, jobs=tuple(j...]
    pallas_call x1, Pallas kernels: 117 us -> 124 us  [finish_attention(): pl.pallas_call(kernel, out_shape=jax.ShapeDtypeStruct((tok_rows, n * widt...]
    gather x2 -> x3, local copies, waits for them, and re-layouts: 7.33 us -> 9.43 us  [the longest x1 3.21 us: local(): k_even[pick]]
where the time goes in v15:
time: 265 us
  Pallas kernels  250 us (94%)
  local copies, waits for them, and re-layouts  12.4 us (5%)
    pallas_call x3, Pallas kernels, exchange(): pl.pallas_call(functools.partial(exchange_kernel, axes=axes, jobs=tuple(j...  127 us
    pallas_call x1, Pallas kernels, finish_attention(): pl.pallas_call(kernel, out_shape=jax.ShapeDtypeStruct((tok_rows, n * widt...  124 us

profile of v15, /device:TPU:1, one launch (start us, length us, event | category | flops | bytes accessed | tf_op | source)
XLA Modules:
  0.0 264.9 jit_solution(3786674633224534141)
XLA Ops:
  0.0 0.7 and_select_fusion
  0.7 0.1 copy.23
  0.8 0.1 mul.19
  0.9 0.1 copy.19
  1.0 0.1 reshape.56
  1.1 0.1 copy.20
  1.2 0.5 fusion.4
  1.6 0.7 add_reduce_fusion.idx_ref
  2.3 0.1 copy.22
  2.4 0.1 select_reduce_fusion
  2.5 0.1 copy.24
  2.6 0.1 reshape.58
  2.7 14.3 %shard_map.46 = bf16[2048,128]{1,0:T(8,128)(2,1)} custom-call(bf16[256,2048]{1,0:T(8,128)(2,1)} %refs_1_.1), custom_call_target="tpu_custom_call" | custom-call | tf_op jit(solution)/shard_map/pallas_call | solution.py:134
  17.0 3.2 %gather_fusion = bf16[32,256,128]{2,1,0:T(8,128)(2,1)} fusion(bf16[8,256,128]{2,1,0:T(8,128)(2,1)} %bitcast.7, s32[1024]{0:T(1024)S(1)} %pad_clamp_fusion), kind=kCustom, calls=%fused_computation | custom fusion | bytes 4194432 | tf_op jit(solution)/shard_map/gather | solution.py:428
  20.2 58.2 %shard_map.47 = (bf16[32,256,128]{2,1,0:T(8,128)(2,1)}, bf16[2048,128]{1,0:T(8,128)(2,1)}, bf16[4096,128]{1,0:T(8,128)(2,1)}) custom-call(bf16[32,256,128]{2,1,0:T(8,128)(2,1)} %gather_fusion, bf16[256,2048]{1,0:T(8,128)(2,1)} %refs_1_.1, bf16[256,2048]{1,0:T(8,128)(2,1)} %refs_2_.1), custom_call_target="tpu_custom_call" | custom-call | tf_op jit(solution)/shard_map/pallas_call | solution.py:134
  78.4 3.2 %gather_fusion.1 = bf16[32,256,128]{2,1,0:T(8,128)(2,1)} fusion(bf16[8,256,128]{2,1,0:T(8,128)(2,1)} %bitcast.9, s32[1024]{0:T(1024)S(1)} %pad_clamp_fusion), kind=kCustom, calls=%fused_computation.1 | custom fusion | bytes 4194432 | tf_op jit(solution)/shard_map/gather | solution.py:432
  81.6 0.0 copy-start
  81.6 54.2 %shard_map.48.fkb_hbm = bf16[32,256,128]{2,1,0:T(8,128)(2,1)} custom-call(bf16[32,256,128]{2,1,0:T(8,128)(2,1)} %gather_fusion.1), custom_call_target="tpu_custom_call" | custom-call | tf_op jit(solution)/shard_map/pallas_call | solution.py:134
  135.8 0.0 copy-done
  135.8 3.0 %gather_fusion.2 = bf16[32,512,128]{2,1,0:T(8,128)(2,1)} fusion(bf16[8,512,128]{2,1,0:T(8,128)(2,1)S(1)} %bitcast.6, s32[1024]{0:T(1024)S(1)} %pad_clamp_fusion), kind=kCustom, calls=%fused_computation.2 | custom fusion | bytes 8388736 | tf_op jit(solution)/shard_map/gather | solution.py:434
  138.8 123.8 %shard_map.49 = bf16[256,2048]{1,0:T(8,128)(2,1)} custom-call(s32[16]{0:T(128)} %add_reduce_fusion.idx_ref, bf16[256,2048]{1,0:T(8,128)(2,1)} %q_hbm.1, bf16[8,256,128]{2,1,0:T(8,128)(2,1)} %bitcast.8, bf16[8,256,128]{2,1,0:T(8,128)(2,1)} %bitcast.10, bf16[8,512,128]{2,1,0:T(8,128)(2,1)} %bitcast.5, bf16[32,256,128]{2,1,0:T(8,128)(2,1)} %get-tuple-element.10.fka_hbm, ...), custom_call_target="tpu_custom_call" | custom-call | flops 3221225472 | bytes 8388608 | tf_op jit(solution)/shard_map/pallas_call | solution.py:368
  262.6 2.3 copy.26
  (4 shorter events, 0.0 us)
Async XLA Ops:
  81.6 54.2 %copy-start = (bf16[4096,128]{1,0:T(8,128)(2,1)S(1)}, bf16[4096,128]{1,0:T(8,128)(2,1)}, u32[]{:S(2)}) copy-start(bf16[4096,128]{1,0:T(8,128)(2,1)} %get-tuple-element.9) | copy-start | bytes 3145732

commit v16 on v15

--- a/solution.py
+++ b/solution.py
@@ -142,6 +142,14 @@
         ],
         compiler_params=pltpu.CompilerParams(collective_id=collective_id, has_side_effects=True),
     )(*arrays)
+
+
+def pick_rows(table, pick):
+    count = table.shape[0]
+    flat = table.reshape(count, -1)
+    chosen = (pick[:, None] == jnp.arange(count, dtype=pick.dtype)[None, :]).astype(table.dtype)
+    out = jnp.dot(chosen, flat, preferred_element_type=jnp.float32).astype(table.dtype)
+    return out.reshape((pick.shape[0],) + table.shape[1:])
 
 
 def route_tables(picks, local_blocks, ctx_count):
@@ -425,13 +433,13 @@
 
     pick = wanted.reshape(-1)
     far_even, k_odd, v_heads = exchange(
-        (k_even[pick], keys, values), (ctx_move, ("head", 1, 0, 1), head_in), axes,
+        (pick_rows(k_even, pick), keys, values), (ctx_move, ("head", 1, 0, 1), head_in), axes,
         collective_id=1,
     )
     k_odd = k_odd.reshape(local_blocks, half_rows, width)
-    (far_odd,) = exchange((k_odd[pick],), (ctx_move,), axes, collective_id=3)
+    (far_odd,) = exchange((pick_rows(k_odd, pick),), (ctx_move,), axes, collective_id=3)
     v_blocks = v_heads.reshape(local_blocks, BLOCK, width)
-    send_v = v_blocks[pick]
+    send_v = pick_rows(v_blocks, pick)
     return finish_attention(
         far_index, queries, (k_even, k_odd), v_blocks, (far_even, far_odd), send_v, score_scale,
         axes, tok_rows,

time: 265 us -> 268 us (1.011)
  matrix products: 0 us -> 2.77 us
    gather x3 -> x0, local copies, waits for them, and re-layouts: 9.43 us -> none  [the longest x1 3.21 us: local(): k_even[pick]]
    unnamed x3 -> x6, local copies, waits for them, and re-layouts: 2.31 us -> 8.84 us
    another operation x0 -> x3, local copies, waits for them, and re-layouts: none -> 3.16 us  [pick_rows(): flat = table.reshape(count, -1)]
    dot_general x0 -> x3, matrix products: none -> 2.77 us  [pick_rows(): jnp.dot(chosen, flat, preferred_element_type=jnp.float32)]
where the time goes in v16:
time: 268 us
  Pallas kernels  250 us (93%)
  local copies, waits for them, and re-layouts  12.7 us (5%)
  matrix products  2.77 us (1%)
    pallas_call x3, Pallas kernels, exchange(): pl.pallas_call(functools.partial(exchange_kernel, axes=axes, jobs=tuple(j...  127 us
    pallas_call x1, Pallas kernels, finish_attention(): pl.pallas_call(kernel, out_shape=jax.ShapeDtypeStruct((tok_rows, n * widt...  124 us
    unnamed x6, local copies, waits for them, and re-layouts  8.84 us

profile of v16, /device:TPU:1, one launch (start us, length us, event | category | flops | bytes accessed | tf_op | source)
XLA Modules:
  0.0 267.9 jit_solution(18340971022367023380)
XLA Ops:
  0.0 0.7 and_select_fusion
  0.7 0.1 copy.19
  0.8 0.1 reshape.35
  1.0 0.5 fusion.9
  1.5 0.1 copy.23
  1.6 0.1 mul.19
  1.7 0.1 select_reduce_fusion
  1.8 0.1 copy.24
  1.9 0.1 eq.38
  2.0 14.3 %shard_map.46 = bf16[2048,128]{1,0:T(8,128)(2,1)} custom-call(bf16[256,2048]{1,0:T(8,128)(2,1)} %refs_1_.1), custom_call_target="tpu_custom_call" | custom-call | tf_op jit(solution)/shard_map/pallas_call | solution.py:134
  16.3 1.3 reshape_reshape.9
  17.5 0.7 fusion.1
  18.3 1.8 copy.25
  20.1 58.2 %shard_map.47 = (bf16[32,256,128]{2,1,0:T(8,128)(2,1)}, bf16[2048,128]{1,0:T(8,128)(2,1)}, bf16[4096,128]{1,0:T(8,128)(2,1)}) custom-call(bf16[32,256,128]{2,1,0:T(8,128)(2,1)} %bitcast.16, bf16[256,2048]{1,0:T(8,128)(2,1)} %refs_1_.1, bf16[256,2048]{1,0:T(8,128)(2,1)} %refs_2_.1), custom_call_target="tpu_custom_call" | custom-call | tf_op jit(solution)/shard_map/pallas_call | solution.py:134
  78.3 1.7 reshape_reshape.11
  80.0 1.3 fusion
  81.3 2.9 %copy.27 = bf16[4,8,512,128]{3,2,1,0:T(8,128)(2,1)} copy(bf16[4,8,512,128]{3,1,2,0:T(8,128)(2,1)S(1)} %fusion) | data formatting | bytes 8388608
  84.1 0.2 reshape_reshape.10
  84.3 0.7 fusion.2
  85.1 1.9 copy.26
  87.0 54.2 %shard_map.48.fkb_hbm = bf16[32,256,128]{2,1,0:T(8,128)(2,1)} custom-call(bf16[32,256,128]{2,1,0:T(8,128)(2,1)} %bitcast.17), custom_call_target="tpu_custom_call" | custom-call | tf_op jit(solution)/shard_map/pallas_call | solution.py:134
  141.2 0.7 add_reduce_fusion.idx_ref
  141.9 123.7 %shard_map.49 = bf16[256,2048]{1,0:T(8,128)(2,1)} custom-call(s32[16]{0:T(128)} %add_reduce_fusion.idx_ref, bf16[256,2048]{1,0:T(8,128)(2,1)} %q_hbm.1, bf16[8,256,128]{2,1,0:T(8,128)(2,1)} %bitcast.18, bf16[8,256,128]{2,1,0:T(8,128)(2,1)} %bitcast.20, bf16[8,512,128]{2,1,0:T(8,128)(2,1)} %bitcast.19, bf16[32,256,128]{2,1,0:T(8,128)(2,1)} %get-tuple-element.10.fka_hbm, ...), custom_call_target="tpu_custom_call" | custom-call | flops 3221225472 | bytes 8388608 | tf_op jit(solution)/shard_map/pallas_call | solution.py:376
  265.6 2.3 copy.29
  (6 shorter events, 0.2 us)
Async XLA Ops:
  81.2 2.9 %copy-start = (bf16[2048,128]{1,0:T(8,128)(2,1)S(1)}, bf16[2048,128]{1,0:T(8,128)(2,1)}, u32[]{:S(2)}) copy-start(bf16[2048,128]{1,0:T(8,128)(2,1)} %get-tuple-element.8) | copy-start | bytes 1572868

commit v17 on v10

--- a/solution.py
+++ b/solution.py
@@ -279,9 +279,10 @@
         finish((t + turn) % local_blocks)
         return carry
 
-    lax.fori_loop(0, local_blocks - 1, settle, 0)
+    lax.fori_loop(0, local_blocks - 2, settle, 0)
     last = (local_blocks - 1 + turn) % local_blocks
     send(last)
+    finish((local_blocks - 2 + turn) % local_blocks)
     finish(last)
     for sender in range(n):
 

time: 265 us -> 264 us (level)
  no operation moved by 1% of the time
where the time goes in v17:
time: 264 us; the launch traced here: 262 us
  Pallas kernels  249 us (94%)
  local copies, waits for them, and re-layouts  11.6 us (4%)
    pallas_call x2, Pallas kernels, exchange(): pl.pallas_call(functools.partial(exchange_kernel, axes=axes, jobs=tuple(j...  132 us
    pallas_call x1, Pallas kernels, finish_attention(): pl.pallas_call(kernel, out_shape=jax.ShapeDtypeStruct((tok_rows, n * widt...  116 us

profile of v17, /device:TPU:1, one launch (start us, length us, event | category | flops | bytes accessed | tf_op | source)
XLA Modules:
  0.0 262.1 jit_solution(16488609378754747874)
XLA Ops:
  0.0 0.7 and_select_fusion
  0.7 0.1 copy.23
  0.8 0.1 mul.19
  0.9 0.1 copy.19
  1.0 0.1 reshape.54
  1.1 0.1 copy.20
  1.2 0.5 fusion.4
  1.6 0.7 add_reduce_fusion.idx_ref
  2.3 0.1 copy.22
  2.4 0.1 select_reduce_fusion
  2.5 0.1 copy.24
  2.6 0.1 reshape.56
  2.7 19.3 %shard_map.46 = bf16[4096,128]{1,0:T(8,128)(2,1)} custom-call(bf16[256,2048]{1,0:T(8,128)(2,1)} %refs_0_.1), custom_call_target="tpu_custom_call" | custom-call | tf_op jit(solution)/shard_map/pallas_call | solution.py:81
  22.1 4.3 %gather_fusion = bf16[32,512,128]{2,1,0:T(8,128)(2,1)} fusion(bf16[8,512,128]{2,1,0:T(8,128)(2,1)} %bitcast.4, s32[1024]{0:T(1024)S(1)} %pad_clamp_fusion), kind=kCustom, calls=%fused_computation | custom fusion | bytes 8388736 | tf_op jit(solution)/shard_map/gather | solution.py:367
  26.4 112.9 %shard_map.47 = (bf16[32,512,128]{2,1,0:T(8,128)(2,1)}, bf16[4096,128]{1,0:T(8,128)(2,1)}) custom-call(bf16[32,512,128]{2,1,0:T(8,128)(2,1)} %gather_fusion, bf16[256,2048]{1,0:T(8,128)(2,1)} %refs_1_.1), custom_call_target="tpu_custom_call" | custom-call | tf_op jit(solution)/shard_map/pallas_call | solution.py:81
  139.3 4.3 %gather_fusion.1 = bf16[32,512,128]{2,1,0:T(8,128)(2,1)} fusion(bf16[8,512,128]{2,1,0:T(8,128)(2,1)} %bitcast.6, s32[1024]{0:T(1024)S(1)} %pad_clamp_fusion), kind=kCustom, calls=%fused_computation.1 | custom fusion | bytes 8388736 | tf_op jit(solution)/shard_map/gather | solution.py:370
  143.6 116.2 %shard_map.48 = bf16[256,2048]{1,0:T(8,128)(2,1)} custom-call(s32[16]{0:T(128)} %add_reduce_fusion.idx_ref, bf16[256,2048]{1,0:T(8,128)(2,1)} %q_hbm.1, bf16[8,512,128]{2,1,0:T(8,128)(2,1)} %bitcast.5, bf16[8,512,128]{2,1,0:T(8,128)(2,1)} %bitcast.7, bf16[32,512,128]{2,1,0:T(8,128)(2,1)} %get-tuple-element.8.fk_hbm, bf16[32,512,128]{2,1,0:T(8,128)(2,1)} %gather_fusion.1), custom_call_target="tpu_custom_call" | custom-call | flops 3221225472 | bytes 8388608 | tf_op jit(solution)/shard_map/pallas_call | solution.py:310
  259.8 2.3 copy.26
  (4 shorter events, 0.0 us)

commit v18 on v10

--- a/solution.py
+++ b/solution.py
@@ -129,7 +129,7 @@
     rows = y_ref.shape[0]
     width = heads_here * HD
     per_block = BLOCK // rows
-    turn = me // per_block
+    turn = me % local_blocks
 
     def device(axis, peer):
         return tuple(peer if name == axis else lax.axis_index(name) for name in axes)

time: 265 us -> 265 us (level)
  no operation moved by 1% of the time
where the time goes in v18:
time: 265 us; the launch traced here: 261 us
  Pallas kernels  248 us (94%)
  local copies, waits for them, and re-layouts  11.6 us (4%)
    pallas_call x2, Pallas kernels, exchange(): pl.pallas_call(functools.partial(exchange_kernel, axes=axes, jobs=tuple(j...  132 us
    pallas_call x1, Pallas kernels, finish_attention(): pl.pallas_call(kernel, out_shape=jax.ShapeDtypeStruct((tok_rows, n * widt...  115 us

profile of v18, /device:TPU:1, one launch (start us, length us, event | category | flops | bytes accessed | tf_op | source)
XLA Modules:
  0.0 261.2 jit_solution(13850824828121860244)
XLA Ops:
  0.0 0.7 and_select_fusion
  0.7 0.1 copy.23
  0.8 0.1 mul.19
  0.9 0.1 copy.19
  1.0 0.1 reshape.54
  1.1 0.1 copy.20
  1.2 0.5 fusion.4
  1.6 0.7 add_reduce_fusion.idx_ref
  2.3 0.1 copy.22
  2.4 0.1 select_reduce_fusion
  2.5 0.1 copy.24
  2.6 0.1 reshape.56
  2.7 19.3 %shard_map.46 = bf16[4096,128]{1,0:T(8,128)(2,1)} custom-call(bf16[256,2048]{1,0:T(8,128)(2,1)} %refs_0_.1), custom_call_target="tpu_custom_call" | custom-call | tf_op jit(solution)/shard_map/pallas_call | solution.py:81
  22.1 4.3 %gather_fusion = bf16[32,512,128]{2,1,0:T(8,128)(2,1)} fusion(bf16[8,512,128]{2,1,0:T(8,128)(2,1)} %bitcast.4, s32[1024]{0:T(1024)S(1)} %pad_clamp_fusion), kind=kCustom, calls=%fused_computation | custom fusion | bytes 8388736 | tf_op jit(solution)/shard_map/gather | solution.py:366
  26.4 112.9 %shard_map.47 = (bf16[32,512,128]{2,1,0:T(8,128)(2,1)}, bf16[4096,128]{1,0:T(8,128)(2,1)}) custom-call(bf16[32,512,128]{2,1,0:T(8,128)(2,1)} %gather_fusion, bf16[256,2048]{1,0:T(8,128)(2,1)} %refs_1_.1), custom_call_target="tpu_custom_call" | custom-call | tf_op jit(solution)/shard_map/pallas_call | solution.py:81
  139.3 4.3 %gather_fusion.1 = bf16[32,512,128]{2,1,0:T(8,128)(2,1)} fusion(bf16[8,512,128]{2,1,0:T(8,128)(2,1)} %bitcast.6, s32[1024]{0:T(1024)S(1)} %pad_clamp_fusion), kind=kCustom, calls=%fused_computation.1 | custom fusion | bytes 8388736 | tf_op jit(solution)/shard_map/gather | solution.py:369
  143.6 115.3 %shard_map.48 = bf16[256,2048]{1,0:T(8,128)(2,1)} custom-call(s32[16]{0:T(128)} %add_reduce_fusion.idx_ref, bf16[256,2048]{1,0:T(8,128)(2,1)} %q_hbm.1, bf16[8,512,128]{2,1,0:T(8,128)(2,1)} %bitcast.5, bf16[8,512,128]{2,1,0:T(8,128)(2,1)} %bitcast.7, bf16[32,512,128]{2,1,0:T(8,128)(2,1)} %get-tuple-element.8.fk_hbm, bf16[32,512,128]{2,1,0:T(8,128)(2,1)} %gather_fusion.1), custom_call_target="tpu_custom_call" | custom-call | flops 3221225472 | bytes 8388608 | tf_op jit(solution)/shard_map/pallas_call | solution.py:309
  258.9 2.3 copy.26
  (4 shorter events, 0.0 us)

commit v19 on v15

--- a/solution.py
+++ b/solution.py
@@ -182,7 +182,7 @@
     rows = y_ref.shape[0]
     width = heads_here * HD
     per_block = BLOCK // rows
-    turn = me // per_block
+    turn = me % local_blocks
 
     def device(axis, peer):
         return tuple(peer if name == axis else lax.axis_index(name) for name in axes)
@@ -338,9 +338,10 @@
         finish((t + turn) % local_blocks)
         return carry
 
-    lax.fori_loop(0, local_blocks - 1, settle, 0)
+    lax.fori_loop(0, local_blocks - 2, settle, 0)
     last = (local_blocks - 1 + turn) % local_blocks
     send(last)
+    finish((local_blocks - 2 + turn) % local_blocks)
     finish(last)
     for sender in range(n):
 

time: 265 us -> 263 us (level)
    pallas_call x1, Pallas kernels: 124 us -> 121 us  [finish_attention(): pl.pallas_call(kernel, out_shape=jax.ShapeDtypeStruct((tok_rows, n * widt...]
where the time goes in v19:
time: 263 us; the launch traced here: 262 us
  Pallas kernels  248 us (94%)
  local copies, waits for them, and re-layouts  12.4 us (5%)
    pallas_call x3, Pallas kernels, exchange(): pl.pallas_call(functools.partial(exchange_kernel, axes=axes, jobs=tuple(j...  127 us
    pallas_call x1, Pallas kernels, finish_attention(): pl.pallas_call(kernel, out_shape=jax.ShapeDtypeStruct((tok_rows, n * widt...  121 us

profile of v19, /device:TPU:1, one launch (start us, length us, event | category | flops | bytes accessed | tf_op | source)
XLA Modules:
  0.0 262.1 jit_solution(8527634061559560054)
XLA Ops:
  0.0 0.7 and_select_fusion
  0.7 0.1 copy.23
  0.8 0.1 mul.19
  0.9 0.1 copy.19
  1.0 0.1 reshape.56
  1.1 0.1 copy.20
  1.2 0.5 fusion.4
  1.6 0.7 add_reduce_fusion.idx_ref
  2.3 0.1 copy.22
  2.4 0.1 select_reduce_fusion
  2.5 0.1 copy.24
  2.6 0.1 reshape.58
  2.7 14.3 %shard_map.46 = bf16[2048,128]{1,0:T(8,128)(2,1)} custom-call(bf16[256,2048]{1,0:T(8,128)(2,1)} %refs_1_.1), custom_call_target="tpu_custom_call" | custom-call | tf_op jit(solution)/shard_map/pallas_call | solution.py:134
  17.0 3.2 %gather_fusion = bf16[32,256,128]{2,1,0:T(8,128)(2,1)} fusion(bf16[8,256,128]{2,1,0:T(8,128)(2,1)} %bitcast.7, s32[1024]{0:T(1024)S(1)} %pad_clamp_fusion), kind=kCustom, calls=%fused_computation | custom fusion | bytes 4194432 | tf_op jit(solution)/shard_map/gather | solution.py:429
  20.2 58.2 %shard_map.47 = (bf16[32,256,128]{2,1,0:T(8,128)(2,1)}, bf16[2048,128]{1,0:T(8,128)(2,1)}, bf16[4096,128]{1,0:T(8,128)(2,1)}) custom-call(bf16[32,256,128]{2,1,0:T(8,128)(2,1)} %gather_fusion, bf16[256,2048]{1,0:T(8,128)(2,1)} %refs_1_.1, bf16[256,2048]{1,0:T(8,128)(2,1)} %refs_2_.1), custom_call_target="tpu_custom_call" | custom-call | tf_op jit(solution)/shard_map/pallas_call | solution.py:134
  78.4 3.2 %gather_fusion.1 = bf16[32,256,128]{2,1,0:T(8,128)(2,1)} fusion(bf16[8,256,128]{2,1,0:T(8,128)(2,1)} %bitcast.9, s32[1024]{0:T(1024)S(1)} %pad_clamp_fusion), kind=kCustom, calls=%fused_computation.1 | custom fusion | bytes 4194432 | tf_op jit(solution)/shard_map/gather | solution.py:433
  81.6 0.0 copy-start
  81.6 54.2 %shard_map.48.fkb_hbm = bf16[32,256,128]{2,1,0:T(8,128)(2,1)} custom-call(bf16[32,256,128]{2,1,0:T(8,128)(2,1)} %gather_fusion.1), custom_call_target="tpu_custom_call" | custom-call | tf_op jit(solution)/shard_map/pallas_call | solution.py:134
  135.8 0.0 copy-done
  135.8 3.0 %gather_fusion.2 = bf16[32,512,128]{2,1,0:T(8,128)(2,1)} fusion(bf16[8,512,128]{2,1,0:T(8,128)(2,1)S(1)} %bitcast.6, s32[1024]{0:T(1024)S(1)} %pad_clamp_fusion), kind=kCustom, calls=%fused_computation.2 | custom fusion | bytes 8388736 | tf_op jit(solution)/shard_map/gather | solution.py:435
  138.8 121.0 %shard_map.49 = bf16[256,2048]{1,0:T(8,128)(2,1)} custom-call(s32[16]{0:T(128)} %add_reduce_fusion.idx_ref, bf16[256,2048]{1,0:T(8,128)(2,1)} %q_hbm.1, bf16[8,256,128]{2,1,0:T(8,128)(2,1)} %bitcast.8, bf16[8,256,128]{2,1,0:T(8,128)(2,1)} %bitcast.10, bf16[8,512,128]{2,1,0:T(8,128)(2,1)} %bitcast.5, bf16[32,256,128]{2,1,0:T(8,128)(2,1)} %get-tuple-element.10.fka_hbm, ...), custom_call_target="tpu_custom_call" | custom-call | flops 3221225472 | bytes 8388608 | tf_op jit(solution)/shard_map/pallas_call | solution.py:369
  259.8 2.3 copy.26
  (4 shorter events, 0.0 us)
Async XLA Ops:
  81.6 54.2 %copy-start = (bf16[4096,128]{1,0:T(8,128)(2,1)S(1)}, bf16[4096,128]{1,0:T(8,128)(2,1)}, u32[]{:S(2)}) copy-start(bf16[4096,128]{1,0:T(8,128)(2,1)} %get-tuple-element.9) | copy-start | bytes 3145732

commit v20 on v19

--- a/solution.py
+++ b/solution.py
@@ -219,17 +219,8 @@
     def q_cols(peer):
         return q_hbm.at[:, pl.ds(peer * width, width)]
 
-    loads = [pltpu.make_async_copy(q_cols(me), q_rows(me), q_send.at[0])]
+    loads = [pltpu.make_async_copy(q_hbm, qv, q_send.at[0])]
     loads[0].start()
-    for k in range(1, n):
-        peer = (me + k) % n
-        copy = pltpu.make_async_remote_copy(
-            src_ref=q_cols(peer), dst_ref=q_rows(me),
-            send_sem=q_send.at[k], recv_sem=q_recv.at[k],
-            device_id=device("head", peer), device_id_type=MESH,
-        )
-        copy.start()
-        loads.append(copy)
     top_rows = pl.ds(0, BLOCK // 2)
     low_rows = pl.ds(BLOCK // 2, BLOCK // 2)
     pairs = (
@@ -430,11 +421,14 @@
         collective_id=1,
     )
     k_odd = k_odd.reshape(local_blocks, half_rows, width)
-    (far_odd,) = exchange((k_odd[pick],), (ctx_move,), axes, collective_id=3)
+    far_odd, q_heads = exchange(
+        (k_odd[pick], queries), (ctx_move, head_in), axes, collective_id=3
+    )
+    q_blocks = q_heads.reshape(local_blocks, BLOCK, width)
     v_blocks = v_heads.reshape(local_blocks, BLOCK, width)
     send_v = v_blocks[pick]
     return finish_attention(
-        far_index, queries, (k_even, k_odd), v_blocks, (far_even, far_odd), send_v, score_scale,
+        far_index, q_blocks, (k_even, k_odd), v_blocks, (far_even, far_odd), send_v, score_scale,
         axes, tok_rows,
         capacity,
     )

time: 263 us -> 262 us (level)
    pallas_call x1, Pallas kernels: 121 us -> 118 us  [finish_attention(): pl.pallas_call(kernel, out_shape=jax.ShapeDtypeStruct((tok_rows, n * widt...]
where the time goes in v20:
time: 262 us
  Pallas kernels  247 us (94%)
  local copies, waits for them, and re-layouts  12.4 us (5%)
    pallas_call x3, Pallas kernels, exchange(): pl.pallas_call(functools.partial(exchange_kernel, axes=axes, jobs=tuple(j...  129 us
    pallas_call x1, Pallas kernels, finish_attention(): pl.pallas_call(kernel, out_shape=jax.ShapeDtypeStruct((tok_rows, n * widt...  118 us

profile of v20, /device:TPU:1, one launch (start us, length us, event | category | flops | bytes accessed | tf_op | source)
XLA Modules:
  0.0 261.6 jit_solution(3854638393750161573)
XLA Ops:
  0.0 0.7 and_select_fusion
  0.7 0.1 copy.23
  0.8 0.1 mul.19
  0.9 0.1 copy.19
  1.0 0.1 reshape.59
  1.1 0.1 copy.20
  1.2 0.5 fusion.4
  1.6 0.7 add_reduce_fusion.idx_ref
  2.3 0.1 copy.22
  2.4 0.1 select_reduce_fusion
  2.5 0.1 copy.24
  2.6 0.1 reshape.61
  2.7 14.3 %shard_map.46 = bf16[2048,128]{1,0:T(8,128)(2,1)} custom-call(bf16[256,2048]{1,0:T(8,128)(2,1)} %refs_1_.2), custom_call_target="tpu_custom_call" | custom-call | tf_op jit(solution)/shard_map/pallas_call | solution.py:134
  17.0 3.2 %gather_fusion = bf16[32,256,128]{2,1,0:T(8,128)(2,1)} fusion(bf16[8,256,128]{2,1,0:T(8,128)(2,1)} %bitcast.8, s32[1024]{0:T(1024)S(1)} %pad_clamp_fusion), kind=kCustom, calls=%fused_computation | custom fusion | bytes 4194432 | tf_op jit(solution)/shard_map/gather | solution.py:420
  20.2 58.2 %shard_map.47 = (bf16[32,256,128]{2,1,0:T(8,128)(2,1)}, bf16[2048,128]{1,0:T(8,128)(2,1)}, bf16[4096,128]{1,0:T(8,128)(2,1)}) custom-call(bf16[32,256,128]{2,1,0:T(8,128)(2,1)} %gather_fusion, bf16[256,2048]{1,0:T(8,128)(2,1)} %refs_1_.2, bf16[256,2048]{1,0:T(8,128)(2,1)} %refs_2_.1), custom_call_target="tpu_custom_call" | custom-call | tf_op jit(solution)/shard_map/pallas_call | solution.py:134
  78.4 3.2 %gather_fusion.1 = bf16[32,256,128]{2,1,0:T(8,128)(2,1)} fusion(bf16[8,256,128]{2,1,0:T(8,128)(2,1)} %bitcast.10, s32[1024]{0:T(1024)S(1)} %pad_clamp_fusion), kind=kCustom, calls=%fused_computation.1 | custom fusion | bytes 4194432 | tf_op jit(solution)/shard_map/gather | solution.py:425
  81.6 0.0 copy-start
  81.6 56.4 %shard_map.48 = (bf16[32,256,128]{2,1,0:T(8,128)(2,1)}, bf16[4096,128]{1,0:T(8,128)(2,1)}) custom-call(bf16[32,256,128]{2,1,0:T(8,128)(2,1)} %gather_fusion.1, bf16[256,2048]{1,0:T(8,128)(2,1)} %refs_1_.3), custom_call_target="tpu_custom_call" | custom-call | tf_op jit(solution)/shard_map/pallas_call | solution.py:134
  138.0 0.0 copy-done
  138.1 3.0 %gather_fusion.2 = bf16[32,512,128]{2,1,0:T(8,128)(2,1)} fusion(bf16[8,512,128]{2,1,0:T(8,128)(2,1)S(1)} %bitcast.7, s32[1024]{0:T(1024)S(1)} %pad_clamp_fusion), kind=kCustom, calls=%fused_computation.2 | custom fusion | bytes 8388736 | tf_op jit(solution)/shard_map/gather | solution.py:429
  141.1 118.2 %shard_map.49 = bf16[256,2048]{1,0:T(8,128)(2,1)} custom-call(s32[16]{0:T(128)} %add_reduce_fusion.idx_ref, bf16[8,512,128]{2,1,0:T(8,128)(2,1)} %bitcast.12, bf16[8,256,128]{2,1,0:T(8,128)(2,1)} %bitcast.9, bf16[8,256,128]{2,1,0:T(8,128)(2,1)} %bitcast.11, bf16[8,512,128]{2,1,0:T(8,128)(2,1)} %bitcast.6, bf16[32,256,128]{2,1,0:T(8,128)(2,1)} %get-tuple-element.13.fka_hbm, ...), custom_call_target="tpu_custom_call" | custom-call | flops 3221225472 | bytes 8388608 | tf_op jit(solution)/shard_map/pallas_call | solution.py:360
  259.3 2.3 copy.26
  (4 shorter events, 0.0 us)
Async XLA Ops:
  81.6 56.4 %copy-start = (bf16[4096,128]{1,0:T(8,128)(2,1)S(1)}, bf16[4096,128]{1,0:T(8,128)(2,1)}, u32[]{:S(2)}) copy-start(bf16[4096,128]{1,0:T(8,128)(2,1)} %get-tuple-element.12) | copy-start | bytes 3145732

commit v21 on v19

--- a/solution.py
+++ b/solution.py
@@ -425,12 +425,13 @@
     far_index = (mine_owner * capacity + mine_pos).astype(jnp.int32)
 
     pick = wanted.reshape(-1)
-    far_even, k_odd, v_heads = exchange(
-        (k_even[pick], keys, values), (ctx_move, ("head", 1, 0, 1), head_in), axes,
-        collective_id=1,
+    far_even, k_odd = exchange(
+        (k_even[pick], keys), (ctx_move, ("head", 1, 0, 1)), axes, collective_id=1
     )
     k_odd = k_odd.reshape(local_blocks, half_rows, width)
-    (far_odd,) = exchange((k_odd[pick],), (ctx_move,), axes, collective_id=3)
+    far_odd, v_heads = exchange(
+        (k_odd[pick], values), (ctx_move, head_in), axes, collective_id=3
+    )
     v_blocks = v_heads.reshape(local_blocks, BLOCK, width)
     send_v = v_blocks[pick]
     return finish_attention(

time: 263 us -> 263 us (level)
    pallas_call x1, Pallas kernels: 121 us -> 118 us  [finish_attention(): pl.pallas_call(kernel, out_shape=jax.ShapeDtypeStruct((tok_rows, n * widt...]
where the time goes in v21:
time: 263 us
  Pallas kernels  247 us (94%)
  local copies, waits for them, and re-layouts  13.7 us (5%)
    pallas_call x3, Pallas kernels, exchange(): pl.pallas_call(functools.partial(exchange_kernel, axes=axes, jobs=tuple(j...  129 us
    pallas_call x1, Pallas kernels, finish_attention(): pl.pallas_call(kernel, out_shape=jax.ShapeDtypeStruct((tok_rows, n * widt...  118 us

profile of v21, /device:TPU:1, one launch (start us, length us, event | category | flops | bytes accessed | tf_op | source)
XLA Modules:
  0.0 262.5 jit_solution(4628139963462842833)
XLA Ops:
  0.0 0.7 and_select_fusion
  0.7 0.1 copy.23
  0.8 0.1 mul.19
  0.9 0.1 copy.19
  1.0 0.1 reshape.56
  1.1 0.1 copy.20
  1.2 0.5 fusion.4
  1.6 0.7 add_reduce_fusion.idx_ref
  2.3 0.1 copy.22
  2.4 0.1 select_reduce_fusion
  2.5 0.1 copy.24
  2.6 0.1 reshape.58
  2.7 14.3 %shard_map.46 = bf16[2048,128]{1,0:T(8,128)(2,1)} custom-call(bf16[256,2048]{1,0:T(8,128)(2,1)} %refs_1_.2), custom_call_target="tpu_custom_call" | custom-call | tf_op jit(solution)/shard_map/pallas_call | solution.py:134
  17.0 3.2 %gather_fusion = bf16[32,256,128]{2,1,0:T(8,128)(2,1)} fusion(bf16[8,256,128]{2,1,0:T(8,128)(2,1)} %bitcast.7, s32[1024]{0:T(1024)S(1)} %pad_clamp_fusion), kind=kCustom, calls=%fused_computation | custom fusion | bytes 4194432 | tf_op jit(solution)/shard_map/gather | solution.py:429
  20.2 57.8 %shard_map.47 = (bf16[32,256,128]{2,1,0:T(8,128)(2,1)}, bf16[2048,128]{1,0:T(8,128)(2,1)}) custom-call(bf16[32,256,128]{2,1,0:T(8,128)(2,1)} %gather_fusion, bf16[256,2048]{1,0:T(8,128)(2,1)} %refs_1_.2), custom_call_target="tpu_custom_call" | custom-call | tf_op jit(solution)/shard_map/pallas_call | solution.py:134
  78.0 3.2 %gather_fusion.1 = bf16[32,256,128]{2,1,0:T(8,128)(2,1)} fusion(bf16[8,256,128]{2,1,0:T(8,128)(2,1)} %bitcast.9, s32[1024]{0:T(1024)S(1)} %pad_clamp_fusion), kind=kCustom, calls=%fused_computation.1 | custom fusion | bytes 4194432 | tf_op jit(solution)/shard_map/gather | solution.py:433
  81.3 56.4 %shard_map.48 = (bf16[32,256,128]{2,1,0:T(8,128)(2,1)}, bf16[4096,128]{1,0:T(8,128)(2,1)}) custom-call(bf16[32,256,128]{2,1,0:T(8,128)(2,1)} %gather_fusion.1, bf16[256,2048]{1,0:T(8,128)(2,1)} %refs_1_.3), custom_call_target="tpu_custom_call" | custom-call | tf_op jit(solution)/shard_map/pallas_call | solution.py:134
  137.7 4.2 %gather_fusion.2 = bf16[32,512,128]{2,1,0:T(8,128)(2,1)} fusion(bf16[8,512,128]{2,1,0:T(8,128)(2,1)} %bitcast.5, s32[1024]{0:T(1024)S(1)} %pad_clamp_fusion), kind=kCustom, calls=%fused_computation.2 | custom fusion | bytes 8388736 | tf_op jit(solution)/shard_map/gather | solution.py:436
  141.9 118.3 %shard_map.49 = bf16[256,2048]{1,0:T(8,128)(2,1)} custom-call(s32[16]{0:T(128)} %add_reduce_fusion.idx_ref, bf16[256,2048]{1,0:T(8,128)(2,1)} %q_hbm.1, bf16[8,256,128]{2,1,0:T(8,128)(2,1)} %bitcast.8, bf16[8,256,128]{2,1,0:T(8,128)(2,1)} %bitcast.10, bf16[8,512,128]{2,1,0:T(8,128)(2,1)} %bitcast.6, bf16[32,256,128]{2,1,0:T(8,128)(2,1)} %get-tuple-element.11.fka_hbm, ...), custom_call_target="tpu_custom_call" | custom-call | flops 3221225472 | bytes 8388608 | tf_op jit(solution)/shard_map/pallas_call | solution.py:369
  260.2 2.3 copy.26
  (4 shorter events, 0.0 us)
